TPU v7x, 512 devices: a whole 4x4x16 slice. The times are simulated.
512 devices in a mesh: head: 8 (over x, core), seq: 64 (over y, z).
Axes of the slice: x: 4, y: 4, z: 16, core: 2. Of those that a mesh axis runs over, the one named last changes fastest.
Arguments:
- tokens: bfloat16 [49152, 3200], P('seq'), may hold values from -6 to 6
- ln_gain: float32 [3200], replicated, may hold values from 0.5 to 2
- w_query: bfloat16 [3200, 2048], P('seq', 'head')
- w_key: bfloat16 [3200, 2048], P('seq', 'head')
- w_value: bfloat16 [3200, 2048], P('seq', 'head'), may hold values from -0.109375 to 0.109375
- q_gain: float32 [2048], P('head'), may hold values from 0.5 to 8
- k_gain: float32 [2048], P('head'), may hold values from 0.5 to 8
- seg_ids: int32 [49152], P('seq'), may hold values from 0 to 94, never falling along the last dimension, each value on 1 to 1025 neighbouring positions
Outputs:
- attended: bfloat16 [49152, 2048], P('seq', 'head')
Inputs may be any that keep to these rules, and one draw needn't show every extreme that they name: `seg_ids`: ids never fall along the tokens; each id covers 1 to 1025 consecutive tokens and one covers exactly 1025.
All inputs are finite; a program needn't handle non-finite values.
Results may differ from a plain program's by a relative error of at most 0.0055.
The roundings to bfloat16 on the way count: a program that leaves them out, or rounds other values in their place, can miss the bound.
Values may be sent and summed in bfloat16 or wider, within the bound.
No kernel may reach another device: no remote copies, remote signals or barrier semaphores. Data moves between devices by JAX's collectives and lax.ppermute only.
A program may use at most 64 MiB of HBM per device.

v0:
```python
import math

import jax
import jax.numpy as jnp
from jax import lax
from jax.sharding import PartitionSpec as P

HEADS = 16
HEAD_DIM = 128
MOST = 1025


EPS = 1e-06


def from_behind(shard, axis, by):
    size = lax.axis_size(axis)
    pairs = [(i, i + by) for i in range(size) if 0 <= i + by < size]
    return lax.ppermute(shard, axis, pairs)


def on_device(tokens, ln_gain, w_query, w_key, w_value, q_gain, k_gain, seg_ids):
    rows_here = tokens.shape[0]
    channels = w_query.shape[1]
    heads_here = channels // HEAD_DIM
    total_channels = HEADS * HEAD_DIM
    floats = tokens.astype(jnp.float32)
    normed = (
        floats * lax.rsqrt(jnp.mean(floats * floats, axis=1, keepdims=True) + EPS) * ln_gain
    ).astype(jnp.bfloat16)

    def add_rows(block_rows):
        return jnp.dot(normed, block_rows, preferred_element_type=jnp.float32)

    queries = add_rows(lax.all_gather(w_query, "seq", axis=0, tiled=True))
    key_part = add_rows(lax.all_gather(w_key, "seq", axis=0, tiled=True))
    value_part = add_rows(lax.all_gather(w_value, "seq", axis=0, tiled=True))
    square_q, square_k = lax.psum(
        (jnp.sum(queries * queries, axis=1), jnp.sum(key_part * key_part, axis=1)), "head"
    )
    q_hat = (queries * lax.rsqrt(square_q[:, None] / total_channels + EPS) * q_gain).astype(
        jnp.bfloat16
    )
    k_hat = (key_part * lax.rsqrt(square_k[:, None] / total_channels + EPS) * k_gain).astype(
        jnp.bfloat16
    )
    v_hat = value_part.astype(jnp.bfloat16)
    packed = jnp.concatenate([k_hat, v_hat], axis=1)
    marks = (seg_ids + 1).astype(jnp.bfloat16)
    reach = (MOST + rows_here - 2) // rows_here
    left_side = []
    right_side = []
    for distance in range(1, reach + 1):
        for direction in (1, -1):
            arrived = from_behind((packed, marks), "seq", direction * distance)
            if direction > 0:
                left_side.insert(0, arrived)
            else:
                right_side.append(arrived)
    window = left_side + [(packed, marks)] + right_side
    near_keys = jnp.concatenate([entry[0] for entry in window], axis=0)
    near_marks = jnp.concatenate([entry[1] for entry in window], axis=0)
    allowed = marks[:, None] == near_marks[None, :]
    scale = 1.0 / math.sqrt(HEAD_DIM)
    outputs = []
    for head_index in range(heads_here):
        first_col = head_index * HEAD_DIM
        q_head = q_hat[:, first_col : first_col + HEAD_DIM]
        k_head = near_keys[:, first_col : first_col + HEAD_DIM]
        v_head = near_keys[:, channels + first_col : channels + first_col + HEAD_DIM]
        scores = jnp.einsum("qd,kd->qk", q_head, k_head, preferred_element_type=jnp.float32) * scale
        scores = jnp.where(allowed, scores, -1e30)
        highest = jnp.max(scores, axis=1, keepdims=True)
        expo = jnp.exp(scores - highest)
        weights = (expo / jnp.sum(expo, axis=1, keepdims=True)).astype(jnp.bfloat16)
        outputs.append(
            jnp.dot(weights, v_head, preferred_element_type=jnp.float32).astype(jnp.bfloat16)
        )
    return jnp.concatenate(outputs, axis=1)


def solution(mesh):
    return jax.shard_map(
        on_device,
        mesh=mesh,
        in_specs=(
            P("seq", None),
            P(),
            P("seq", "head"),
            P("seq", "head"),
            P("seq", "head"),
            P("head"),
            P("head"),
            P("seq"),
        ),
        out_specs=P("seq", "head"),
        check_vma=False,
    )
```

profile of v0, /device:TPU:24, one launch (start us, length us, event | category | flops | bytes accessed | tf_op | source)
XLA Modules:
  0.0 599.2 jit_solution(8748373051620311312)
XLA Ops:
  6.5 0.0 all-gather.9.cloned.1.call-start
  6.5 0.7 all-gather.9.cloned.1.call-update
  7.3 0.0 all-gather.11.cloned.1.call-start
  7.3 0.7 all-gather.11.cloned.1.call-update
  8.0 0.0 all-gather.7.cloned.1.call-start
  8.1 0.7 all-gather.7.cloned.1.call-update
  8.7 0.0 copy-start.3
  8.8 3.4 fusion.2
  12.2 142.0 %all-gather.9.cloned.1.call-done = bf16[64,50,256]{2,1,0:T(8,128)(2,1)} async-done(((bf16[1,50,256]{2,1,0:T(8,128)(2,1)}), bf16[64,50,256]{2,1,0:T(8,128)(2,1)}) %all-gather.9.cloned.1.call-update) | async-done | bytes 1638416 | tf_op jit(solution)/shard_map/all_gather | solution.py:36
  154.1 2.5 reshape.28
  156.6 137.1 %all-gather.11.cloned.1.call-done = bf16[64,50,256]{2,1,0:T(8,128)(2,1)} async-done(((bf16[1,50,256]{2,1,0:T(8,128)(2,1)}), bf16[64,50,256]{2,1,0:T(8,128)(2,1)}) %all-gather.11.cloned.1.call-update) | async-done | bytes 1638416 | tf_op jit(solution)/shard_map/all_gather | solution.py:37
  293.8 3.7 reshape.30
  297.5 0.0 copy-done.3
  297.5 4.9 convolution_convert_fusion
  302.4 0.0 slice-done
  302.4 0.0 slice-done.1
  302.4 0.0 copy-done.4
  302.4 1.9 multiply_reduce_fusion
  304.3 129.2 %all-gather.7.cloned.1.call-done = bf16[64,50,256]{2,1,0:T(8,128)(2,1)} async-done(((bf16[1,50,256]{2,1,0:T(8,128)(2,1)}), bf16[64,50,256]{2,1,0:T(8,128)(2,1)}) %all-gather.7.cloned.1.call-update) | async-done | bytes 1638416 | tf_op jit(solution)/shard_map/all_gather | solution.py:35
  433.4 2.5 reshape.26
  436.0 0.0 copy-start.1
  436.0 0.0 copy-start
  436.0 0.0 copy-start.2
  436.0 5.1 multiply_reduce_fusion.1
  441.1 12.6 %all-reduce = (f32[768]{0:T(1024)S(1)}, f32[768]{0:T(1024)S(1)}) all-reduce(f32[768]{0:T(1024)S(1)} %get-tuple-element.7, f32[768]{0:T(1024)S(1)} %get-tuple-element.9), channel_id=1, replica_groups=mesh['head'=8,'seq'=64] {'head'}, use_global_device_ids=true, to_apply=%region_4.0 | all-reduce | flops 1536 | bytes 12288 | tf_op jit(solution)/shard_map/psum | solution.py:38
  453.8 0.0 copy-done.1
  453.8 0.1 multiply_convert_fusion
  453.9 0.1 pad_maximum_fusion
  454.0 3.2 collective-permute-start.5
  457.1 3.4 collective-permute-start.4
  460.6 0.0 copy-done
  460.6 3.7 collective-permute-start
  464.3 3.5 collective-permute-start.1
  467.8 4.5 collective-permute-start.2
  472.2 38.9 %collective-permute-done = bf16[768]{0:T(1024)(128)(2,1)S(1)} collective-permute-done((bf16[768]{0:T(1024)(128)(2,1)S(1)}, bf16[768]{0:T(1024)(128)(2,1)S(1)}, u32[]{:S(2)}, u32[]{:S(2)}) %collective-permute-start) | collective-permute-done | bytes 1568 | tf_op jit(solution)/shard_map/ppermute | solution.py:19
  511.2 1.9 collective-permute-start.3
  513.1 0.2 dynamic-update-slice.5
  513.3 0.0 collective-permute-done.1
  513.3 0.2 dynamic-update-slice.6
  513.5 0.2 dynamic-update-slice.7
  513.7 0.0 collective-permute-done.2
  513.8 0.2 dynamic-update-slice.8
  514.0 3.7 collective-permute-done.3
  517.6 4.0 collective-permute-start.7
  521.7 3.0 collective-permute-start.6
  524.6 0.0 copy-start.6
  524.7 1.2 multiply_convert_fusion.1
  525.9 0.0 collective-permute-done.4
  525.9 0.1 constant_dynamic-update-slice_fusion.4
  526.0 0.0 collective-permute-done.5
  526.0 0.1 constant_dynamic-update-slice_fusion.3
  526.1 0.1 constant_dynamic-update-slice_fusion.2
  526.1 40.3 %collective-permute-done.6 = bf16[768,512]{0,1:T(8,128)(2,1)S(1)} collective-permute-done((bf16[768,512]{0,1:T(8,128)(2,1)S(1)}, bf16[768,512]{0,1:T(8,128)(2,1)S(1)}, u32[]{:S(2)}, u32[]{:S(2)}) %collective-permute-start.6) | collective-permute-done | bytes 786464 | tf_op jit(solution)/shard_map/ppermute | solution.py:19
  566.4 0.1 constant_dynamic-update-slice_fusion.1
  566.5 0.0 collective-permute-done.7
  566.5 0.1 constant_dynamic-update-slice_fusion
  566.6 0.0 copy-done.6
  566.6 5.6 fusion.20
  572.2 2.3 fusion.21
  574.5 6.0 %fusion.1 = f32[768]{0:T(1024)S(1)} fusion(f32[768,3840]{1,0:T(8,128)} %get-tuple-element.12, f32[768]{0:T(1024)S(1)} %get-tuple-element.11), kind=kLoop, calls=%fused_computation.9 | loop fusion | flops 5897472 | bytes 11802624 | tf_op jit(solution)/shard_map/reduce_sum | solution.py:75
  580.5 6.9 %fusion.7 = bf16[768,128]{0,1:T(8,128)(2,1)S(1)} fusion(f32[768,3840]{1,0:T(8,128)} %get-tuple-element.12, f32[768]{0:T(1024)S(1)} %fusion.1, f32[768]{0:T(1024)S(1)} %get-tuple-element.11, bf16[3840,512]{0,1:T(8,128)(2,1)S(1)} %constant_dynamic-update-slice_fusion), kind=kOutput, calls=%fused_computation.16 | convolution fusion | flops 763920384 | bytes 12984320 | tf_op jit(solution)/shard_map/dot_general | solution.py:77
  587.4 1.8 fusion
  589.2 2.6 fusion.8
  591.8 0.9 copy.11
  (14 shorter events, 0.1 us)
Async XLA Ops:
  6.5 147.6 %all-gather.9.cloned.1.call-start = ((), (), s32[]{:S(2)}) async-start(), calls=%async_computation.1 | async-start | bytes 1863680 | tf_op jit(solution)/shard_map/all_gather | solution.py:36
  7.3 286.5 %all-gather.11.cloned.1.call-start = ((), (), s32[]{:S(2)}) async-start(), calls=%async_computation.2 | async-start | bytes 1863680 | tf_op jit(solution)/shard_map/all_gather | solution.py:37
  8.0 425.4 %all-gather.7.cloned.1.call-start = ((), (), s32[]{:S(2)}) async-start(), calls=%async_computation | async-start | bytes 1863680 | tf_op jit(solution)/shard_map/all_gather | solution.py:35
  8.7 288.8 %copy-start.3 = (f32[3200]{0:T(1024)S(1)}, f32[3200]{0:T(1024)}, u32[]{:S(2)}) copy-start(f32[3200]{0:T(1024)} %param.9) | copy-start | bytes 38404
  293.8 8.6 %slice-start = ((s8[4915200]{0:T(1024)(128)(4,1)}), s8[720896]{0:T(1024)(128)(4,1)S(1)}, s32[]{:S(2)}) async-start(s8[4915200]{0:T(1024)(128)(4,1)} %bitcast.6), calls=%async_computation.3 | async-start | bytes 1441792
  297.5 4.9 slice-start.1
  297.5 4.9 copy-start.4
  436.0 17.8 %copy-start.1 = (f32[256]{0:T(256)S(1)}, f32[256]{0:T(256)}, u32[]{:S(2)}) copy-start(f32[256]{0:T(256)} %param.14) | copy-start | bytes 3076
  436.0 24.6 %copy-start = (s32[768]{0:T(1024)S(1)}, s32[768]{0:T(1024)}, u32[]{:S(2)}) copy-start(s32[768]{0:T(1024)} %param.15) | copy-start | bytes 9220
  436.0 88.7 %copy-start.2 = (f32[256]{0:T(256)S(1)}, f32[256]{0:T(256)}, u32[]{:S(2)}) copy-start(f32[256]{0:T(256)} %param.13) | copy-start | bytes 3076
  454.0 72.0 %collective-permute-start.5 = (bf16[768,512]{0,1:T(8,128)(2,1)S(1)}, bf16[768,512]{0,1:T(8,128)(2,1)S(1)}, u32[]{:S(2)}, u32[]{:S(2)}) collective-permute-start(bf16[768,512]{0,1:T(8,128)(2,1)S(1)} %pad_maximum_fusion), channel_id=1, source_target_pairs={{0,1},{1,2},{2,3},{3,4},{4,5},{5,6},{6,7},{7,8},{8,9},{9,10},{10,1... | collective-permute-start | bytes 2359304 | tf_op jit(solution)/shard_map/ppermute | solution.py:19
  457.1 68.8 %collective-permute-start.4 = (bf16[768,512]{0,1:T(8,128)(2,1)S(1)}, bf16[768,512]{0,1:T(8,128)(2,1)S(1)}, u32[]{:S(2)}, u32[]{:S(2)}) collective-permute-start(bf16[768,512]{0,1:T(8,128)(2,1)S(1)} %pad_maximum_fusion), channel_id=1, source_target_pairs={{0,2},{1,3},{2,4},{3,5},{4,6},{5,7},{6,8},{7,9},{8,10},{9,11},{10,... | collective-permute-start | bytes 2359304 | tf_op jit(solution)/shard_map/ppermute | solution.py:19
  460.6 50.6 %collective-permute-start = (bf16[768]{0:T(1024)(128)(2,1)S(1)}, bf16[768]{0:T(1024)(128)(2,1)S(1)}, u32[]{:S(2)}, u32[]{:S(2)}) collective-permute-start(bf16[768]{0:T(1024)(128)(2,1)S(1)} %add_convert_fusion), channel_id=1, source_target_pairs={{0,2},{1,3},{2,4},{3,5},{4,6},{5,7},{6,8},{7,9},{8,10},{9,11},{10,... | collective-permute-start | bytes 4616 | tf_op jit(solution)/shard_map/ppermute | solution.py:19
  464.3 49.1 %collective-permute-start.1 = (bf16[768]{0:T(1024)(128)(2,1)S(1)}, bf16[768]{0:T(1024)(128)(2,1)S(1)}, u32[]{:S(2)}, u32[]{:S(2)}) collective-permute-start(bf16[768]{0:T(1024)(128)(2,1)S(1)} %add_convert_fusion), channel_id=1, source_target_pairs={{0,1},{1,2},{2,3},{3,4},{4,5},{5,6},{6,7},{7,8},{8,9},{9,10},{10,1... | collective-permute-start | bytes 4616 | tf_op jit(solution)/shard_map/ppermute | solution.py:19
  467.8 46.0 %collective-permute-start.2 = (bf16[768]{0:T(1024)(128)(2,1)S(1)}, bf16[768]{0:T(1024)(128)(2,1)S(1)}, u32[]{:S(2)}, u32[]{:S(2)}) collective-permute-start(bf16[768]{0:T(1024)(128)(2,1)S(1)} %add_convert_fusion), channel_id=1, source_target_pairs={{1,0},{2,1},{3,2},{4,3},{5,4},{6,5},{7,6},{8,7},{9,8},{10,9},{11,1... | collective-permute-start | bytes 4616 | tf_op jit(solution)/shard_map/ppermute | solution.py:19
  511.2 6.5 %collective-permute-start.3 = (bf16[768]{0:T(1024)(128)(2,1)S(1)}, bf16[768]{0:T(1024)(128)(2,1)S(1)}, u32[]{:S(2)}, u32[]{:S(2)}) collective-permute-start(bf16[768]{0:T(1024)(128)(2,1)S(1)} %add_convert_fusion), channel_id=1, source_target_pairs={{2,0},{3,1},{4,2},{5,3},{6,4},{7,5},{8,6},{9,7},{10,8},{11,9},{12,... | collective-permute-start | bytes 4616 | tf_op jit(solution)/shard_map/ppermute | solution.py:19
  517.6 7.0 %copy-start.5 = (bf16[3840]{0:T(1024)(128)(2,1)}, bf16[3840]{0:T(1024)(128)(2,1)S(1)}, u32[]{:S(2)}) copy-start(bf16[3840]{0:T(1024)(128)(2,1)S(1)} %constant_dynamic-update-slice_fusion.5) | copy-start | bytes 23044
  517.6 48.8 %collective-permute-start.7 = (bf16[768,512]{0,1:T(8,128)(2,1)S(1)}, bf16[768,512]{0,1:T(8,128)(2,1)S(1)}, u32[]{:S(2)}, u32[]{:S(2)}) collective-permute-start(bf16[768,512]{0,1:T(8,128)(2,1)S(1)} %pad_maximum_fusion), channel_id=1, source_target_pairs={{2,0},{3,1},{4,2},{5,3},{6,4},{7,5},{8,6},{9,7},{10,8},{11,9},{12,... | collective-permute-start | bytes 2359304 | tf_op jit(solution)/shard_map/ppermute | solution.py:19
  521.7 44.8 %collective-permute-start.6 = (bf16[768,512]{0,1:T(8,128)(2,1)S(1)}, bf16[768,512]{0,1:T(8,128)(2,1)S(1)}, u32[]{:S(2)}, u32[]{:S(2)}) collective-permute-start(bf16[768,512]{0,1:T(8,128)(2,1)S(1)} %pad_maximum_fusion), channel_id=1, source_target_pairs={{1,0},{2,1},{3,2},{4,3},{5,4},{6,5},{7,6},{8,7},{9,8},{10,9},{11,1... | collective-permute-start | bytes 2359304 | tf_op jit(solution)/shard_map/ppermute | solution.py:19
  524.6 41.9 %copy-start.6 = (bf16[3840]{0:T(1024)(128)(2,1)S(1)}, bf16[3840]{0:T(1024)(128)(2,1)}, u32[]{:S(2)}) copy-start(bf16[3840]{0:T(1024)(128)(2,1)} %copy-done.5) | copy-start | bytes 23044
Sparse Core Ops, SparseCore 0:
  10.3 143.7 all-gather.8
  157.1 136.6 all-gather.10
  296.8 136.6 all-gather.6
where the time goes:
time: 601 us; the launch traced here: 599 us
  waiting for transfers between devices  493 us (82%)
  matrix products  29.2 us (5%)
  starting transfers between devices  27.1 us (5%)
  between operations  13.4 us (2%)
  other arithmetic  12.7 us (2%)
  blocking collectives  12.6 us (2%)
  local copies, waits for them, and re-layouts  10.7 us (2%)
    all_gather x1, waiting for transfers between devices, on_device(): key_part = add_rows(lax.all_gather(w_key, 'seq', axis=0, tiled=True))  142 us
    all_gather x1, waiting for transfers between devices, on_device(): value_part = add_rows(lax.all_gather(w_value, 'seq', axis=0, tiled=True))  137 us
    all_gather x1, waiting for transfers between devices, on_device(): queries = add_rows(lax.all_gather(w_query, 'seq', axis=0, tiled=True))  129 us
    ppermute x8, waiting for transfers between devices, from_behind(): return lax.ppermute(shard, axis, pairs)  82.9 us
    ppermute x8, starting transfers between devices, from_behind(): return lax.ppermute(shard, axis, pairs)  27.1 us
    psum x1, blocking collectives, on_device(): lax.psum((jnp.sum(queries * queries, axis=1), jnp.sum(key_part * key_part...  12.6 us
  transfers between devices with their start and end apart: 11, of which 6 were waited for; matrix products, arithmetic and copies ran while one was open for 3% of the time, Pallas kernels for 0%

commit v1 on v0

v1 whole, which is shorter than its diff:
```python
import functools
import math

import jax
import jax.numpy as jnp
from jax import lax
from jax.experimental import pallas as pl
from jax.experimental.pallas import tpu as pltpu
from jax.sharding import PartitionSpec as P

HEADS = 16
HEAD_DIM = 128
MOST = 1025
EPS = 1e-06
NY = 4
NZ = 16
N_SEQ = NY * NZ
N_HEAD = 8
ROWS = 768
FAR = 256
WINDOW = 2 * FAR + 3 * ROWS
CHUNK = 256
Q_BLOCK = 256
NEG = -1e30

OVER_Y = [[y * NZ + z for y in range(NY)] for z in range(NZ)]
OVER_Z = [[y * NZ + z for z in range(NZ)] for y in range(NY)]


def copies_to_all(value, axis, size, groups=None):
    stacked = jnp.broadcast_to(value[None], (size,) + value.shape)
    return lax.all_to_all(stacked, axis, 0, 0, axis_index_groups=groups)


def shifted(value, by):
    pairs = [(i, i + by) for i in range(N_SEQ) if 0 <= i + by < N_SEQ]
    return lax.ppermute(value, "seq", pairs)


def halo(value):
    far = value[ROWS - FAR :]
    near = value[:FAR]
    return shifted(far, 2), shifted(value, 1), shifted(value, -1), shifted(near, -2)


def attend_kernel(
    lo_ref, hi_ref, q_ref, own_ref, near_ref, ka, kb, kc, kd, ke, va, vb, vc, vd, ve,
    out_ref, k_win, v_win, s_ref,
):
    start = 0
    for k_part, v_part in ((ka, va), (kb, vb), (kc, vc), (kd, vd), (ke, ve)):
        rows = k_part.shape[0]
        k_win[start : start + rows, :] = k_part[...]
        v_win[start : start + rows, :] = v_part[...]
        start += rows
    scale = 1.0 / math.sqrt(HEAD_DIM)
    heads_here = q_ref.shape[1] // HEAD_DIM
    for block in range(ROWS // Q_BLOCK):
        first, last = lo_ref[block], hi_ref[block]
        r0 = block * Q_BLOCK
        own = own_ref[r0 : r0 + Q_BLOCK, :]
        for head in range(heads_here):
            c0 = head * HEAD_DIM
            q = q_ref[r0 : r0 + Q_BLOCK, c0 : c0 + HEAD_DIM]

            def scores(c, top):
                k = k_win[pl.ds(c * CHUNK, CHUNK), c0 : c0 + HEAD_DIM]
                s = lax.dot_general(
                    q, k, (((1,), (1,)), ((), ())), preferred_element_type=jnp.float32
                )
                s = jnp.where(own == near_ref[c], s * scale, NEG)
                s_ref[c] = s
                for part in range(CHUNK // 128):
                    top = jnp.maximum(top, s[:, part * 128 : part * 128 + 128])
                return top

            top = lax.fori_loop(
                first, last, scores, jnp.full((Q_BLOCK, 128), NEG, jnp.float32)
            )
            highest = jnp.max(top, axis=1, keepdims=True)

            def expos(c, total):
                e = jnp.exp(s_ref[c] - highest)
                s_ref[c] = e
                for part in range(CHUNK // 128):
                    total = total + e[:, part * 128 : part * 128 + 128]
                return total

            total = lax.fori_loop(first, last, expos, jnp.zeros((Q_BLOCK, 128), jnp.float32))
            inverse = 1.0 / jnp.sum(total, axis=1, keepdims=True)

            def mix(c, acc):
                w = (s_ref[c] * inverse).astype(jnp.bfloat16)
                v = v_win[pl.ds(c * CHUNK, CHUNK), c0 : c0 + HEAD_DIM]
                return acc + jnp.dot(w, v, preferred_element_type=jnp.float32)

            acc = lax.fori_loop(first, last, mix, jnp.zeros((Q_BLOCK, HEAD_DIM), jnp.float32))
            out_ref[r0 : r0 + Q_BLOCK, c0 : c0 + HEAD_DIM] = acc.astype(jnp.bfloat16)


def attend(lo, hi, q, own, near, k_parts, v_parts):
    vmem = pl.BlockSpec(memory_space=pltpu.VMEM)
    smem = pl.BlockSpec(memory_space=pltpu.SMEM)
    width = q.shape[1]
    return pl.pallas_call(
        attend_kernel,
        out_shape=jax.ShapeDtypeStruct((ROWS, width), jnp.bfloat16),
        in_specs=[smem, smem] + [vmem] * 13,
        out_specs=vmem,
        scratch_shapes=[
            pltpu.VMEM((WINDOW, width), jnp.bfloat16),
            pltpu.VMEM((WINDOW, width), jnp.bfloat16),
            pltpu.VMEM((WINDOW // CHUNK, Q_BLOCK, CHUNK), jnp.float32),
        ],
        compiler_params=pltpu.CompilerParams(vmem_limit_bytes=32 << 20),
        cost_estimate=pl.CostEstimate(
            flops=4 * ROWS * WINDOW * width, transcendentals=ROWS * WINDOW * 2, bytes_accessed=4 << 20
        ),
        name="attend",
    )(lo, hi, q, own, near, *k_parts, *v_parts)


def on_device(tokens, ln_gain, w_query, w_key, w_value, q_gain, k_gain, seg_ids):
    total_channels = HEADS * HEAD_DIM
    width = w_query.shape[1]
    vq = copies_to_all(jnp.concatenate([w_value, w_query], axis=1), "seq", NY, OVER_Y)
    w_key, vq = lax.optimization_barrier((w_key, vq))
    vq = lax.all_gather(vq, "seq", axis=0, axis_index_groups=OVER_Z)
    k_z = lax.all_gather(w_key, "seq", axis=0, axis_index_groups=OVER_Z)
    k_all = copies_to_all(k_z, "seq", NY, OVER_Y).reshape(-1, width)

    floats = tokens.astype(jnp.float32)
    normed = (
        floats * lax.rsqrt(jnp.mean(floats * floats, axis=1, keepdims=True) + EPS) * ln_gain
    ).astype(jnp.bfloat16)
    normed = lax.optimization_barrier(normed)

    def project(rows):
        return jnp.dot(normed, rows, preferred_element_type=jnp.float32)

    def unit(values, gain):
        own = jnp.sum(values * values, axis=1)
        square = jnp.sum(copies_to_all(own, "head", N_HEAD), axis=0)
        return (values * lax.rsqrt(square[:, None] / total_channels + EPS) * gain).astype(
            jnp.bfloat16
        )

    marks = seg_ids + 1
    mark_parts = halo(marks.astype(jnp.bfloat16))
    k_hat = unit(project(k_all), k_gain)
    k_parts = halo(k_hat)

    vq = jnp.transpose(vq, (1, 0, 2, 3)).reshape(-1, 2 * width)
    v_hat = project(vq[:, :width]).astype(jnp.bfloat16)
    v_parts = halo(v_hat)
    q_hat = unit(project(vq[:, width:]), q_gain)

    near = jnp.concatenate(
        [p.astype(jnp.int32) for p in mark_parts[:2]] + [marks] + [p.astype(jnp.int32) for p in mark_parts[2:]]
    )
    blocks = marks.reshape(-1, Q_BLOCK)
    low, high = blocks[:, :1], blocks[:, -1:]
    hit = (near[None, :] >= low) & (near[None, :] <= high)
    spots = jnp.arange(WINDOW, dtype=jnp.int32)[None, :]
    lo = jnp.min(jnp.where(hit, spots, WINDOW), axis=1) // CHUNK
    hi = jnp.max(jnp.where(hit, spots, -1), axis=1) // CHUNK + 1
    return attend(
        lo,
        hi,
        q_hat,
        marks[:, None],
        near.reshape(WINDOW // CHUNK, 1, CHUNK),
        (*k_parts[:2], k_hat, *k_parts[2:]),
        (*v_parts[:2], v_hat, *v_parts[2:]),
    )


def solution(mesh):
    return jax.shard_map(
        on_device,
        mesh=mesh,
        in_specs=(
            P("seq", None),
            P(),
            P("seq", "head"),
            P("seq", "head"),
            P("seq", "head"),
            P("head"),
            P("head"),
            P("seq"),
        ),
        out_specs=P("seq", "head"),
        check_vma=False,
    )
```

time: 601 us -> 218 us (0.36)
  the two profiles are of different devices: /device:TPU:24 before, /device:TPU:42 now
where the time goes in v1:
time: 218 us; the launch traced here: 217 us
  starting transfers between devices  67.1 us (31%)
  blocking collectives  42.9 us (20%)
  waiting for transfers between devices  27.5 us (13%)
  local copies, waits for them, and re-layouts  22.8 us (10%)
  Pallas kernels  19.3 us (9%)
  matrix products  13.9 us (6%)
  between operations  13.8 us (6%)
  other arithmetic  9.83 us (5%)
    ppermute x12, starting transfers between devices, shifted(): return lax.ppermute(value, 'seq', pairs)  52.6 us
    all_gather x1, blocking collectives, on_device(): k_z = lax.all_gather(w_key, 'seq', axis=0, axis_index_groups=OVER_Z)  33.1 us
    pallas_call x1, Pallas kernels, attend(): pl.pallas_call(attend_kernel, out_shape=jax.ShapeDtypeStruct((ROWS, width...  19.3 us
    all_to_all x3, waiting for transfers between devices, copies_to_all(): return lax.all_to_all(stacked, axis, 0, 0, axis_index_groups=groups)  17 us
    all_to_all x3, starting transfers between devices, copies_to_all(): return lax.all_to_all(stacked, axis, 0, 0, axis_index_groups=groups)  14.5 us
    dot_general x3, matrix products, project(): return jnp.dot(normed, rows, preferred_element_type=jnp.float32)  13.9 us
    ppermute x12, waiting for transfers between devices, shifted(): return lax.ppermute(value, 'seq', pairs)  10.4 us
    all_to_all x1, blocking collectives, copies_to_all(): return lax.all_to_all(stacked, axis, 0, 0, axis_index_groups=groups)  9.86 us
  transfers between devices with their start and end apart: 16, of which 4 were waited for; matrix products, arithmetic and copies ran while one was open for 21% of the time, Pallas kernels for 0%

profile of v1, /device:TPU:42, one launch (start us, length us, event | category | flops | bytes accessed | tf_op | source)
XLA Modules:
  0.0 217.1 jit_solution(18411553269151715710)
XLA Ops:
  6.5 0.8 pad_maximum_fusion
  7.3 9.9 %all_to_all.22 = bf16[4,50,512]{2,1,0:T(8,128)(2,1)} all-to-all(bf16[4,50,512]{2,1,0:T(8,128)(2,1)S(1)} %broadcast_in_dim.60), channel_id=1, replica_groups={{0,16,32,48},{1,17,33,49},{2,18,34,50},{3,19,35,51},{4,20,36,52},{5,21,..., dimensions={0} | all-to-all | bytes 409600 | tf_op jit(solution)/shard_map/all_to_all | solution.py:32
  17.2 0.0 all-gather.5.cloned.1.call-update
  17.2 0.7 broadcast_add_fusion
  17.9 2.0 collective-permute-start.2
  19.9 3.8 %collective-permute-start.1 = (bf16[768]{0:T(1024)(128)(2,1)S(1)}, bf16[768]{0:T(1024)(128)(2,1)S(1)}, u32[]{:S(2)}, u32[]{:S(2)}) collective-permute-start(bf16[768]{0:T(1024)(128)(2,1)S(1)} %get-tuple-element.18), channel_id=1, source_target_pairs={{0,1},{1,2},{2,3},{3,4},{4,5},{5,6},{6,7},{7,8},{8,9},{9,10},{10,1... | collective-permute-start | bytes 4616 | tf_op jit(solution)/shard_map/ppermute | solution.py:37
  23.8 14.0 %collective-permute-start.3 = (bf16[256]{0:T(256)(128)(2,1)S(1)}, bf16[256]{0:T(256)(128)(2,1)S(1)}, u32[]{:S(2)}, u32[]{:S(2)}) collective-permute-start(bf16[256]{0:T(256)(128)(2,1)S(1)} %get-tuple-element.19), channel_id=1, source_target_pairs={{2,0},{3,1},{4,2},{5,3},{6,4},{7,5},{8,6},{9,7},{10,8},{11,9},{12,... | collective-permute-start | bytes 1544 | tf_op jit(solution)/shard_map/ppermute | solution.py:37
  37.7 1.9 collective-permute-start
  39.7 0.0 copy-start
  39.7 0.2 broadcast_in_dim.65.own_ref
  39.9 3.6 %fusion = f32[768]{0:T(1024)S(1)} fusion(bf16[768,3200]{1,0:T(8,128)(2,1)} %param.8), kind=kLoop, calls=%fused_computation.2 | loop fusion | flops 7372032 | bytes 4918272 | tf_op jit(solution)/shard_map/reduce_sum | solution.py:134
  43.5 0.1 copy-done
  43.6 4.0 %fusion.2 = bf16[768,3200]{1,0:T(8,128)(2,1)} fusion(bf16[768,3200]{1,0:T(8,128)(2,1)S(1)} %copy-done, f32[3200]{0:T(1024)S(1)} %copy-done.3, f32[768]{0:T(1024)S(1)} %add_rsqrt_fusion.2), kind=kLoop, calls=%fused_computation.4 | loop fusion | flops 9830400 | bytes 9846272 | tf_op jit(solution)/shard_map/convert_element_type | solution.py:135
  47.7 0.2 slice_reduce_fusion.1
  47.8 0.0 copy-done.2
  47.8 33.1 %all-gather.2 = bf16[16,50,256]{2,1,0:T(8,128)(2,1)S(1)} all-gather(bf16[1,50,256]{2,1,0:T(8,128)(2,1)S(1)} %bitcast.11), channel_id=3, replica_groups={{0,1,2,3,4,5,6,7,8,9,10,11,12,13,14,15},{16,17,18,19,20,21,22,23,24,25,..., dimensions={0}, use_global_device_ids=true | all-gather | bytes 435200 | tf_op jit(solution)/shard_map/all_gather | solution.py:129
  80.9 0.1 copy.36
  81.0 1.3 broadcast_in_dim.63
  82.3 5.2 %all-to-all-start.2 = ((bf16[4,16,50,256]{3,1,2,0:T(8,128)(2,1)}), bf16[4,16,50,256]{3,1,2,0:T(8,128)(2,1)}, u32[]{:S(2)}, u32[]{:S(2)}) async-start(bf16[4,16,50,256]{3,1,2,0:T(8,128)(2,1)} %broadcast_in_dim.63), calls=%async_computation.2 | async-start | bytes 3276800 | tf_op jit(solution)/shard_map/all_to_all | solution.py:32
  87.5 0.0 collective-permute-done
  87.5 0.0 collective-permute-done.1
  87.5 0.0 collective-permute-done.2
  87.6 0.0 collective-permute-done.3
  87.6 0.2 select_reduce_fusion
  87.8 13.4 %all-to-all-done.2 = bf16[4,16,50,256]{3,1,2,0:T(8,128)(2,1)} async-done(((bf16[4,16,50,256]{3,1,2,0:T(8,128)(2,1)}), bf16[4,16,50,256]{3,1,2,0:T(8,128)(2,1)}, u32[]{:S(2)}, u32[]{:S(2)}) %all-to-all-start.2) | async-done | bytes 1638432 | tf_op jit(solution)/shard_map/all_to_all | solution.py:32
  101.2 2.1 copy.37
  103.3 1.5 reshape.57
  104.7 4.5 %multiply_reduce_fusion = (f32[768]{0:T(1024)S(1)}, f32[768,256]{0,1:T(8,128)S(1)}) fusion(bf16[768,3200]{1,0:T(8,128)(2,1)} %fusion.2, bf16[3200,256]{1,0:T(8,128)(2,1)} %reshape.57), kind=kOutput, calls=%fused_computation.12 | convolution fusion | flops 1258683648 | bytes 7343104 | tf_op jit(solution)/shard_map/dot_general | solution.py:139
  109.2 0.6 broadcast_in_dim.64
  109.8 4.6 %all-to-all-start.3 = ((f32[8,1,768]{2,1,0:T(1,128)}), f32[8,1,768]{2,1,0:T(1,128)S(1)}, u32[]{:S(2)}, u32[]{:S(2)}) async-start(f32[8,1,768]{2,1,0:T(1,128)} %broadcast_in_dim.64), calls=%async_computation.3 | async-start | bytes 49152 | tf_op jit(solution)/shard_map/all_to_all | solution.py:32
  114.5 0.3 copy.39
  114.8 3.6 %all-to-all-done.3 = f32[8,1,768]{2,1,0:T(1,128)S(1)} async-done(((f32[8,1,768]{2,1,0:T(1,128)}), f32[8,1,768]{2,1,0:T(1,128)S(1)}, u32[]{:S(2)}, u32[]{:S(2)}) %all-to-all-start.3) | async-done | bytes 24608 | tf_op jit(solution)/shard_map/all_to_all | solution.py:32
  118.4 0.2 multiply_convert_fusion.kc
  118.6 4.0 %collective-permute-start.6 = (bf16[768,256]{1,0:T(8,128)(2,1)S(1)}, bf16[768,256]{1,0:T(8,128)(2,1)S(1)}, u32[]{:S(2)}, u32[]{:S(2)}) collective-permute-start(bf16[768,256]{1,0:T(8,128)(2,1)S(1)} %multiply_convert_fusion.kc), channel_id=1, source_target_pairs={{1,0},{2,1},{3,2},{4,3},{5,4},{6,5},{7,6},{8,7},{9,8},{10,9},{11,1... | collective-permute-start | bytes 1179656 | tf_op jit(solution)/shard_map/ppermute | solution.py:37
  122.6 1.9 collective-permute-start.5
  124.5 0.7 fusion.13
  125.2 6.1 %collective-permute-start.7 = (bf16[256,256]{1,0:T(8,128)(2,1)}, bf16[256,256]{1,0:T(8,128)(2,1)S(1)}, u32[]{:S(2)}, u32[]{:S(2)}) collective-permute-start(bf16[256,256]{1,0:T(8,128)(2,1)} %get-tuple-element.15), channel_id=1, source_target_pairs={{2,0},{3,1},{4,2},{5,3},{6,4},{7,5},{8,6},{9,7},{10,8},{11,9},{12,... | collective-permute-start | bytes 393224 | tf_op jit(solution)/shard_map/ppermute | solution.py:37
  131.4 2.1 collective-permute-start.4
  133.5 0.0 all-gather.5.cloned.1.call-done
  133.5 3.7 %copy.45 = bf16[16,4,50,512]{3,1,0,2:T(4,128)(2,1)S(1)} copy(bf16[16,4,50,512]{3,2,1,0:T(8,128)(2,1)} %bitcast.10) | data formatting | bytes 6553600 | tf_op jit(solution)/shard_map/all_gather | solution.py:128
  137.3 3.7 %copy.33 = bf16[4,16,50,512]{3,2,1,0:T(8,128)(2,1)} copy(bf16[4,16,50,512]{3,0,1,2:T(4,128)(2,1)S(1)} %bitcast.9) | data formatting | bytes 6553600 | tf_op jit(solution)/shard_map/transpose | solution.py:153
  141.0 5.6 %reshape.55 = bf16[3200,512]{1,0:T(8,128)(2,1)} reshape(bf16[4,16,50,512]{3,2,1,0:T(8,128)(2,1)} %copy.33) | data formatting | bytes 6553600 | tf_op jit(solution)/shard_map/reshape | solution.py:153
  146.5 4.5 %fusion.7.vc = bf16[768,256]{1,0:T(8,128)(2,1)S(1)} fusion(bf16[768,3200]{1,0:T(8,128)(2,1)} %fusion.2, bf16[3200,512]{1,0:T(8,128)(2,1)} %reshape.55), kind=kOutput, calls=%fused_computation.10 | convolution fusion | flops 1258487808 | bytes 6946816 | tf_op jit(solution)/shard_map/dot_general | solution.py:139
  151.1 0.0 copy-start.6
  151.1 4.9 %multiply_reduce_fusion.1 = (f32[768]{0:T(1024)S(1)}, f32[768,256]{0,1:T(8,128)}) fusion(bf16[768,3200]{1,0:T(8,128)(2,1)} %fusion.2, bf16[3200,512]{1,0:T(8,128)(2,1)S(1)} %copy-done.1), kind=kOutput, calls=%fused_computation.14 | convolution fusion | flops 1258683648 | bytes 7343104 | tf_op jit(solution)/shard_map/dot_general | solution.py:139
  156.0 0.6 broadcast_in_dim.61
  156.6 4.7 %all-to-all-start.1 = ((f32[8,1,768]{2,1,0:T(1,128)}), f32[8,1,768]{2,1,0:T(1,128)S(1)}, u32[]{:S(2)}, u32[]{:S(2)}) async-start(f32[8,1,768]{2,1,0:T(1,128)} %broadcast_in_dim.61), calls=%async_computation.1 | async-start | bytes 49152 | tf_op jit(solution)/shard_map/all_to_all | solution.py:32
  161.3 0.7 fusion.12
  162.0 2.6 %collective-permute-start.10 = (bf16[768,256]{1,0:T(8,128)(2,1)S(1)}, bf16[768,256]{1,0:T(8,128)(2,1)S(1)}, u32[]{:S(2)}, u32[]{:S(2)}) collective-permute-start(bf16[768,256]{1,0:T(8,128)(2,1)S(1)} %fusion.7.vc), channel_id=1, source_target_pairs={{1,0},{2,1},{3,2},{4,3},{5,4},{6,5},{7,6},{8,7},{9,8},{10,9},{11,1... | collective-permute-start | bytes 1179656 | tf_op jit(solution)/shard_map/ppermute | solution.py:37
  164.6 1.4 copy.35
  166.0 0.0 all-to-all-done.1
  166.1 0.0 collective-permute-done.7.ke
  166.1 3.3 %collective-permute-start.9 = (bf16[768,256]{1,0:T(8,128)(2,1)S(1)}, bf16[768,256]{1,0:T(8,128)(2,1)S(1)}, u32[]{:S(2)}, u32[]{:S(2)}) collective-permute-start(bf16[768,256]{1,0:T(8,128)(2,1)S(1)} %fusion.7.vc), channel_id=1, source_target_pairs={{0,1},{1,2},{2,3},{3,4},{4,5},{5,6},{6,7},{7,8},{8,9},{9,10},{10,1... | collective-permute-start | bytes 1179656 | tf_op jit(solution)/shard_map/ppermute | solution.py:37
  169.4 0.0 collective-permute-done.4.ka
  169.4 9.0 %collective-permute-start.11 = (bf16[256,256]{1,0:T(8,128)(2,1)}, bf16[256,256]{1,0:T(8,128)(2,1)S(1)}, u32[]{:S(2)}, u32[]{:S(2)}) collective-permute-start(bf16[256,256]{1,0:T(8,128)(2,1)} %get-tuple-element.13), channel_id=1, source_target_pairs={{2,0},{3,1},{4,2},{5,3},{6,4},{7,5},{8,6},{9,7},{10,8},{11,9},{12,... | collective-permute-start | bytes 393224 | tf_op jit(solution)/shard_map/ppermute | solution.py:37
  178.4 0.0 collective-permute-done.6.kd
  178.4 1.9 collective-permute-start.8
  180.4 0.2 multiply_convert_fusion.1.q_ref
  180.5 0.0 collective-permute-done.5.kb
  180.6 2.5 %collective-permute-done.11.ve = bf16[256,256]{1,0:T(8,128)(2,1)S(1)} collective-permute-done((bf16[256,256]{1,0:T(8,128)(2,1)}, bf16[256,256]{1,0:T(8,128)(2,1)S(1)}, u32[]{:S(2)}, u32[]{:S(2)}) %collective-permute-start.11) | collective-permute-done | bytes 131104 | tf_op jit(solution)/shard_map/ppermute | solution.py:37
  183.0 7.9 %collective-permute-done.8.va = bf16[256,256]{1,0:T(8,128)(2,1)S(1)} collective-permute-done((bf16[256,256]{1,0:T(8,128)(2,1)}, bf16[256,256]{1,0:T(8,128)(2,1)S(1)}, u32[]{:S(2)}, u32[]{:S(2)}) %collective-permute-start.8) | collective-permute-done | bytes 131104 | tf_op jit(solution)/shard_map/ppermute | solution.py:37
  190.9 0.0 collective-permute-done.10.vd
  190.9 0.0 collective-permute-done.9.vb
  190.9 19.3 %attend.1 = bf16[768,256]{1,0:T(8,128)(2,1)} custom-call(s32[3]{0:T(128)S(1)} %get-tuple-element.25.lo_ref, s32[3]{0:T(128)S(1)} %get-tuple-element.26.hi_ref, bf16[768,256]{1,0:T(8,128)(2,1)S(1)} %multiply_convert_fusion.1.q_ref, s32[768,1]{1,0:T(8,128)S(1)} %broadcast_in_dim.65.own_ref, s32[11,1,256]{2,1,0:T(1,128)S(1)} %reshape.56.near_ref, ...), custom_call_target="tpu_custom_call" | custom-call | flops 2214592512 | bytes 4194304 | tf_op jit(solution)/shard_map/attend/pallas_call | solution.py:105
  (27 shorter events, 0.2 us)
Async XLA Ops:
  6.5 37.0 %copy-start.3 = (f32[3200]{0:T(1024)S(1)}, f32[3200]{0:T(1024)}, u32[]{:S(2)}) copy-start(f32[3200]{0:T(1024)} %param.9) | copy-start | bytes 38404
  6.5 127.0 %all-gather.5.cloned.1.call-start = ((), (), s32[]{:S(2)}) async-start(), calls=%async_computation.4 | async-start | bytes 3899392 | tf_op jit(solution)/shard_map/all_gather | solution.py:128
  17.9 69.6 %collective-permute-start.2 = (bf16[768]{0:T(1024)(128)(2,1)S(1)}, bf16[768]{0:T(1024)(128)(2,1)S(1)}, u32[]{:S(2)}, u32[]{:S(2)}) collective-permute-start(bf16[768]{0:T(1024)(128)(2,1)S(1)} %get-tuple-element.18), channel_id=1, source_target_pairs={{1,0},{2,1},{3,2},{4,3},{5,4},{6,5},{7,6},{8,7},{9,8},{10,9},{11,1... | collective-permute-start | bytes 4616 | tf_op jit(solution)/shard_map/ppermute | solution.py:37
  19.9 67.6 %collective-permute-start.1 = (bf16[768]{0:T(1024)(128)(2,1)S(1)}, bf16[768]{0:T(1024)(128)(2,1)S(1)}, u32[]{:S(2)}, u32[]{:S(2)}) collective-permute-start(bf16[768]{0:T(1024)(128)(2,1)S(1)} %get-tuple-element.18), channel_id=1, source_target_pairs={{0,1},{1,2},{2,3},{3,4},{4,5},{5,6},{6,7},{7,8},{8,9},{9,10},{10,1... | collective-permute-start | bytes 4616 | tf_op jit(solution)/shard_map/ppermute | solution.py:37
  23.8 63.8 %collective-permute-start.3 = (bf16[256]{0:T(256)(128)(2,1)S(1)}, bf16[256]{0:T(256)(128)(2,1)S(1)}, u32[]{:S(2)}, u32[]{:S(2)}) collective-permute-start(bf16[256]{0:T(256)(128)(2,1)S(1)} %get-tuple-element.19), channel_id=1, source_target_pairs={{2,0},{3,1},{4,2},{5,3},{6,4},{7,5},{8,6},{9,7},{10,8},{11,9},{12,... | collective-permute-start | bytes 1544 | tf_op jit(solution)/shard_map/ppermute | solution.py:37
  37.7 49.7 %collective-permute-start = (bf16[256]{0:T(256)(128)(2,1)S(1)}, bf16[256]{0:T(256)(128)(2,1)S(1)}, u32[]{:S(2)}, u32[]{:S(2)}) collective-permute-start(bf16[256]{0:T(256)(128)(2,1)S(1)} %get-tuple-element.20), channel_id=1, source_target_pairs={{0,2},{1,3},{2,4},{3,5},{4,6},{5,7},{6,8},{7,9},{8,10},{9,11},{10,... | collective-permute-start | bytes 1544 | tf_op jit(solution)/shard_map/ppermute | solution.py:37
  39.7 3.9 %copy-start = (bf16[768,3200]{1,0:T(8,128)(2,1)S(1)}, bf16[768,3200]{1,0:T(8,128)(2,1)}, u32[]{:S(2)}) copy-start(bf16[768,3200]{1,0:T(8,128)(2,1)} %param.8) | copy-start | bytes 14745604
  43.6 4.2 %copy-start.2 = (bf16[50,256]{1,0:T(8,128)(2,1)S(1)}, bf16[50,256]{1,0:T(8,128)(2,1)}, u32[]{:S(2)}) copy-start(bf16[50,256]{1,0:T(8,128)(2,1)} %param.11) | copy-start | bytes 76804
  47.7 39.9 %copy-start.4 = (s32[768]{0:T(1024)S(1)}, s32[768]{0:T(1024)}, u32[]{:S(2)}) copy-start(s32[768]{0:T(1024)} %param.15) | copy-start | bytes 9220
  82.3 18.9 %all-to-all-start.2 = ((bf16[4,16,50,256]{3,1,2,0:T(8,128)(2,1)}), bf16[4,16,50,256]{3,1,2,0:T(8,128)(2,1)}, u32[]{:S(2)}, u32[]{:S(2)}) async-start(bf16[4,16,50,256]{3,1,2,0:T(8,128)(2,1)} %broadcast_in_dim.63), calls=%async_computation.2 | async-start | bytes 3276800 | tf_op jit(solution)/shard_map/all_to_all | solution.py:32
  104.7 13.7 %copy-start.5 = (f32[256]{0:T(256)S(1)}, f32[256]{0:T(256)}, u32[]{:S(2)}) copy-start(f32[256]{0:T(256)} %param.14) | copy-start | bytes 3076
  109.8 8.6 %all-to-all-start.3 = ((f32[8,1,768]{2,1,0:T(1,128)}), f32[8,1,768]{2,1,0:T(1,128)S(1)}, u32[]{:S(2)}, u32[]{:S(2)}) async-start(f32[8,1,768]{2,1,0:T(1,128)} %broadcast_in_dim.64), calls=%async_computation.3 | async-start | bytes 49152 | tf_op jit(solution)/shard_map/all_to_all | solution.py:32
  118.6 59.8 %collective-permute-start.6 = (bf16[768,256]{1,0:T(8,128)(2,1)S(1)}, bf16[768,256]{1,0:T(8,128)(2,1)S(1)}, u32[]{:S(2)}, u32[]{:S(2)}) collective-permute-start(bf16[768,256]{1,0:T(8,128)(2,1)S(1)} %multiply_convert_fusion.kc), channel_id=1, source_target_pairs={{1,0},{2,1},{3,2},{4,3},{5,4},{6,5},{7,6},{8,7},{9,8},{10,9},{11,1... | collective-permute-start | bytes 1179656 | tf_op jit(solution)/shard_map/ppermute | solution.py:37
  122.6 58.0 %collective-permute-start.5 = (bf16[768,256]{1,0:T(8,128)(2,1)S(1)}, bf16[768,256]{1,0:T(8,128)(2,1)S(1)}, u32[]{:S(2)}, u32[]{:S(2)}) collective-permute-start(bf16[768,256]{1,0:T(8,128)(2,1)S(1)} %multiply_convert_fusion.kc), channel_id=1, source_target_pairs={{0,1},{1,2},{2,3},{3,4},{4,5},{5,6},{6,7},{7,8},{8,9},{9,10},{10,1... | collective-permute-start | bytes 1179656 | tf_op jit(solution)/shard_map/ppermute | solution.py:37
  125.2 40.8 %collective-permute-start.7 = (bf16[256,256]{1,0:T(8,128)(2,1)}, bf16[256,256]{1,0:T(8,128)(2,1)S(1)}, u32[]{:S(2)}, u32[]{:S(2)}) collective-permute-start(bf16[256,256]{1,0:T(8,128)(2,1)} %get-tuple-element.15), channel_id=1, source_target_pairs={{2,0},{3,1},{4,2},{5,3},{6,4},{7,5},{8,6},{9,7},{10,8},{11,9},{12,... | collective-permute-start | bytes 393224 | tf_op jit(solution)/shard_map/ppermute | solution.py:37
  131.4 38.0 %collective-permute-start.4 = (bf16[256,256]{1,0:T(8,128)(2,1)}, bf16[256,256]{1,0:T(8,128)(2,1)S(1)}, u32[]{:S(2)}, u32[]{:S(2)}) collective-permute-start(bf16[256,256]{1,0:T(8,128)(2,1)} %get-tuple-element.16), channel_id=1, source_target_pairs={{0,2},{1,3},{2,4},{3,5},{4,6},{5,7},{6,8},{7,9},{8,10},{9,11},{10,... | collective-permute-start | bytes 393224 | tf_op jit(solution)/shard_map/ppermute | solution.py:37
  146.5 4.5 %copy-start.1 = (bf16[3200,512]{1,0:T(8,128)(2,1)S(1)}, bf16[3200,512]{1,0:T(8,128)(2,1)}, u32[]{:S(2)}) copy-start(bf16[3200,512]{1,0:T(8,128)(2,1)} %reshape.55) | copy-start | bytes 9830404
  151.1 29.3 %copy-start.6 = (f32[256]{0:T(256)S(1)}, f32[256]{0:T(256)}, u32[]{:S(2)}) copy-start(f32[256]{0:T(256)} %param.13) | copy-start | bytes 3076
  156.6 9.4 %all-to-all-start.1 = ((f32[8,1,768]{2,1,0:T(1,128)}), f32[8,1,768]{2,1,0:T(1,128)S(1)}, u32[]{:S(2)}, u32[]{:S(2)}) async-start(f32[8,1,768]{2,1,0:T(1,128)} %broadcast_in_dim.61), calls=%async_computation.1 | async-start | bytes 49152 | tf_op jit(solution)/shard_map/all_to_all | solution.py:32
  162.0 28.9 %collective-permute-start.10 = (bf16[768,256]{1,0:T(8,128)(2,1)S(1)}, bf16[768,256]{1,0:T(8,128)(2,1)S(1)}, u32[]{:S(2)}, u32[]{:S(2)}) collective-permute-start(bf16[768,256]{1,0:T(8,128)(2,1)S(1)} %fusion.7.vc), channel_id=1, source_target_pairs={{1,0},{2,1},{3,2},{4,3},{5,4},{6,5},{7,6},{8,7},{9,8},{10,9},{11,1... | collective-permute-start | bytes 1179656 | tf_op jit(solution)/shard_map/ppermute | solution.py:37
  166.1 24.9 %collective-permute-start.9 = (bf16[768,256]{1,0:T(8,128)(2,1)S(1)}, bf16[768,256]{1,0:T(8,128)(2,1)S(1)}, u32[]{:S(2)}, u32[]{:S(2)}) collective-permute-start(bf16[768,256]{1,0:T(8,128)(2,1)S(1)} %fusion.7.vc), channel_id=1, source_target_pairs={{0,1},{1,2},{2,3},{3,4},{4,5},{5,6},{6,7},{7,8},{8,9},{9,10},{10,1... | collective-permute-start | bytes 1179656 | tf_op jit(solution)/shard_map/ppermute | solution.py:37
  169.4 13.7 %collective-permute-start.11 = (bf16[256,256]{1,0:T(8,128)(2,1)}, bf16[256,256]{1,0:T(8,128)(2,1)S(1)}, u32[]{:S(2)}, u32[]{:S(2)}) collective-permute-start(bf16[256,256]{1,0:T(8,128)(2,1)} %get-tuple-element.13), channel_id=1, source_target_pairs={{2,0},{3,1},{4,2},{5,3},{6,4},{7,5},{8,6},{9,7},{10,8},{11,9},{12,... | collective-permute-start | bytes 393224 | tf_op jit(solution)/shard_map/ppermute | solution.py:37
  178.4 12.5 %collective-permute-start.8 = (bf16[256,256]{1,0:T(8,128)(2,1)}, bf16[256,256]{1,0:T(8,128)(2,1)S(1)}, u32[]{:S(2)}, u32[]{:S(2)}) collective-permute-start(bf16[256,256]{1,0:T(8,128)(2,1)} %get-tuple-element.14), channel_id=1, source_target_pairs={{0,2},{1,3},{2,4},{3,5},{4,6},{5,7},{6,8},{7,9},{8,10},{9,11},{10,... | collective-permute-start | bytes 393224 | tf_op jit(solution)/shard_map/ppermute | solution.py:37
Sparse Core Ops, SparseCore 0:
  17.3 81.5 all-gather.4

commit v2 on v1

v2 whole, which is shorter than its diff:
```python
import math

import jax
import jax.numpy as jnp
from jax import lax
from jax.experimental import pallas as pl
from jax.experimental.pallas import tpu as pltpu
from jax.sharding import PartitionSpec as P

D = 3200
HEADS = 16
HEAD_DIM = 128
MOST = 1025
EPS = 1e-06
NX = 4
NY = 4
NZ = 16
N_SEQ = NY * NZ
N_HEAD = 8
ROWS = 768
FAR = 256
NEAR_PART = ROWS // N_HEAD
FAR_PART = FAR // N_HEAD
HALF = NEAR_PART + FAR_PART
WINDOW = 2 * FAR + 3 * ROWS
OWN = FAR + ROWS
BLOCK = 256
N_BLOCKS = WINDOW // BLOCK
Q_BLOCKS = ROWS // BLOCK
CHUNK = 256
NEG = -1e30
SHARD_ROWS = D // N_SEQ

OVER_Y = [[y * NZ + z for y in range(NY)] for z in range(NZ)]
OVER_Z = [[y * NZ + z for z in range(NZ)] for y in range(NY)]
VMEM = pl.BlockSpec(memory_space=pltpu.VMEM)
SMEM = pl.BlockSpec(memory_space=pltpu.SMEM)
ANY = pl.BlockSpec(memory_space=pl.ANY)


def copies_to_all(value, axis, size, groups=None):
    stacked = jnp.broadcast_to(value[None], (size,) + value.shape)
    return lax.all_to_all(stacked, axis, 0, 0, axis_index_groups=groups)


def shifted(value, by):
    pairs = [(i, i + by) for i in range(N_SEQ) if 0 <= i + by < N_SEQ]
    return lax.ppermute(value, "seq", pairs)


def along_x(value, by):
    pairs = [(2 * x + c, 2 * ((x + by) % NX) + c) for x in range(NX) for c in range(2)]
    return lax.ppermute(value, "head", pairs)


def other_core(value):
    return lax.ppermute(value, "head", [(i, i ^ 1) for i in range(N_HEAD)])


def norm_kernel(x_ref, gain_ref, out_ref, plain, moved):
    x = x_ref[...].astype(jnp.float32)
    mean = jnp.sum(x * x, axis=1, keepdims=True) * (1.0 / D)
    plain[...] = x * lax.rsqrt(mean + EPS) * gain_ref[...]
    for z in range(NZ):
        for y in range(NY):
            source = (y * NZ + z) * SHARD_ROWS
            target = (z * NY + y) * SHARD_ROWS
            moved[:, target : target + SHARD_ROWS] = plain[:, source : source + SHARD_ROWS]
    out_ref[...] = moved[...].astype(jnp.bfloat16)


def norm(tokens, gain):
    rows = 128
    return pl.pallas_call(
        norm_kernel,
        out_shape=jax.ShapeDtypeStruct((ROWS, D), jnp.bfloat16),
        grid=(ROWS // rows,),
        in_specs=[
            pl.BlockSpec((rows, D), lambda i: (i, 0)),
            pl.BlockSpec((1, D), lambda i: (0, 0)),
        ],
        out_specs=pl.BlockSpec((rows, D), lambda i: (i, 0)),
        scratch_shapes=[pltpu.VMEM((rows, D), jnp.float32)] * 2,
        compiler_params=pltpu.CompilerParams(vmem_limit_bytes=24 << 20),
        name="norm",
    )(tokens, gain)


def window_kernel(shards_ref, own_ref, *refs):
    parts, out_ref, sem = refs[:-2], refs[-2], refs[-1]
    copies = [pltpu.make_async_copy(own_ref, out_ref.at[pl.ds(OWN, ROWS)], sem.at[0])]

    def move(ref, at, rows, to):
        n = len(copies)
        to = pl.multiple_of(to, 32)
        copies.append(
            pltpu.make_async_copy(
                ref.at[pl.ds(at, rows)], out_ref.at[pl.ds(to, rows)], sem.at[n]
            )
        )

    for slot in range(N_HEAD):
        shard = shards_ref[slot]
        left, right = parts[2 * slot], parts[2 * slot + 1]
        move(left, 0, FAR_PART, shard * FAR_PART)
        move(left, FAR_PART, NEAR_PART, FAR + shard * NEAR_PART)
        move(right, 0, NEAR_PART, OWN + ROWS + shard * NEAR_PART)
        move(right, NEAR_PART, FAR_PART, OWN + 2 * ROWS + shard * FAR_PART)
    for copy in copies:
        copy.start()
    for copy in copies:
        copy.wait()


def window_of(shards, own, parts):
    return pl.pallas_call(
        window_kernel,
        out_shape=jax.ShapeDtypeStruct((WINDOW, D), jnp.bfloat16),
        in_specs=[SMEM] + [ANY] * (1 + len(parts)),
        out_specs=ANY,
        scratch_shapes=[pltpu.SemaphoreType.DMA((1 + 4 * N_HEAD,))],
        name="window",
    )(shards, own, *parts)


def row_squares(values):
    sums = jnp.sum(values * values, axis=1, keepdims=True)
    return jnp.transpose(jnp.broadcast_to(sums, (BLOCK, 128)))[:1]


def keys_kernel(x_ref, wq_ref, wk_ref, k_ref, ks_ref, q_ref, qs_ref):
    i = pl.program_id(0)
    x = x_ref[...]
    k = jnp.dot(x, wk_ref[...], preferred_element_type=jnp.float32)
    k_ref[...] = k
    ks_ref[0] = row_squares(k)

    @pl.when((i >= OWN // BLOCK) & (i < OWN // BLOCK + Q_BLOCKS))
    def _():
        q = jnp.dot(x, wq_ref[...], preferred_element_type=jnp.float32)
        q_ref[...] = q
        qs_ref[0] = row_squares(q)


def q_step(i):
    return jnp.clip(i - OWN // BLOCK, 0, Q_BLOCKS - 1)


def project_keys(window, w_all, width):
    return pl.pallas_call(
        keys_kernel,
        out_shape=(
            jax.ShapeDtypeStruct((WINDOW, width), jnp.float32),
            jax.ShapeDtypeStruct((N_BLOCKS, 1, BLOCK), jnp.float32),
            jax.ShapeDtypeStruct((ROWS, width), jnp.float32),
            jax.ShapeDtypeStruct((Q_BLOCKS, 1, BLOCK), jnp.float32),
        ),
        grid=(N_BLOCKS,),
        in_specs=[
            pl.BlockSpec((BLOCK, D), lambda i: (i, 0)),
            pl.BlockSpec((D, width), lambda i: (0, 0)),
            pl.BlockSpec((D, width), lambda i: (0, 1)),
        ],
        out_specs=(
            pl.BlockSpec((BLOCK, width), lambda i: (i, 0)),
            pl.BlockSpec((1, 1, BLOCK), lambda i: (i, 0, 0)),
            pl.BlockSpec((BLOCK, width), lambda i: (q_step(i), 0)),
            pl.BlockSpec((1, 1, BLOCK), lambda i: (q_step(i), 0, 0)),
        ),
        compiler_params=pltpu.CompilerParams(vmem_limit_bytes=32 << 20),
        name="keys",
    )(window, w_all, w_all)


def values_kernel(x_ref, w_ref, v_ref):
    v_ref[...] = jnp.dot(
        x_ref[...], w_ref[...], preferred_element_type=jnp.float32
    ).astype(jnp.bfloat16)


def project_values(window, w_all, width):
    return pl.pallas_call(
        values_kernel,
        out_shape=jax.ShapeDtypeStruct((WINDOW, width), jnp.bfloat16),
        grid=(N_BLOCKS,),
        in_specs=[
            pl.BlockSpec((BLOCK, D), lambda i: (i, 0)),
            pl.BlockSpec((D, width), lambda i: (0, 2)),
        ],
        out_specs=pl.BlockSpec((BLOCK, width), lambda i: (i, 0)),
        compiler_params=pltpu.CompilerParams(vmem_limit_bytes=32 << 20),
        name="values",
    )(window, w_all)


def attend_kernel(
    lo_ref, hi_ref, q_ref, k_ref, v_ref, squares_ref, q_gain_ref, k_gain_ref, own_ref, near_ref,
    out_ref, q_hat, k_hat, s_ref,
):
    total = squares_ref[0]
    for device in range(1, N_HEAD):
        total = total + squares_ref[device]
    factors = lax.rsqrt(total / (HEADS * HEAD_DIM) + EPS)
    heads_here = q_ref.shape[1] // HEAD_DIM

    def unit(source, target, gain, block, row):
        factor = jnp.transpose(jnp.broadcast_to(factors[row : row + 1], (128, BLOCK)))
        rows = slice(block * BLOCK, block * BLOCK + BLOCK)
        for head in range(heads_here):
            cols = slice(head * HEAD_DIM, head * HEAD_DIM + HEAD_DIM)
            target[rows, cols] = (source[rows, cols] * factor * gain[:, cols]).astype(jnp.bfloat16)

    for block in range(N_BLOCKS):
        unit(k_ref, k_hat, k_gain_ref, block, block)
    for block in range(Q_BLOCKS):
        unit(q_ref, q_hat, q_gain_ref, block, N_BLOCKS + block)

    scale = 1.0 / math.sqrt(HEAD_DIM)
    for block in range(Q_BLOCKS):
        first, last = lo_ref[block], hi_ref[block]
        r0 = block * BLOCK
        own = own_ref[r0 : r0 + BLOCK, :]
        for head in range(heads_here):
            c0 = head * HEAD_DIM
            q = q_hat[r0 : r0 + BLOCK, c0 : c0 + HEAD_DIM]

            def scores(c, top):
                k = k_hat[pl.ds(c * CHUNK, CHUNK), c0 : c0 + HEAD_DIM]
                s = lax.dot_general(
                    q, k, (((1,), (1,)), ((), ())), preferred_element_type=jnp.float32
                )
                s = jnp.where(own == near_ref[c], s * scale, NEG)
                s_ref[c] = s
                for part in range(CHUNK // 128):
                    top = jnp.maximum(top, s[:, part * 128 : part * 128 + 128])
                return top

            top = lax.fori_loop(first, last, scores, jnp.full((BLOCK, 128), NEG, jnp.float32))
            highest = jnp.max(top, axis=1, keepdims=True)

            def expos(c, total):
                e = jnp.exp(s_ref[c] - highest)
                s_ref[c] = e
                for part in range(CHUNK // 128):
                    total = total + e[:, part * 128 : part * 128 + 128]
                return total

            total = lax.fori_loop(first, last, expos, jnp.zeros((BLOCK, 128), jnp.float32))
            inverse = 1.0 / jnp.sum(total, axis=1, keepdims=True)

            def mix(c, acc):
                w = (s_ref[c] * inverse).astype(jnp.bfloat16)
                v = v_ref[pl.ds(c * CHUNK, CHUNK), c0 : c0 + HEAD_DIM]
                return acc + jnp.dot(w, v, preferred_element_type=jnp.float32)

            acc = lax.fori_loop(first, last, mix, jnp.zeros((BLOCK, HEAD_DIM), jnp.float32))
            out_ref[r0 : r0 + BLOCK, c0 : c0 + HEAD_DIM] = acc.astype(jnp.bfloat16)


def attend(lo, hi, q, k, v, squares, q_gain, k_gain, own, near):
    width = q.shape[1]
    return pl.pallas_call(
        attend_kernel,
        out_shape=jax.ShapeDtypeStruct((ROWS, width), jnp.bfloat16),
        in_specs=[SMEM, SMEM] + [VMEM] * 8,
        out_specs=VMEM,
        scratch_shapes=[
            pltpu.VMEM((ROWS, width), jnp.bfloat16),
            pltpu.VMEM((WINDOW, width), jnp.bfloat16),
            pltpu.VMEM((WINDOW // CHUNK, BLOCK, CHUNK), jnp.float32),
        ],
        compiler_params=pltpu.CompilerParams(vmem_limit_bytes=32 << 20),
        name="attend",
    )(lo, hi, q, k, v, squares, q_gain, k_gain, own, near)


def on_device(tokens, ln_gain, w_query, w_key, w_value, q_gain, k_gain, seg_ids):
    width = w_query.shape[1]
    w_all = jnp.concatenate([w_query, w_key, w_value], axis=1)
    w_all = copies_to_all(w_all, "seq", NY, OVER_Y).reshape(NY * SHARD_ROWS, 3 * width)
    w_all, tokens, seg_ids = lax.optimization_barrier((w_all, tokens, seg_ids))
    w_all = lax.all_gather(w_all, "seq", axis=0, axis_index_groups=OVER_Z, tiled=True)

    normed = norm(tokens, ln_gain[None, :])

    me = lax.axis_index("head")
    near_rows = lax.dynamic_slice_in_dim(normed, me * NEAR_PART, NEAR_PART, 0)
    last_rows = lax.dynamic_slice_in_dim(normed, ROWS - FAR + me * FAR_PART, FAR_PART, 0)
    first_rows = lax.dynamic_slice_in_dim(normed, me * FAR_PART, FAR_PART, 0)
    left = jnp.concatenate([shifted(last_rows, 2), shifted(near_rows, 1)], axis=0)
    right = jnp.concatenate([shifted(near_rows, -1), shifted(first_rows, -2)], axis=0)
    own = jnp.concatenate([left, right], axis=0)
    before = along_x(own, 1)
    after = along_x(own, -1)
    across_left = along_x(before[:HALF], 1)
    across_right = along_x(after[HALF:], -1)
    pairs = [
        (own[:HALF], own[HALF:]),
        (before[:HALF], before[HALF:]),
        (after[:HALF], after[HALF:]),
        (across_left, across_right),
    ]
    twins = [other_core(t) for t in (own, before, after, across_left, across_right)]
    pairs += [(t[:HALF], t[HALF:]) for t in twins[:3]] + [(twins[3], twins[4])]
    x, core = me // 2, me % 2
    shards = jnp.stack(
        [2 * ((x + by) % NX) + c for c in (core, 1 - core) for by in (0, NX - 1, 1, 2)]
    ).astype(jnp.int32)
    window = window_of(shards, normed, [half for pair in pairs for half in pair])

    marks = seg_ids + 1
    sent = marks.astype(jnp.bfloat16)
    near = jnp.concatenate(
        [
            shifted(sent[ROWS - FAR :], 2).astype(jnp.int32),
            shifted(sent, 1).astype(jnp.int32),
            marks,
            shifted(sent, -1).astype(jnp.int32),
            shifted(sent[:FAR], -2).astype(jnp.int32),
        ]
    )
    blocks = marks.reshape(-1, BLOCK)
    low, high = blocks[:, :1], blocks[:, -1:]
    hit = (near[None, :] >= low) & (near[None, :] <= high)
    spots = jnp.arange(WINDOW, dtype=jnp.int32)[None, :]
    lo = jnp.min(jnp.where(hit, spots, WINDOW), axis=1) // CHUNK
    hi = jnp.max(jnp.where(hit, spots, -1), axis=1) // CHUNK + 1

    keys, key_squares, queries, query_squares = project_keys(window, w_all, width)
    squares = jnp.concatenate([key_squares, query_squares], axis=0)[:, 0]
    squares = copies_to_all(squares, "head", N_HEAD)
    values = project_values(window, w_all, width)
    return attend(
        lo,
        hi,
        queries,
        keys,
        values,
        squares,
        q_gain[None, :],
        k_gain[None, :],
        marks[:, None],
        near.reshape(WINDOW // CHUNK, 1, CHUNK),
    )


def solution(mesh):
    return jax.shard_map(
        on_device,
        mesh=mesh,
        in_specs=(
            P("seq", None),
            P(),
            P("seq", "head"),
            P("seq", "head"),
            P("seq", "head"),
            P("head"),
            P("head"),
            P("seq"),
        ),
        out_specs=P("seq", "head"),
        check_vma=False,
    )
```

time: 218 us -> 773 us (3.55)
  the two profiles are of different devices: /device:TPU:42 before, /device:TPU:24 now
where the time goes in v2:
time: 773 us; the launch traced here: 771 us
  Pallas kernels  606 us (78%)
  starting transfers between devices  68 us (9%)
  waiting for transfers between devices  54.9 us (7%)
  local copies, waits for them, and re-layouts  25.2 us (3%)
  between operations  13.8 us (2%)
    pallas_call x1, Pallas kernels, window_of(): pl.pallas_call(window_kernel, out_shape=jax.ShapeDtypeStruct((WINDOW, D),...  548 us
    ppermute x4, waiting for transfers between devices, along_x(): return lax.ppermute(value, 'head', pairs)  38.4 us
    ppermute x8, starting transfers between devices, shifted(): return lax.ppermute(value, 'seq', pairs)  30 us
    pallas_call x1, Pallas kernels, attend(): pl.pallas_call(attend_kernel, out_shape=jax.ShapeDtypeStruct((ROWS, width...  19.6 us
  transfers between devices with their start and end apart: 20, of which 7 were waited for; matrix products, arithmetic and copies ran while one was open for 1% of the time, Pallas kernels for 73%

profile of v2, /device:TPU:24, one launch (start us, length us, event | category | flops | bytes accessed | tf_op | source)
XLA Modules:
  0.0 771.0 jit_solution(17603546200917859173)
XLA Ops:
  6.5 0.8 pad_maximum_fusion.2
  7.3 0.8 broadcast_in_dim.48
  8.1 9.0 %all-to-all-start = ((bf16[4,50,768]{2,1,0:T(8,128)(2,1)}), bf16[4,50,768]{2,1,0:T(8,128)(2,1)S(1)}, u32[]{:S(2)}, u32[]{:S(2)}) async-start(bf16[4,50,768]{2,1,0:T(8,128)(2,1)} %broadcast_in_dim.48), calls=%async_computation | async-start | bytes 688128 | tf_op jit(solution)/shard_map/all_to_all | solution.py:43
  17.1 0.7 broadcast_in_dim.53.gain_ref
  17.8 0.6 stack.35.shards_ref
  18.4 3.7 all-to-all-done
  22.1 0.8 reshape.12
  23.0 2.4 copy-done.3
  25.3 11.4 %norm.1.own_ref = bf16[768,3200]{1,0:T(8,128)(2,1)S(1)} custom-call(bf16[768,3200]{1,0:T(8,128)(2,1)S(1)} %copy-done.3, f32[1,3200]{1,0:T(1,128)S(1)} %broadcast_in_dim.53.gain_ref), custom_call_target="tpu_custom_call" | custom-call | tf_op jit(solution)/shard_map/norm/pallas_call | solution.py:74
  36.8 2.3 copy-done.2
  39.1 1.9 collective-permute-start.5
  41.0 6.9 collective-permute-start.6
  47.9 1.9 collective-permute-start.1
  49.9 6.0 collective-permute-start.2
  55.9 0.0 all-gather.2.cloned.1.call-update
  55.9 1.9 collective-permute-start
  57.9 1.1 constant_dynamic-slice_fusion
  58.9 0.2 slice_reduce_fusion.1
  59.1 0.2 broadcast_in_dim.59.own_ref
  59.3 5.1 collective-permute-done
  64.4 1.9 collective-permute-start.4
  66.4 0.0 collective-permute-done.1
  66.4 6.9 collective-permute-start.7
  73.3 1.9 collective-permute-done.4
  75.2 2.5 collective-permute-start.3
  77.7 0.0 collective-permute-done.5
  77.7 0.1 constant_dynamic-update-slice_fusion.3
  77.8 0.0 collective-permute-done.6
  77.8 0.1 constant_dynamic-update-slice_fusion.2
  77.9 5.7 collective-permute-done.7
  83.6 3.4 collective-permute-start.8
  87.1 0.0 collective-permute-done.2
  87.1 0.2 select_reduce_fusion
  87.4 3.7 collective-permute-start.9
  91.0 1.9 collective-permute-start.12
  92.9 1.0 pad_maximum_fusion.1.refs_1_
  93.9 1.0 pad_maximum_fusion.refs_0_
  94.9 25.6 %collective-permute-done.8 = bf16[256,3200]{1,0:T(8,128)(2,1)S(1)} collective-permute-done((bf16[256,3200]{1,0:T(8,128)(2,1)S(1)}, bf16[256,3200]{1,0:T(8,128)(2,1)S(1)}, u32[]{:S(2)}, u32[]{:S(2)}) %collective-permute-start.8) | collective-permute-done | bytes 1638432 | tf_op jit(solution)/shard_map/ppermute | solution.py:53
  120.5 1.0 fusion.6
  121.5 2.2 collective-permute-start.10
  123.7 1.9 collective-permute-start.14
  125.7 1.0 fusion.5
  126.7 4.9 collective-permute-start.11
  131.6 2.1 collective-permute-start.13
  133.7 1.3 fusion.4
  135.0 5.1 collective-permute-done.10.refs_6_
  140.1 1.9 collective-permute-start.15
  142.0 7.7 %collective-permute-done.11.refs_7_ = bf16[128,3200]{1,0:T(8,128)(2,1)S(1)} collective-permute-done((bf16[128,3200]{1,0:T(8,128)(2,1)S(1)}, bf16[128,3200]{1,0:T(8,128)(2,1)S(1)}, u32[]{:S(2)}, u32[]{:S(2)}) %collective-permute-start.11) | collective-permute-done | bytes 819232 | tf_op jit(solution)/shard_map/ppermute | solution.py:53
  149.7 1.9 collective-permute-start.16
  151.6 1.3 fusion.2
  152.9 1.3 fusion.3
  154.3 0.9 copy-done.12
  155.2 0.2 copy-done.13
  155.4 548.0 %window.1.x_ref = bf16[2816,3200]{1,0:T(8,128)(2,1)} custom-call(s32[8]{0:T(128)} %stack.35.shards_ref, bf16[768,3200]{1,0:T(8,128)(2,1)} %copy-done.2, bf16[128,3200]{1,0:T(8,128)(2,1)} %pad_maximum_fusion.refs_0_, bf16[128,3200]{1,0:T(8,128)(2,1)} %pad_maximum_fusion.1.refs_1_, bf16[128,3200]{1,0:T(8,128)(2,1)} %copy-done.8, ...), custom_call_target="tpu_custom_call" | custom-call | tf_op jit(solution)/shard_map/window/pallas_call | solution.py:116
  703.4 0.0 all-gather.2.cloned.1.call-done.wq_ref.wk_ref.w_ref
  703.5 2.4 copy-done
  705.9 14.4 %keys.1 = (f32[2816,256]{1,0:T(8,128)S(1)}, f32[11,1,256]{2,1,0:T(1,128)S(1)}, f32[768,256]{1,0:T(8,128)S(1)}, f32[3,1,256]{2,1,0:T(1,128)S(1)}) custom-call(bf16[2816,3200]{1,0:T(8,128)(2,1)} %window.1.x_ref, bf16[3200,768]{1,0:T(8,128)(2,1)S(1)} %copy-done, bf16[3200,768]{1,0:T(8,128)(2,1)S(1)} %copy-done), custom_call_target="tpu_custom_call" | custom-call | tf_op jit(solution)/shard_map/keys/pallas_call | solution.py:150
  720.3 1.6 copy-done.4
  721.9 0.7 broadcast_in_dim.55
  722.6 5.1 all-to-all-start.1
  727.7 2.4 copy-done.1
  730.1 12.6 %values.1.v_ref = bf16[2816,256]{1,0:T(8,128)(2,1)S(1)} custom-call(bf16[2816,3200]{1,0:T(8,128)(2,1)} %window.1.x_ref, bf16[3200,768]{1,0:T(8,128)(2,1)S(1)} %copy-done.1), custom_call_target="tpu_custom_call" | custom-call | tf_op jit(solution)/shard_map/values/pallas_call | solution.py:182
  742.8 1.8 copy-done.5
  744.6 19.6 %attend.1 = bf16[768,256]{1,0:T(8,128)(2,1)} custom-call(s32[3]{0:T(128)S(1)} %get-tuple-element.39.lo_ref, s32[3]{0:T(128)S(1)} %get-tuple-element.40.hi_ref, f32[768,256]{1,0:T(8,128)S(1)} %get-tuple-element.15.q_ref, f32[2816,256]{1,0:T(8,128)S(1)} %copy-done.5, bf16[2816,256]{1,0:T(8,128)(2,1)S(1)} %values.1.v_ref, ...), custom_call_target="tpu_custom_call" | custom-call | tf_op jit(solution)/shard_map/attend/pallas_call | solution.py:262
  (47 shorter events, 0.2 us)
Async XLA Ops:
  8.1 14.1 %all-to-all-start = ((bf16[4,50,768]{2,1,0:T(8,128)(2,1)}), bf16[4,50,768]{2,1,0:T(8,128)(2,1)S(1)}, u32[]{:S(2)}, u32[]{:S(2)}) async-start(bf16[4,50,768]{2,1,0:T(8,128)(2,1)} %broadcast_in_dim.48), calls=%async_computation | async-start | bytes 688128 | tf_op jit(solution)/shard_map/all_to_all | solution.py:43
  17.1 686.4 %all-gather.2.cloned.1.call-start = ((), (), s32[]{:S(2)}) async-start(), calls=%async_computation.2 | async-start | bytes 5222400 | tf_op jit(solution)/shard_map/all_gather | solution.py:282
  23.0 2.4 copy-start.3
  25.3 22.6 %copy-start.14 = (s32[768]{0:T(1024)S(1)}, s32[768]{0:T(1024)}, u32[]{:S(2)}) copy-start(s32[768]{0:T(1024)} %param.15) | copy-start | bytes 9220
  36.7 2.3 copy-start.2
  39.1 38.7 %collective-permute-start.5 = (bf16[96,3200]{1,0:T(8,128)(2,1)S(1)}, bf16[96,3200]{1,0:T(8,128)(2,1)S(1)}, u32[]{:S(2)}, u32[]{:S(2)}) collective-permute-start(bf16[96,3200]{1,0:T(8,128)(2,1)S(1)} %constant_dynamic-slice_fusion.1), channel_id=1, source_target_pairs={{0,1},{1,2},{2,3},{3,4},{4,5},{5,6},{6,7},{7,8},{8,9},{9,10},{10,1... | collective-permute-start | bytes 1843208 | tf_op jit(solution)/shard_map/ppermute | solution.py:48
  41.0 36.8 %collective-permute-start.6 = (bf16[96,3200]{1,0:T(8,128)(2,1)S(1)}, bf16[96,3200]{1,0:T(8,128)(2,1)S(1)}, u32[]{:S(2)}, u32[]{:S(2)}) collective-permute-start(bf16[96,3200]{1,0:T(8,128)(2,1)S(1)} %constant_dynamic-slice_fusion.1), channel_id=1, source_target_pairs={{1,0},{2,1},{3,2},{4,3},{5,4},{6,5},{7,6},{8,7},{9,8},{10,9},{11,1... | collective-permute-start | bytes 1843208 | tf_op jit(solution)/shard_map/ppermute | solution.py:48
  47.9 18.4 %collective-permute-start.1 = (bf16[768]{0:T(1024)(128)(2,1)S(1)}, bf16[768]{0:T(1024)(128)(2,1)S(1)}, u32[]{:S(2)}, u32[]{:S(2)}) collective-permute-start(bf16[768]{0:T(1024)(128)(2,1)S(1)} %get-tuple-element.36), channel_id=1, source_target_pairs={{0,1},{1,2},{2,3},{3,4},{4,5},{5,6},{6,7},{7,8},{8,9},{9,10},{10,1... | collective-permute-start | bytes 4616 | tf_op jit(solution)/shard_map/ppermute | solution.py:48
  49.9 37.2 %collective-permute-start.2 = (bf16[768]{0:T(1024)(128)(2,1)S(1)}, bf16[768]{0:T(1024)(128)(2,1)S(1)}, u32[]{:S(2)}, u32[]{:S(2)}) collective-permute-start(bf16[768]{0:T(1024)(128)(2,1)S(1)} %get-tuple-element.36), channel_id=1, source_target_pairs={{1,0},{2,1},{3,2},{4,3},{5,4},{6,5},{7,6},{8,7},{9,8},{10,9},{11,1... | collective-permute-start | bytes 4616 | tf_op jit(solution)/shard_map/ppermute | solution.py:48
  55.9 8.5 %collective-permute-start = (bf16[256]{0:T(256)(128)(2,1)S(1)}, bf16[256]{0:T(256)(128)(2,1)S(1)}, u32[]{:S(2)}, u32[]{:S(2)}) collective-permute-start(bf16[256]{0:T(256)(128)(2,1)S(1)} %get-tuple-element.38), channel_id=1, source_target_pairs={{0,2},{1,3},{2,4},{3,5},{4,6},{5,7},{6,8},{7,9},{8,10},{9,11},{10,... | collective-permute-start | bytes 1544 | tf_op jit(solution)/shard_map/ppermute | solution.py:48
  64.4 10.7 %collective-permute-start.4 = (bf16[32,3200]{1,0:T(8,128)(2,1)S(1)}, bf16[32,3200]{1,0:T(8,128)(2,1)S(1)}, u32[]{:S(2)}, u32[]{:S(2)}) collective-permute-start(bf16[32,3200]{1,0:T(8,128)(2,1)S(1)} %get-tuple-element.24), channel_id=1, source_target_pairs={{0,2},{1,3},{2,4},{3,5},{4,6},{5,7},{6,8},{7,9},{8,10},{9,11},{10,... | collective-permute-start | bytes 614408 | tf_op jit(solution)/shard_map/ppermute | solution.py:48
  66.4 17.2 %collective-permute-start.7 = (bf16[32,3200]{1,0:T(8,128)(2,1)S(1)}, bf16[32,3200]{1,0:T(8,128)(2,1)S(1)}, u32[]{:S(2)}, u32[]{:S(2)}) collective-permute-start(bf16[32,3200]{1,0:T(8,128)(2,1)S(1)} %get-tuple-element.23), channel_id=1, source_target_pairs={{2,0},{3,1},{4,2},{5,3},{6,4},{7,5},{8,6},{9,7},{10,8},{11,9},{12,... | collective-permute-start | bytes 614408 | tf_op jit(solution)/shard_map/ppermute | solution.py:48
  75.2 11.9 %collective-permute-start.3 = (bf16[256]{0:T(256)(128)(2,1)S(1)}, bf16[256]{0:T(256)(128)(2,1)S(1)}, u32[]{:S(2)}, u32[]{:S(2)}) collective-permute-start(bf16[256]{0:T(256)(128)(2,1)S(1)} %get-tuple-element.37), channel_id=1, source_target_pairs={{2,0},{3,1},{4,2},{5,3},{6,4},{7,5},{8,6},{9,7},{10,8},{11,9},{12,... | collective-permute-start | bytes 1544 | tf_op jit(solution)/shard_map/ppermute | solution.py:48
  83.6 36.9 %collective-permute-start.8 = (bf16[256,3200]{1,0:T(8,128)(2,1)S(1)}, bf16[256,3200]{1,0:T(8,128)(2,1)S(1)}, u32[]{:S(2)}, u32[]{:S(2)}) collective-permute-start(bf16[256,3200]{1,0:T(8,128)(2,1)S(1)} %constant_dynamic-update-slice_fusion.1), channel_id=1, source_target_pairs={{0,128},{64,192},{128,256},{192,320},{256,384},{320,448},{384,0},{... | collective-permute-start | bytes 4915208 | tf_op jit(solution)/shard_map/ppermute | solution.py:53
  87.4 36.4 %collective-permute-start.9 = (bf16[256,3200]{1,0:T(8,128)(2,1)S(1)}, bf16[256,3200]{1,0:T(8,128)(2,1)S(1)}, u32[]{:S(2)}, u32[]{:S(2)}) collective-permute-start(bf16[256,3200]{1,0:T(8,128)(2,1)S(1)} %constant_dynamic-update-slice_fusion.1), channel_id=1, source_target_pairs={{0,384},{64,448},{128,0},{192,64},{256,128},{320,192},{384,256},{4... | collective-permute-start | bytes 4915208 | tf_op jit(solution)/shard_map/ppermute | solution.py:53
  91.0 42.7 %collective-permute-start.12 = (bf16[256,3200]{1,0:T(8,128)(2,1)S(1)}, bf16[256,3200]{1,0:T(8,128)(2,1)S(1)}, u32[]{:S(2)}, u32[]{:S(2)}) collective-permute-start(bf16[256,3200]{1,0:T(8,128)(2,1)S(1)} %constant_dynamic-update-slice_fusion.1), channel_id=1, source_target_pairs={{0,64},{64,0},{128,192},{192,128},{256,320},{320,256},{384,448},{4... | collective-permute-start | bytes 4915208 | tf_op jit(solution)/shard_map/ppermute | solution.py:57
  121.5 5.2 copy-start.8
  121.5 18.5 %collective-permute-start.10 = (bf16[128,3200]{1,0:T(8,128)(2,1)S(1)}, bf16[128,3200]{1,0:T(8,128)(2,1)S(1)}, u32[]{:S(2)}, u32[]{:S(2)}) collective-permute-start(bf16[128,3200]{1,0:T(8,128)(2,1)S(1)} %get-tuple-element.34.refs_2_), channel_id=1, source_target_pairs={{0,128},{64,192},{128,256},{192,320},{256,384},{320,448},{384,0},{... | collective-permute-start | bytes 2457608 | tf_op jit(solution)/shard_map/ppermute | solution.py:53
  123.7 27.9 %collective-permute-start.14 = (bf16[256,3200]{1,0:T(8,128)(2,1)S(1)}, bf16[256,3200]{1,0:T(8,128)(2,1)S(1)}, u32[]{:S(2)}, u32[]{:S(2)}) collective-permute-start(bf16[256,3200]{1,0:T(8,128)(2,1)S(1)} %collective-permute-done.9), channel_id=1, source_target_pairs={{0,64},{64,0},{128,192},{192,128},{256,320},{320,256},{384,448},{4... | collective-permute-start | bytes 4915208 | tf_op jit(solution)/shard_map/ppermute | solution.py:57
  126.7 8.3 %copy-start.9 = (bf16[128,3200]{1,0:T(8,128)(2,1)}, bf16[128,3200]{1,0:T(8,128)(2,1)S(1)}, u32[]{:S(2)}) copy-start(bf16[128,3200]{1,0:T(8,128)(2,1)S(1)} %get-tuple-element.31.refs_5_) | copy-start | bytes 2457604
  126.7 23.0 %collective-permute-start.11 = (bf16[128,3200]{1,0:T(8,128)(2,1)S(1)}, bf16[128,3200]{1,0:T(8,128)(2,1)S(1)}, u32[]{:S(2)}, u32[]{:S(2)}) collective-permute-start(bf16[128,3200]{1,0:T(8,128)(2,1)S(1)} %get-tuple-element.31.refs_5_), channel_id=1, source_target_pairs={{0,384},{64,448},{128,0},{192,64},{256,128},{320,192},{384,256},{4... | collective-permute-start | bytes 2457608 | tf_op jit(solution)/shard_map/ppermute | solution.py:53
  131.6 21.4 %collective-permute-start.13 = (bf16[256,3200]{1,0:T(8,128)(2,1)S(1)}, bf16[256,3200]{1,0:T(8,128)(2,1)S(1)}, u32[]{:S(2)}, u32[]{:S(2)}) collective-permute-start(bf16[256,3200]{1,0:T(8,128)(2,1)S(1)} %collective-permute-done.8), channel_id=1, source_target_pairs={{0,64},{64,0},{128,192},{192,128},{256,320},{320,256},{384,448},{4... | collective-permute-start | bytes 4915208 | tf_op jit(solution)/shard_map/ppermute | solution.py:57
  140.1 12.9 %copy-start.10 = (bf16[128,3200]{1,0:T(8,128)(2,1)}, bf16[128,3200]{1,0:T(8,128)(2,1)S(1)}, u32[]{:S(2)}) copy-start(bf16[128,3200]{1,0:T(8,128)(2,1)S(1)} %collective-permute-done.10.refs_6_) | copy-start | bytes 2457604
  140.1 14.2 %collective-permute-start.15 = (bf16[128,3200]{1,0:T(8,128)(2,1)S(1)}, bf16[128,3200]{1,0:T(8,128)(2,1)S(1)}, u32[]{:S(2)}, u32[]{:S(2)}) collective-permute-start(bf16[128,3200]{1,0:T(8,128)(2,1)S(1)} %collective-permute-done.10.refs_6_), channel_id=1, source_target_pairs={{0,64},{64,0},{128,192},{192,128},{256,320},{320,256},{384,448},{4... | collective-permute-start | bytes 2457608 | tf_op jit(solution)/shard_map/ppermute | solution.py:57
  149.7 3.2 copy-start.11
  149.7 4.5 collective-permute-start.16
  154.3 0.9 copy-start.12
  154.3 1.1 copy-start.13
  703.5 2.4 copy-start
  720.3 1.6 copy-start.4
  722.6 20.1 %all-to-all-start.1 = ((f32[8,14,256]{2,1,0:T(8,128)}), f32[8,14,256]{2,1,0:T(8,128)S(1)}, u32[]{:S(2)}, u32[]{:S(2)}) async-start(f32[8,14,256]{2,1,0:T(8,128)} %broadcast_in_dim.55), calls=%async_computation.1 | async-start | bytes 262144 | tf_op jit(solution)/shard_map/all_to_all | solution.py:43
  727.7 2.4 copy-start.1
  730.1 12.6 %copy-start.6 = (f32[256]{0:T(256)S(1)}, f32[256]{0:T(256)}, u32[]{:S(2)}) copy-start(f32[256]{0:T(256)} %param.13) | copy-start | bytes 3076
  730.1 12.6 %copy-start.7 = (f32[256]{0:T(256)S(1)}, f32[256]{0:T(256)}, u32[]{:S(2)}) copy-start(f32[256]{0:T(256)} %param.14) | copy-start | bytes 3076
  742.8 1.8 copy-start.5
Sparse Core Ops, SparseCore 0:
  56.0 79.4 all-gather.1

commit v3 on v2

v3 whole, which is shorter than its diff:
```python
import math

import jax
import jax.numpy as jnp
from jax import lax
from jax.experimental import pallas as pl
from jax.experimental.pallas import tpu as pltpu
from jax.sharding import PartitionSpec as P

D = 3200
HEADS = 16
HEAD_DIM = 128
MOST = 1025
EPS = 1e-06
NX = 4
NY = 4
NZ = 16
N_SEQ = NY * NZ
N_HEAD = 8
ROWS = 768
FAR = 256
NEAR_PART = ROWS // N_HEAD
FAR_PART = FAR // N_HEAD
HALF = NEAR_PART + FAR_PART
WINDOW = 2 * FAR + 3 * ROWS
OWN = FAR + ROWS
BLOCK = 256
N_BLOCKS = WINDOW // BLOCK
Q_BLOCKS = ROWS // BLOCK
CHUNK = 256
NEG = -1e30
LIMIT = 24
SHARD_ROWS = D // N_SEQ

OVER_Y = [[y * NZ + z for y in range(NY)] for z in range(NZ)]
OVER_Z = [[y * NZ + z for z in range(NZ)] for y in range(NY)]
VMEM = pl.BlockSpec(memory_space=pltpu.VMEM)
SMEM = pl.BlockSpec(memory_space=pltpu.SMEM)
HBM = pl.BlockSpec(memory_space=pltpu.HBM)


def copies_to_all(value, axis, size, groups=None):
    stacked = jnp.broadcast_to(value[None], (size,) + value.shape)
    return lax.all_to_all(stacked, axis, 0, 0, axis_index_groups=groups)


def shifted(value, by):
    pairs = [(i, i + by) for i in range(N_SEQ) if 0 <= i + by < N_SEQ]
    return lax.ppermute(value, "seq", pairs)


def along_x(value, by):
    pairs = [(2 * x + c, 2 * ((x + by) % NX) + c) for x in range(NX) for c in range(2)]
    return lax.ppermute(value, "head", pairs)


def other_core(value):
    return lax.ppermute(value, "head", [(i, i ^ 1) for i in range(N_HEAD)])


def norm_kernel(x_ref, gain_ref, out_ref, plain, moved):
    x = x_ref[...].astype(jnp.float32)
    mean = jnp.sum(x * x, axis=1, keepdims=True) * (1.0 / D)
    plain[...] = x * lax.rsqrt(mean + EPS) * gain_ref[...]
    for z in range(NZ):
        for y in range(NY):
            source = (y * NZ + z) * SHARD_ROWS
            target = (z * NY + y) * SHARD_ROWS
            moved[:, target : target + SHARD_ROWS] = plain[:, source : source + SHARD_ROWS]
    out_ref[...] = moved[...].astype(jnp.bfloat16)


def norm(tokens, gain):
    rows = 128
    return pl.pallas_call(
        norm_kernel,
        out_shape=jax.ShapeDtypeStruct((ROWS, D), jnp.bfloat16),
        grid=(ROWS // rows,),
        in_specs=[
            pl.BlockSpec((rows, D), lambda i: (i, 0)),
            pl.BlockSpec((1, D), lambda i: (0, 0)),
        ],
        out_specs=pl.BlockSpec((rows, D), lambda i: (i, 0)),
        scratch_shapes=[pltpu.VMEM((rows, D), jnp.float32)] * 2,
        compiler_params=pltpu.CompilerParams(vmem_limit_bytes=10 << 20),
        cost_estimate=pl.CostEstimate(flops=1, transcendentals=0, bytes_accessed=1),
        name="norm",
    )(tokens, gain)


def row_squares(values):
    sums = jnp.sum(values * values, axis=1, keepdims=True)
    return jnp.transpose(jnp.broadcast_to(sums, (BLOCK, 128)))[:1]


def project_kernel(
    shards_ref, w_ref, own_ref, p0, p1, p2, p3l, p3r, p4, p5, p6, p7l, p7r,
    k_ref, q_ref, v_ref, squares_ref, x, w, sem,
):
    width = k_ref.shape[1]

    def columns(at, n):
        cols = pl.ds(at * width, width)
        return pltpu.make_async_copy(w_ref.at[:, cols], w.at[at], sem.at[n])

    def rows(ref, at, n):
        return pltpu.make_async_copy(ref, x.at[pl.ds(at, ref.shape[0])], sem.at[n])

    wq, wk, wv = columns(0, 0), columns(1, 1), columns(2, 2)
    own = rows(own_ref, 0, 3)
    pieces = [
        [rows(p0, ROWS, 4), rows(p1, ROWS + BLOCK, 5)],
        [rows(p2, ROWS + 2 * BLOCK, 6), rows(p3l, ROWS + 3 * BLOCK, 7)]
        + [rows(p3r, ROWS + 3 * BLOCK + HALF, 8)],
        [rows(p4, ROWS + 4 * BLOCK, 9), rows(p5, ROWS + 5 * BLOCK, 10)],
        [rows(p6, ROWS + 6 * BLOCK, 11), rows(p7l, ROWS + 7 * BLOCK, 12)]
        + [rows(p7r, ROWS + 7 * BLOCK + HALF, 13)],
    ]
    wk.start()
    own.start()
    for pair in pieces:
        for copy in pair:
            copy.start()
    wq.start()
    wv.start()

    def project(which, target, first):
        def dot(at, n):
            y = jnp.dot(x[at : at + n, :], w[which], preferred_element_type=jnp.float32)
            return y.astype(target.dtype)

        for block in range(Q_BLOCKS):
            at = block * BLOCK
            target[OWN + at : OWN + at + BLOCK, :] = dot(at, BLOCK)
        for pair in range(N_HEAD // 2):
            if first:
                for copy in pieces[pair]:
                    copy.wait()
            y = dot(ROWS + pair * 2 * BLOCK, 2 * BLOCK)
            for half in range(2):
                shard = shards_ref[2 * pair + half]
                far, near = shard * FAR_PART, shard * NEAR_PART
                part = y[half * BLOCK : half * BLOCK + BLOCK]
                places = (
                    (far, 0, FAR_PART),
                    (FAR + near, FAR_PART, NEAR_PART),
                    (OWN + ROWS + near, HALF, NEAR_PART),
                    (OWN + 2 * ROWS + far, HALF + NEAR_PART, FAR_PART),
                )
                for to, start, n in places:
                    target[pl.ds(pl.multiple_of(to, 32), n), :] = part[start : start + n]

    wk.wait()
    own.wait()
    project(1, k_ref, True)
    wq.wait()
    for block in range(Q_BLOCKS):
        here = slice(block * BLOCK, block * BLOCK + BLOCK)
        q_ref[here, :] = jnp.dot(x[here, :], w[0], preferred_element_type=jnp.float32)
    wv.wait()
    project(2, v_ref, False)
    for source, count, to in ((k_ref, N_BLOCKS, 0), (q_ref, Q_BLOCKS, N_BLOCKS)):
        for block in range(count):
            here = slice(block * BLOCK, block * BLOCK + BLOCK)
            squares_ref[to + block : to + block + 1, :] = row_squares(source[here, :])


def project(shards, w_all, own, pieces, width):
    return pl.pallas_call(
        project_kernel,
        out_shape=(
            jax.ShapeDtypeStruct((WINDOW, width), jnp.float32),
            jax.ShapeDtypeStruct((ROWS, width), jnp.float32),
            jax.ShapeDtypeStruct((WINDOW, width), jnp.bfloat16),
            jax.ShapeDtypeStruct((N_BLOCKS + Q_BLOCKS, BLOCK), jnp.float32),
        ),
        in_specs=[SMEM] + [HBM] * (2 + len(pieces)),
        out_specs=(VMEM,) * 4,
        scratch_shapes=[
            pltpu.VMEM((WINDOW, D), jnp.bfloat16),
            pltpu.VMEM((3, D, width), jnp.bfloat16),
            pltpu.SemaphoreType.DMA((14,)),
        ],
        compiler_params=pltpu.CompilerParams(vmem_limit_bytes=40 << 20),
        name="project",
    )(shards, w_all, own, *pieces)


def attend_kernel(
    lo_ref, hi_ref, q_ref, k_ref, v_ref, squares_ref, q_gain_ref, k_gain_ref, own_ref, near_ref,
    out_ref, q_hat, k_hat, s_ref,
):
    total = squares_ref[0]
    for device in range(1, N_HEAD):
        total = total + squares_ref[device]
    factors = lax.rsqrt(total / (HEADS * HEAD_DIM) + EPS)
    heads_here = q_ref.shape[1] // HEAD_DIM

    def unit(source, target, gain, block, row):
        factor = jnp.transpose(jnp.broadcast_to(factors[row : row + 1], (128, BLOCK)))
        rows = slice(block * BLOCK, block * BLOCK + BLOCK)
        for head in range(heads_here):
            cols = slice(head * HEAD_DIM, head * HEAD_DIM + HEAD_DIM)
            target[rows, cols] = (source[rows, cols] * factor * gain[:, cols]).astype(jnp.bfloat16)

    for block in range(N_BLOCKS):
        unit(k_ref, k_hat, k_gain_ref, block, block)
    for block in range(Q_BLOCKS):
        unit(q_ref, q_hat, q_gain_ref, block, N_BLOCKS + block)

    scale = 1.0 / math.sqrt(HEAD_DIM)
    heads = range(heads_here)
    cols = [slice(head * HEAD_DIM, head * HEAD_DIM + HEAD_DIM) for head in heads]
    for block in range(Q_BLOCKS):
        first, last = lo_ref[block], hi_ref[block]
        rows = slice(block * BLOCK, block * BLOCK + BLOCK)
        own = own_ref[rows, :]

        def scores(c, tops):
            allowed = own == near_ref[c]
            new = []
            for head in heads:
                s = lax.dot_general(
                    q_hat[rows, cols[head]],
                    k_hat[pl.ds(c * CHUNK, CHUNK), cols[head]],
                    (((1,), (1,)), ((), ())),
                    preferred_element_type=jnp.float32,
                )
                s = jnp.where(allowed, s * scale, NEG)
                s_ref[head, c] = s
                top = tops[head]
                for part in range(CHUNK // 128):
                    top = jnp.maximum(top, s[:, part * 128 : part * 128 + 128])
                new.append(top)
            return tuple(new)

        lowest = jnp.full((BLOCK, 128), NEG, jnp.float32)
        tops = lax.fori_loop(first, last, scores, (lowest,) * heads_here)
        highest = [jnp.max(top, axis=1, keepdims=True) for top in tops]

        def expos(c, totals):
            new = []
            for head in heads:
                e = jnp.exp(s_ref[head, c] - highest[head])
                s_ref[head, c] = e
                total = totals[head]
                for part in range(CHUNK // 128):
                    total = total + e[:, part * 128 : part * 128 + 128]
                new.append(total)
            return tuple(new)

        zeros = jnp.zeros((BLOCK, 128), jnp.float32)
        totals = lax.fori_loop(first, last, expos, (zeros,) * heads_here)
        inverse = [1.0 / jnp.sum(total, axis=1, keepdims=True) for total in totals]

        def mix(c, accs):
            new = []
            for head in heads:
                w = (s_ref[head, c] * inverse[head]).astype(jnp.bfloat16)
                v = v_ref[pl.ds(c * CHUNK, CHUNK), cols[head]]
                new.append(accs[head] + jnp.dot(w, v, preferred_element_type=jnp.float32))
            return tuple(new)

        accs = lax.fori_loop(first, last, mix, (zeros,) * heads_here)
        for head in heads:
            out_ref[rows, cols[head]] = accs[head].astype(jnp.bfloat16)


def attend(lo, hi, q, k, v, squares, q_gain, k_gain, own, near):
    width = q.shape[1]
    return pl.pallas_call(
        attend_kernel,
        out_shape=jax.ShapeDtypeStruct((ROWS, width), jnp.bfloat16),
        in_specs=[SMEM, SMEM] + [VMEM] * 8,
        out_specs=VMEM,
        scratch_shapes=[
            pltpu.VMEM((ROWS, width), jnp.bfloat16),
            pltpu.VMEM((WINDOW, width), jnp.bfloat16),
            pltpu.VMEM((width // HEAD_DIM, WINDOW // CHUNK, BLOCK, CHUNK), jnp.float32),
        ],
        compiler_params=pltpu.CompilerParams(vmem_limit_bytes=LIMIT << 20),
        name="attend",
    )(lo, hi, q, k, v, squares, q_gain, k_gain, own, near)


def on_device(tokens, ln_gain, w_query, w_key, w_value, q_gain, k_gain, seg_ids):
    width = w_query.shape[1]
    w_all = jnp.concatenate([w_query, w_key, w_value], axis=1)
    w_all = copies_to_all(w_all, "seq", NY, OVER_Y).reshape(NY * SHARD_ROWS, 3 * width)
    normed = norm(tokens, ln_gain[None, :])
    w_all, normed, seg_ids = lax.optimization_barrier((w_all, normed, seg_ids))
    w_all = lax.all_gather(w_all, "seq", axis=0, axis_index_groups=OVER_Z, tiled=True)

    me = lax.axis_index("head")
    near_rows = lax.dynamic_slice_in_dim(normed, me * NEAR_PART, NEAR_PART, 0)
    last_rows = lax.dynamic_slice_in_dim(normed, ROWS - FAR + me * FAR_PART, FAR_PART, 0)
    first_rows = lax.dynamic_slice_in_dim(normed, me * FAR_PART, FAR_PART, 0)
    left = jnp.concatenate([shifted(last_rows, 2), shifted(near_rows, 1)], axis=0)
    right = jnp.concatenate([shifted(near_rows, -1), shifted(first_rows, -2)], axis=0)
    own = jnp.concatenate([left, right], axis=0)
    before = along_x(own, 1)
    after = along_x(own, -1)
    across_left = along_x(before[:HALF], 1)
    across_right = along_x(after[HALF:], -1)
    pieces = (own, before, after, across_left, across_right)
    pieces += tuple(other_core(piece) for piece in pieces)
    x, core = me // 2, me % 2
    shards = jnp.stack(
        [2 * ((x + by) % NX) + c for c in (core, 1 - core) for by in (0, NX - 1, 1, 2)]
    ).astype(jnp.int32)

    marks = seg_ids + 1
    sent = marks.astype(jnp.bfloat16)
    near = jnp.concatenate(
        [
            shifted(sent[ROWS - FAR :], 2).astype(jnp.int32),
            shifted(sent, 1).astype(jnp.int32),
            marks,
            shifted(sent, -1).astype(jnp.int32),
            shifted(sent[:FAR], -2).astype(jnp.int32),
        ]
    )
    blocks = marks.reshape(-1, BLOCK)
    low, high = blocks[:, :1], blocks[:, -1:]
    hit = (near[None, :] >= low) & (near[None, :] <= high)
    spots = jnp.arange(WINDOW, dtype=jnp.int32)[None, :]
    lo = jnp.min(jnp.where(hit, spots, WINDOW), axis=1) // CHUNK
    hi = jnp.max(jnp.where(hit, spots, -1), axis=1) // CHUNK + 1

    w_all = pltpu.with_memory_space_constraint(w_all, pltpu.HBM)
    keys, queries, values, squares = project(shards, w_all, normed, pieces, width)
    squares = copies_to_all(squares, "head", N_HEAD)
    return attend(
        lo,
        hi,
        queries,
        keys,
        values,
        squares,
        q_gain[None, :],
        k_gain[None, :],
        marks[:, None],
        near.reshape(WINDOW // CHUNK, 1, CHUNK),
    )


def solution(mesh):
    return jax.shard_map(
        on_device,
        mesh=mesh,
        in_specs=(
            P("seq", None),
            P(),
            P("seq", "head"),
            P("seq", "head"),
            P("seq", "head"),
            P("head"),
            P("head"),
            P("seq"),
        ),
        out_specs=P("seq", "head"),
        check_vma=False,
    )
```

time: 773 us -> 222 us (0.29)
  Pallas kernels: 606 us -> 44.1 us
  waiting for transfers between devices: 54.9 us -> 64 us
    pallas_call x3 -> x1, Pallas kernels: 575 us -> 21.6 us  [project(): pl.pallas_call(project_kernel, out_shape=(jax.ShapeDtypeStruct((WINDOW, w...]
    ppermute x8, waiting for transfers between devices: 12.7 us -> 36.7 us  [shifted(): return lax.ppermute(value, 'seq', pairs)]
    ppermute x4, waiting for transfers between devices: 38.4 us -> 20.2 us  [along_x(): return lax.ppermute(value, 'head', pairs)]
    pallas_call x1, Pallas kernels: 19.6 us -> 11.2 us  [attend(): pl.pallas_call(attend_kernel, out_shape=jax.ShapeDtypeStruct((ROWS, width...]
    unnamed x34 -> x33, local copies, waits for them, and re-layouts: 14.2 us -> 18.5 us
  transfers between devices with their start and end apart: 20 -> 20, of which waited for: 7 -> 9; matrix products, arithmetic and copies ran while one was open for 1% -> 4% of each run, Pallas kernels for 73% -> 5%
where the time goes in v3:
time: 222 us; the launch traced here: 220 us
  starting transfers between devices  69.8 us (31%)
  waiting for transfers between devices  64 us (29%)
  Pallas kernels  44.1 us (20%)
  local copies, waits for them, and re-layouts  27.4 us (12%)
  between operations  13.9 us (6%)
    ppermute x8, waiting for transfers between devices, shifted(): return lax.ppermute(value, 'seq', pairs)  36.7 us
    ppermute x8, starting transfers between devices, shifted(): return lax.ppermute(value, 'seq', pairs)  32.6 us
    pallas_call x1, Pallas kernels, project(): pl.pallas_call(project_kernel, out_shape=(jax.ShapeDtypeStruct((WINDOW, w...  21.6 us
    ppermute x4, waiting for transfers between devices, along_x(): return lax.ppermute(value, 'head', pairs)  20.2 us
    unnamed x33, local copies, waits for them, and re-layouts  18.5 us
    ppermute x4, starting transfers between devices, along_x(): return lax.ppermute(value, 'head', pairs)  14.1 us
    all_to_all x2, starting transfers between devices, copies_to_all(): return lax.all_to_all(stacked, axis, 0, 0, axis_index_groups=groups)  12.4 us
    pallas_call x1, Pallas kernels, norm(): pl.pallas_call(norm_kernel, out_shape=jax.ShapeDtypeStruct((ROWS, D), jnp...  11.4 us
  transfers between devices with their start and end apart: 20, of which 9 were waited for; matrix products, arithmetic and copies ran while one was open for 4% of the time, Pallas kernels for 5%

profile of v3, /device:TPU:24, one launch (start us, length us, event | category | flops | bytes accessed | tf_op | source)
XLA Modules:
  0.0 220.4 jit_solution(7960112059438713006)
XLA Ops:
  6.5 0.8 pad_maximum_fusion
  7.3 0.8 broadcast_in_dim.47
  8.1 9.0 %all-to-all-start = ((bf16[4,50,768]{2,1,0:T(8,128)(2,1)}), bf16[4,50,768]{2,1,0:T(8,128)(2,1)S(1)}, u32[]{:S(2)}, u32[]{:S(2)}) async-start(bf16[4,50,768]{2,1,0:T(8,128)(2,1)} %broadcast_in_dim.47), calls=%async_computation | async-start | bytes 688128 | tf_op jit(solution)/shard_map/all_to_all | solution.py:44
  17.1 0.7 broadcast_in_dim.48.gain_ref
  17.8 0.0 copy-start.1
  17.8 2.4 %copy-done.1 = bf16[768,3200]{1,0:T(8,128)(2,1)S(1)} copy-done((bf16[768,3200]{1,0:T(8,128)(2,1)S(1)}, bf16[768,3200]{1,0:T(8,128)(2,1)}, u32[]{:S(2)}) %copy-start.1) | copy-done | bytes 4915224
  20.2 11.4 %norm.1.own_ref = bf16[768,3200]{1,0:T(8,128)(2,1)S(1)} custom-call(bf16[768,3200]{1,0:T(8,128)(2,1)S(1)} %copy-done.1, f32[1,3200]{1,0:T(1,128)S(1)} %broadcast_in_dim.48.gain_ref), custom_call_target="tpu_custom_call" | custom-call | flops 1 | bytes 1 | tf_op jit(solution)/shard_map/norm/pallas_call | solution.py:75
  31.6 2.2 copy-done
  33.8 0.8 reshape.12
  34.7 0.0 all-gather.2.cloned.1.call-update
  34.7 1.1 constant_dynamic-slice_fusion
  35.8 1.9 collective-permute-start.4
  37.7 1.1 constant_dynamic-slice_fusion.1
  38.8 2.7 %collective-permute-start.5 = (bf16[96,3200]{1,0:T(8,128)(2,1)S(1)}, bf16[96,3200]{1,0:T(8,128)(2,1)S(1)}, u32[]{:S(2)}, u32[]{:S(2)}) collective-permute-start(bf16[96,3200]{1,0:T(8,128)(2,1)S(1)} %constant_dynamic-slice_fusion.1), channel_id=1, source_target_pairs={{0,1},{1,2},{2,3},{3,4},{4,5},{5,6},{6,7},{7,8},{8,9},{9,10},{10,1... | collective-permute-start | bytes 1843208 | tf_op jit(solution)/shard_map/ppermute | solution.py:49
  41.6 6.5 %collective-permute-start.6 = (bf16[96,3200]{1,0:T(8,128)(2,1)S(1)}, bf16[96,3200]{1,0:T(8,128)(2,1)S(1)}, u32[]{:S(2)}, u32[]{:S(2)}) collective-permute-start(bf16[96,3200]{1,0:T(8,128)(2,1)S(1)} %constant_dynamic-slice_fusion.1), channel_id=1, source_target_pairs={{1,0},{2,1},{3,2},{4,3},{5,4},{6,5},{7,6},{8,7},{9,8},{10,9},{11,1... | collective-permute-start | bytes 1843208 | tf_op jit(solution)/shard_map/ppermute | solution.py:49
  48.1 0.0 copy-start.14
  48.1 4.8 %collective-permute-start.7 = (bf16[32,3200]{1,0:T(8,128)(2,1)S(1)}, bf16[32,3200]{1,0:T(8,128)(2,1)S(1)}, u32[]{:S(2)}, u32[]{:S(2)}) collective-permute-start(bf16[32,3200]{1,0:T(8,128)(2,1)S(1)} %get-tuple-element.23), channel_id=1, source_target_pairs={{2,0},{3,1},{4,2},{5,3},{6,4},{7,5},{8,6},{9,7},{10,8},{11,9},{12,... | collective-permute-start | bytes 614408 | tf_op jit(solution)/shard_map/ppermute | solution.py:49
  52.9 0.1 collective-permute-done.4
  53.1 0.7 constant_dynamic-update-slice_fusion.4
  53.8 21.2 %collective-permute-done.5 = bf16[96,3200]{1,0:T(8,128)(2,1)S(1)} collective-permute-done((bf16[96,3200]{1,0:T(8,128)(2,1)S(1)}, bf16[96,3200]{1,0:T(8,128)(2,1)S(1)}, u32[]{:S(2)}, u32[]{:S(2)}) %collective-permute-start.5) | collective-permute-done | bytes 614432 | tf_op jit(solution)/shard_map/ppermute | solution.py:49
  75.0 0.9 constant_dynamic-update-slice_fusion.3
  75.9 0.9 collective-permute-done.6
  76.8 0.9 constant_dynamic-update-slice_fusion.2
  77.7 7.3 %collective-permute-done.7 = bf16[32,3200]{1,0:T(8,128)(2,1)S(1)} collective-permute-done((bf16[32,3200]{1,0:T(8,128)(2,1)S(1)}, bf16[32,3200]{1,0:T(8,128)(2,1)S(1)}, u32[]{:S(2)}, u32[]{:S(2)}) %collective-permute-start.7) | collective-permute-done | bytes 204832 | tf_op jit(solution)/shard_map/ppermute | solution.py:49
  85.0 0.7 constant_dynamic-update-slice_fusion.1.p0
  85.7 3.4 %collective-permute-start.8 = (bf16[256,3200]{1,0:T(8,128)(2,1)}, bf16[256,3200]{1,0:T(8,128)(2,1)S(1)}, u32[]{:S(2)}, u32[]{:S(2)}) collective-permute-start(bf16[256,3200]{1,0:T(8,128)(2,1)} %constant_dynamic-update-slice_fusion.1.p0), channel_id=1, source_target_pairs={{0,128},{64,192},{128,256},{192,320},{256,384},{320,448},{384,0},{... | collective-permute-start | bytes 4915208 | tf_op jit(solution)/shard_map/ppermute | solution.py:54
  89.1 3.6 %collective-permute-start.9 = (bf16[256,3200]{1,0:T(8,128)(2,1)}, bf16[256,3200]{1,0:T(8,128)(2,1)S(1)}, u32[]{:S(2)}, u32[]{:S(2)}) collective-permute-start(bf16[256,3200]{1,0:T(8,128)(2,1)} %constant_dynamic-update-slice_fusion.1.p0), channel_id=1, source_target_pairs={{0,384},{64,448},{128,0},{192,64},{256,128},{320,192},{384,256},{4... | collective-permute-start | bytes 4915208 | tf_op jit(solution)/shard_map/ppermute | solution.py:54
  92.7 1.9 collective-permute-start.1
  94.7 6.0 %collective-permute-start.2 = (bf16[768]{0:T(1024)(128)(2,1)S(1)}, bf16[768]{0:T(1024)(128)(2,1)S(1)}, u32[]{:S(2)}, u32[]{:S(2)}) collective-permute-start(bf16[768]{0:T(1024)(128)(2,1)S(1)} %get-tuple-element.26), channel_id=1, source_target_pairs={{1,0},{2,1},{3,2},{4,3},{5,4},{6,5},{7,6},{8,7},{9,8},{10,9},{11,1... | collective-permute-start | bytes 4616 | tf_op jit(solution)/shard_map/ppermute | solution.py:49
  100.7 20.2 %collective-permute-done.8.p1 = bf16[256,3200]{1,0:T(8,128)(2,1)S(1)} collective-permute-done((bf16[256,3200]{1,0:T(8,128)(2,1)}, bf16[256,3200]{1,0:T(8,128)(2,1)S(1)}, u32[]{:S(2)}, u32[]{:S(2)}) %collective-permute-start.8) | collective-permute-done | bytes 1638432 | tf_op jit(solution)/shard_map/ppermute | solution.py:54
  120.9 1.0 slice.26
  121.9 3.0 %collective-permute-start.10 = (bf16[128,3200]{1,0:T(8,128)(2,1)}, bf16[128,3200]{1,0:T(8,128)(2,1)}, u32[]{:S(2)}, u32[]{:S(2)}) collective-permute-start(bf16[128,3200]{1,0:T(8,128)(2,1)} %slice.26), channel_id=1, source_target_pairs={{0,128},{64,192},{128,256},{192,320},{256,384},{320,448},{384,0},{... | collective-permute-start | bytes 2457608 | tf_op jit(solution)/shard_map/ppermute | solution.py:54
  125.0 0.9 slice.27
  125.9 4.0 %collective-permute-start.11 = (bf16[128,3200]{1,0:T(8,128)(2,1)}, bf16[128,3200]{1,0:T(8,128)(2,1)}, u32[]{:S(2)}, u32[]{:S(2)}) collective-permute-start(bf16[128,3200]{1,0:T(8,128)(2,1)} %slice.27), channel_id=1, source_target_pairs={{0,384},{64,448},{128,0},{192,64},{256,128},{320,192},{384,256},{4... | collective-permute-start | bytes 2457608 | tf_op jit(solution)/shard_map/ppermute | solution.py:54
  129.9 3.9 %collective-permute-start = (bf16[256]{0:T(256)(128)(2,1)S(1)}, bf16[256]{0:T(256)(128)(2,1)S(1)}, u32[]{:S(2)}, u32[]{:S(2)}) collective-permute-start(bf16[256]{0:T(256)(128)(2,1)S(1)} %get-tuple-element.28), channel_id=1, source_target_pairs={{0,2},{1,3},{2,4},{3,5},{4,6},{5,7},{6,8},{7,9},{8,10},{9,11},{10,... | collective-permute-start | bytes 1544 | tf_op jit(solution)/shard_map/ppermute | solution.py:49
  133.8 5.6 %collective-permute-done = bf16[256]{0:T(256)(128)(2,1)S(1)} collective-permute-done((bf16[256]{0:T(256)(128)(2,1)S(1)}, bf16[256]{0:T(256)(128)(2,1)S(1)}, u32[]{:S(2)}, u32[]{:S(2)}) %collective-permute-start) | collective-permute-done | bytes 544 | tf_op jit(solution)/shard_map/ppermute | solution.py:49
  139.4 4.8 %collective-permute-start.3 = (bf16[256]{0:T(256)(128)(2,1)S(1)}, bf16[256]{0:T(256)(128)(2,1)S(1)}, u32[]{:S(2)}, u32[]{:S(2)}) collective-permute-start(bf16[256]{0:T(256)(128)(2,1)S(1)} %get-tuple-element.27), channel_id=1, source_target_pairs={{2,0},{3,1},{4,2},{5,3},{6,4},{7,5},{8,6},{9,7},{10,8},{11,9},{12,... | collective-permute-start | bytes 1544 | tf_op jit(solution)/shard_map/ppermute | solution.py:49
  144.2 1.5 collective-permute-done.3
  145.7 1.9 collective-permute-start.12
  147.6 2.4 %collective-permute-start.13 = (bf16[256,3200]{1,0:T(8,128)(2,1)S(1)}, bf16[256,3200]{1,0:T(8,128)(2,1)}, u32[]{:S(2)}, u32[]{:S(2)}) collective-permute-start(bf16[256,3200]{1,0:T(8,128)(2,1)S(1)} %collective-permute-done.8.p1), channel_id=1, source_target_pairs={{0,64},{64,0},{128,192},{192,128},{256,320},{320,256},{384,448},{4... | collective-permute-start | bytes 4915208 | tf_op jit(solution)/shard_map/ppermute | solution.py:58
  150.1 1.9 collective-permute-start.14
  152.1 0.1 stack.35.shards_ref
  152.2 0.9 broadcast_in_dim.57.own_ref
  153.1 0.2 slice_reduce_fusion.1
  153.3 2.4 %collective-permute-start.15 = (bf16[128,3200]{1,0:T(8,128)(2,1)}, bf16[128,3200]{1,0:T(8,128)(2,1)S(1)}, u32[]{:S(2)}, u32[]{:S(2)}) collective-permute-start(bf16[128,3200]{1,0:T(8,128)(2,1)} %collective-permute-done.10.p3l), channel_id=1, source_target_pairs={{0,64},{64,0},{128,192},{192,128},{256,320},{320,256},{384,448},{4... | collective-permute-start | bytes 2457608 | tf_op jit(solution)/shard_map/ppermute | solution.py:58
  155.7 2.1 collective-permute-start.16
  157.9 0.0 copy-start.12
  157.9 0.2 select_reduce_fusion
  158.2 0.9 copy-done.6
  159.1 1.1 collective-permute-done.16.p7r
  160.2 0.9 copy-done.8
  161.1 1.1 copy-done.7
  162.2 1.1 copy-done.9
  163.3 21.6 %project.1 = (f32[2816,256]{1,0:T(8,128)}, f32[768,256]{1,0:T(8,128)S(1)}, bf16[2816,256]{1,0:T(8,128)(2,1)S(1)}, f32[14,256]{1,0:T(8,128)S(1)}) custom-call(s32[8]{0:T(128)S(1)} %stack.35.shards_ref, bf16[3200,768]{1,0:T(8,128)(2,1)} %all-gather.2.cloned.1.call-done.w_ref, bf16[768,3200]{1,0:T(8,128)(2,1)} %copy-done, ...), custom_call_target="tpu_custom_call" | custom-call | tf_op jit(solution)/shard_map/project/pallas_call | solution.py:169
  184.9 1.1 copy-done.4
  186.1 0.9 copy-done.10
  186.9 0.7 broadcast_in_dim.53
  187.6 3.4 %all-to-all-start.1 = ((f32[8,14,256]{2,1,0:T(8,128)}), f32[8,14,256]{2,1,0:T(8,128)S(1)}, u32[]{:S(2)}, u32[]{:S(2)}) async-start(f32[8,14,256]{2,1,0:T(8,128)} %broadcast_in_dim.53), calls=%async_computation.1 | async-start | bytes 262144 | tf_op jit(solution)/shard_map/all_to_all | solution.py:44
  191.0 6.0 %all-to-all-done.1.squares_ref = f32[8,14,256]{2,1,0:T(8,128)S(1)} async-done(((f32[8,14,256]{2,1,0:T(8,128)}), f32[8,14,256]{2,1,0:T(8,128)S(1)}, u32[]{:S(2)}, u32[]{:S(2)}) %all-to-all-start.1) | async-done | bytes 114720 | tf_op jit(solution)/shard_map/all_to_all | solution.py:44
  197.0 1.8 copy-done.2
  198.9 1.0 copy-done.3
  199.9 1.4 copy-done.5
  201.2 1.1 copy-done.11
  202.4 11.2 %attend.1 = bf16[768,256]{1,0:T(8,128)(2,1)} custom-call(s32[3]{0:T(128)S(1)} %get-tuple-element.29.lo_ref, s32[3]{0:T(128)S(1)} %get-tuple-element.30.hi_ref, f32[768,256]{1,0:T(8,128)S(1)} %copy-done.11, f32[2816,256]{1,0:T(8,128)S(1)} %copy-done.2, bf16[2816,256]{1,0:T(8,128)(2,1)S(1)} %copy-done.5, f32[8,14,256]{2,1,0:T(8,128)S(1)} %all-to-all-done.1.squares_ref, ...), custom_call_target="tpu_custom_call" | custom-call | tf_op jit(solution)/shard_map/attend/pallas_call | solution.py:271
  (38 shorter events, 0.1 us)
Async XLA Ops:
  8.1 25.8 %all-to-all-start = ((bf16[4,50,768]{2,1,0:T(8,128)(2,1)}), bf16[4,50,768]{2,1,0:T(8,128)(2,1)S(1)}, u32[]{:S(2)}, u32[]{:S(2)}) async-start(bf16[4,50,768]{2,1,0:T(8,128)(2,1)} %broadcast_in_dim.47), calls=%async_computation | async-start | bytes 688128 | tf_op jit(solution)/shard_map/all_to_all | solution.py:44
  17.1 143.9 %all-gather.2.cloned.1.call-start = ((), (), s32[]{:S(2)}) async-start(), calls=%async_computation.2 | async-start | bytes 5222400 | tf_op jit(solution)/shard_map/all_gather | solution.py:292
  17.8 2.4 %copy-start.1 = (bf16[768,3200]{1,0:T(8,128)(2,1)S(1)}, bf16[768,3200]{1,0:T(8,128)(2,1)}, u32[]{:S(2)}) copy-start(bf16[768,3200]{1,0:T(8,128)(2,1)} %x_ref.1) | copy-start | bytes 14745604
  31.6 2.2 %copy-start = (bf16[768,3200]{1,0:T(8,128)(2,1)}, bf16[768,3200]{1,0:T(8,128)(2,1)S(1)}, u32[]{:S(2)}) copy-start(bf16[768,3200]{1,0:T(8,128)(2,1)S(1)} %norm.1.own_ref) | copy-start | bytes 14745604
  35.8 17.3 %collective-permute-start.4 = (bf16[32,3200]{1,0:T(8,128)(2,1)S(1)}, bf16[32,3200]{1,0:T(8,128)(2,1)S(1)}, u32[]{:S(2)}, u32[]{:S(2)}) collective-permute-start(bf16[32,3200]{1,0:T(8,128)(2,1)S(1)} %get-tuple-element.24), channel_id=1, source_target_pairs={{0,2},{1,3},{2,4},{3,5},{4,6},{5,7},{6,8},{7,9},{8,10},{9,11},{10,... | collective-permute-start | bytes 614408 | tf_op jit(solution)/shard_map/ppermute | solution.py:49
  38.8 36.2 %collective-permute-start.5 = (bf16[96,3200]{1,0:T(8,128)(2,1)S(1)}, bf16[96,3200]{1,0:T(8,128)(2,1)S(1)}, u32[]{:S(2)}, u32[]{:S(2)}) collective-permute-start(bf16[96,3200]{1,0:T(8,128)(2,1)S(1)} %constant_dynamic-slice_fusion.1), channel_id=1, source_target_pairs={{0,1},{1,2},{2,3},{3,4},{4,5},{5,6},{6,7},{7,8},{8,9},{9,10},{10,1... | collective-permute-start | bytes 1843208 | tf_op jit(solution)/shard_map/ppermute | solution.py:49
  41.6 35.2 %collective-permute-start.6 = (bf16[96,3200]{1,0:T(8,128)(2,1)S(1)}, bf16[96,3200]{1,0:T(8,128)(2,1)S(1)}, u32[]{:S(2)}, u32[]{:S(2)}) collective-permute-start(bf16[96,3200]{1,0:T(8,128)(2,1)S(1)} %constant_dynamic-slice_fusion.1), channel_id=1, source_target_pairs={{1,0},{2,1},{3,2},{4,3},{5,4},{6,5},{7,6},{8,7},{9,8},{10,9},{11,1... | collective-permute-start | bytes 1843208 | tf_op jit(solution)/shard_map/ppermute | solution.py:49
  48.1 44.6 %copy-start.14 = (s32[768]{0:T(1024)S(1)}, s32[768]{0:T(1024)}, u32[]{:S(2)}) copy-start(s32[768]{0:T(1024)} %param.15) | copy-start | bytes 9220
  48.1 36.8 %collective-permute-start.7 = (bf16[32,3200]{1,0:T(8,128)(2,1)S(1)}, bf16[32,3200]{1,0:T(8,128)(2,1)S(1)}, u32[]{:S(2)}, u32[]{:S(2)}) collective-permute-start(bf16[32,3200]{1,0:T(8,128)(2,1)S(1)} %get-tuple-element.23), channel_id=1, source_target_pairs={{2,0},{3,1},{4,2},{5,3},{6,4},{7,5},{8,6},{9,7},{10,8},{11,9},{12,... | collective-permute-start | bytes 614408 | tf_op jit(solution)/shard_map/ppermute | solution.py:49
  85.7 35.3 %collective-permute-start.8 = (bf16[256,3200]{1,0:T(8,128)(2,1)}, bf16[256,3200]{1,0:T(8,128)(2,1)S(1)}, u32[]{:S(2)}, u32[]{:S(2)}) collective-permute-start(bf16[256,3200]{1,0:T(8,128)(2,1)} %constant_dynamic-update-slice_fusion.1.p0), channel_id=1, source_target_pairs={{0,128},{64,192},{128,256},{192,320},{256,384},{320,448},{384,0},{... | collective-permute-start | bytes 4915208 | tf_op jit(solution)/shard_map/ppermute | solution.py:54
  89.1 35.9 %collective-permute-start.9 = (bf16[256,3200]{1,0:T(8,128)(2,1)}, bf16[256,3200]{1,0:T(8,128)(2,1)S(1)}, u32[]{:S(2)}, u32[]{:S(2)}) collective-permute-start(bf16[256,3200]{1,0:T(8,128)(2,1)} %constant_dynamic-update-slice_fusion.1.p0), channel_id=1, source_target_pairs={{0,384},{64,448},{128,0},{192,64},{256,128},{320,192},{384,256},{4... | collective-permute-start | bytes 4915208 | tf_op jit(solution)/shard_map/ppermute | solution.py:54
  92.7 54.9 %collective-permute-start.1 = (bf16[768]{0:T(1024)(128)(2,1)S(1)}, bf16[768]{0:T(1024)(128)(2,1)S(1)}, u32[]{:S(2)}, u32[]{:S(2)}) collective-permute-start(bf16[768]{0:T(1024)(128)(2,1)S(1)} %get-tuple-element.26), channel_id=1, source_target_pairs={{0,1},{1,2},{2,3},{3,4},{4,5},{5,6},{6,7},{7,8},{8,9},{9,10},{10,1... | collective-permute-start | bytes 4616 | tf_op jit(solution)/shard_map/ppermute | solution.py:49
  94.7 55.4 %collective-permute-start.2 = (bf16[768]{0:T(1024)(128)(2,1)S(1)}, bf16[768]{0:T(1024)(128)(2,1)S(1)}, u32[]{:S(2)}, u32[]{:S(2)}) collective-permute-start(bf16[768]{0:T(1024)(128)(2,1)S(1)} %get-tuple-element.26), channel_id=1, source_target_pairs={{1,0},{2,1},{3,2},{4,3},{5,4},{6,5},{7,6},{8,7},{9,8},{10,9},{11,1... | collective-permute-start | bytes 4616 | tf_op jit(solution)/shard_map/ppermute | solution.py:49
  121.9 31.4 %collective-permute-start.10 = (bf16[128,3200]{1,0:T(8,128)(2,1)}, bf16[128,3200]{1,0:T(8,128)(2,1)}, u32[]{:S(2)}, u32[]{:S(2)}) collective-permute-start(bf16[128,3200]{1,0:T(8,128)(2,1)} %slice.26), channel_id=1, source_target_pairs={{0,128},{64,192},{128,256},{192,320},{256,384},{320,448},{384,0},{... | collective-permute-start | bytes 2457608 | tf_op jit(solution)/shard_map/ppermute | solution.py:54
  125.9 29.8 %collective-permute-start.11 = (bf16[128,3200]{1,0:T(8,128)(2,1)}, bf16[128,3200]{1,0:T(8,128)(2,1)}, u32[]{:S(2)}, u32[]{:S(2)}) collective-permute-start(bf16[128,3200]{1,0:T(8,128)(2,1)} %slice.27), channel_id=1, source_target_pairs={{0,384},{64,448},{128,0},{192,64},{256,128},{320,192},{384,256},{4... | collective-permute-start | bytes 2457608 | tf_op jit(solution)/shard_map/ppermute | solution.py:54
  129.9 9.5 %collective-permute-start = (bf16[256]{0:T(256)(128)(2,1)S(1)}, bf16[256]{0:T(256)(128)(2,1)S(1)}, u32[]{:S(2)}, u32[]{:S(2)}) collective-permute-start(bf16[256]{0:T(256)(128)(2,1)S(1)} %get-tuple-element.28), channel_id=1, source_target_pairs={{0,2},{1,3},{2,4},{3,5},{4,6},{5,7},{6,8},{7,9},{8,10},{9,11},{10,... | collective-permute-start | bytes 1544 | tf_op jit(solution)/shard_map/ppermute | solution.py:49
  139.4 6.3 %collective-permute-start.3 = (bf16[256]{0:T(256)(128)(2,1)S(1)}, bf16[256]{0:T(256)(128)(2,1)S(1)}, u32[]{:S(2)}, u32[]{:S(2)}) collective-permute-start(bf16[256]{0:T(256)(128)(2,1)S(1)} %get-tuple-element.27), channel_id=1, source_target_pairs={{2,0},{3,1},{4,2},{5,3},{6,4},{7,5},{8,6},{9,7},{10,8},{11,9},{12,... | collective-permute-start | bytes 1544 | tf_op jit(solution)/shard_map/ppermute | solution.py:49
  145.7 12.5 %collective-permute-start.12 = (bf16[256,3200]{1,0:T(8,128)(2,1)}, bf16[256,3200]{1,0:T(8,128)(2,1)}, u32[]{:S(2)}, u32[]{:S(2)}) collective-permute-start(bf16[256,3200]{1,0:T(8,128)(2,1)} %constant_dynamic-update-slice_fusion.1.p0), channel_id=1, source_target_pairs={{0,64},{64,0},{128,192},{192,128},{256,320},{320,256},{384,448},{4... | collective-permute-start | bytes 4915208 | tf_op jit(solution)/shard_map/ppermute | solution.py:58
  147.6 13.4 %collective-permute-start.13 = (bf16[256,3200]{1,0:T(8,128)(2,1)S(1)}, bf16[256,3200]{1,0:T(8,128)(2,1)}, u32[]{:S(2)}, u32[]{:S(2)}) collective-permute-start(bf16[256,3200]{1,0:T(8,128)(2,1)S(1)} %collective-permute-done.8.p1), channel_id=1, source_target_pairs={{0,64},{64,0},{128,192},{192,128},{256,320},{320,256},{384,448},{4... | collective-permute-start | bytes 4915208 | tf_op jit(solution)/shard_map/ppermute | solution.py:58
  150.1 11.0 %collective-permute-start.14 = (bf16[256,3200]{1,0:T(8,128)(2,1)S(1)}, bf16[256,3200]{1,0:T(8,128)(2,1)}, u32[]{:S(2)}, u32[]{:S(2)}) collective-permute-start(bf16[256,3200]{1,0:T(8,128)(2,1)S(1)} %collective-permute-done.9.p2), channel_id=1, source_target_pairs={{0,64},{64,0},{128,192},{192,128},{256,320},{320,256},{384,448},{4... | collective-permute-start | bytes 4915208 | tf_op jit(solution)/shard_map/ppermute | solution.py:58
  153.3 4.9 %collective-permute-start.15 = (bf16[128,3200]{1,0:T(8,128)(2,1)}, bf16[128,3200]{1,0:T(8,128)(2,1)S(1)}, u32[]{:S(2)}, u32[]{:S(2)}) collective-permute-start(bf16[128,3200]{1,0:T(8,128)(2,1)} %collective-permute-done.10.p3l), channel_id=1, source_target_pairs={{0,64},{64,0},{128,192},{192,128},{256,320},{320,256},{384,448},{4... | collective-permute-start | bytes 2457608 | tf_op jit(solution)/shard_map/ppermute | solution.py:58
  155.7 4.4 %collective-permute-start.16 = (bf16[128,3200]{1,0:T(8,128)(2,1)}, bf16[128,3200]{1,0:T(8,128)(2,1)S(1)}, u32[]{:S(2)}, u32[]{:S(2)}) collective-permute-start(bf16[128,3200]{1,0:T(8,128)(2,1)} %collective-permute-done.11.p3r), channel_id=1, source_target_pairs={{0,64},{64,0},{128,192},{192,128},{256,320},{320,256},{384,448},{4... | collective-permute-start | bytes 2457608 | tf_op jit(solution)/shard_map/ppermute | solution.py:58
  157.9 39.2 %copy-start.12 = (f32[256]{0:T(256)S(1)}, f32[256]{0:T(256)}, u32[]{:S(2)}) copy-start(f32[256]{0:T(256)} %param.13) | copy-start | bytes 3076
  157.9 39.1 %copy-start.13 = (f32[256]{0:T(256)S(1)}, f32[256]{0:T(256)}, u32[]{:S(2)}) copy-start(f32[256]{0:T(256)} %param.14) | copy-start | bytes 3076
  158.2 0.9 copy-start.6
  160.2 0.9 copy-start.8
  161.1 1.1 copy-start.7
  162.2 1.1 copy-start.9
  184.9 1.1 copy-start.4
  186.1 0.9 copy-start.10
  187.6 9.4 %all-to-all-start.1 = ((f32[8,14,256]{2,1,0:T(8,128)}), f32[8,14,256]{2,1,0:T(8,128)S(1)}, u32[]{:S(2)}, u32[]{:S(2)}) async-start(f32[8,14,256]{2,1,0:T(8,128)} %broadcast_in_dim.53), calls=%async_computation.1 | async-start | bytes 262144 | tf_op jit(solution)/shard_map/all_to_all | solution.py:44
  197.0 1.8 copy-start.2
  198.9 1.0 copy-start.3
  199.9 1.4 copy-start.5
  201.2 1.1 copy-start.11
Sparse Core Ops, SparseCore 0:
  34.8 93.4 all-gather.1

commit v4 on v1

v4 whole, which is shorter than its diff:
```python
import math

import jax
import jax.numpy as jnp
from jax import lax
from jax.experimental import pallas as pl
from jax.experimental.pallas import tpu as pltpu
from jax.sharding import PartitionSpec as P

D = 3200
HEADS = 16
HEAD_DIM = 128
MOST = 1025
EPS = 1e-06
NY = 4
NZ = 16
N_SEQ = NY * NZ
N_HEAD = 8
ROWS = 768
FAR = 256
WINDOW = 2 * FAR + 3 * ROWS
OWN = FAR + ROWS
BLOCK = 256
N_BLOCKS = WINDOW // BLOCK
Q_BLOCKS = ROWS // BLOCK
CHUNK = 256
NEG = -1e30
BEYOND = 1e6
SHARD_ROWS = D // N_SEQ
MARK_ROWS = 8

OVER_Y = [[y * NZ + z for y in range(NY)] for z in range(NZ)]
OVER_Z = [[y * NZ + z for z in range(NZ)] for y in range(NY)]
VMEM = pl.BlockSpec(memory_space=pltpu.VMEM)
SMEM = pl.BlockSpec(memory_space=pltpu.SMEM)
HBM = pl.BlockSpec(memory_space=pltpu.HBM)


def copies_to_all(value, axis, size, groups=None):
    stacked = jnp.broadcast_to(value[None], (size,) + value.shape)
    return lax.all_to_all(stacked, axis, 0, 0, axis_index_groups=groups)


def shifted(value, by):
    pairs = [(i, i + by) for i in range(N_SEQ) if 0 <= i + by < N_SEQ]
    return lax.ppermute(value, "seq", pairs)


def norm_kernel(x_ref, gain_ref, out_ref, moved_ref):
    x = x_ref[...].astype(jnp.float32)
    mean = jnp.sum(x * x, axis=1, keepdims=True) * (1.0 / D)
    out_ref[...] = (x * lax.rsqrt(mean + EPS) * gain_ref[...]).astype(jnp.bfloat16)
    for z in range(NZ):
        for y in range(NY):
            source = (y * NZ + z) * SHARD_ROWS
            target = (z * NY + y) * SHARD_ROWS
            moved_ref[:, target : target + SHARD_ROWS] = out_ref[:, source : source + SHARD_ROWS]


def norm(tokens, gain):
    rows = 128
    block = pl.BlockSpec((rows, D), lambda i: (i, 0))
    shape = jax.ShapeDtypeStruct((ROWS, D), jnp.bfloat16)
    return pl.pallas_call(
        norm_kernel,
        out_shape=(shape, shape),
        grid=(ROWS // rows,),
        in_specs=[block, pl.BlockSpec((1, D), lambda i: (0, 0))],
        out_specs=(block, block),
        compiler_params=pltpu.CompilerParams(vmem_limit_bytes=10 << 20),
        name="norm",
    )(tokens, gain)


def row_squares(values):
    sums = jnp.sum(values * values, axis=1, keepdims=True)
    return jnp.transpose(jnp.broadcast_to(sums, (BLOCK, 128)))[:1]


def keys_kernel(x_ref, w_ref, k_ref, squares_ref):
    for block in range(Q_BLOCKS):
        rows = slice(block * BLOCK, block * BLOCK + BLOCK)
        k = jnp.dot(x_ref[rows, :], w_ref[...], preferred_element_type=jnp.float32)
        k_ref[rows, :] = k
        squares_ref[block : block + 1, :] = row_squares(k)


def project_keys(x, w):
    width = w.shape[1]
    return pl.pallas_call(
        keys_kernel,
        out_shape=(
            jax.ShapeDtypeStruct((ROWS, width), jnp.float32),
            jax.ShapeDtypeStruct((Q_BLOCKS, BLOCK), jnp.float32),
        ),
        in_specs=[VMEM, VMEM],
        out_specs=(VMEM, VMEM),
        compiler_params=pltpu.CompilerParams(vmem_limit_bytes=12 << 20),
        name="keys",
    )(x, w)


def values_kernel(x_ref, w_ref, q_ref, squares_ref, v_ref, last_ref, first_ref, w, sem):
    width = v_ref.shape[1]
    loads = [
        pltpu.make_async_copy(w_ref.at[:, pl.ds(n * width, width)], w.at[n], sem.at[n])
        for n in range(2)
    ]
    loads[1].start()
    loads[0].start()
    loads[1].wait()
    for block in range(Q_BLOCKS):
        rows = slice(block * BLOCK, block * BLOCK + BLOCK)
        q = jnp.dot(x_ref[rows, :], w[1], preferred_element_type=jnp.float32)
        q_ref[rows, :] = q
        squares_ref[block : block + 1, :] = row_squares(q)
    loads[0].wait()
    for block in range(Q_BLOCKS):
        rows = slice(block * BLOCK, block * BLOCK + BLOCK)
        v_ref[rows, :] = jnp.dot(
            x_ref[rows, :], w[0], preferred_element_type=jnp.float32
        ).astype(jnp.bfloat16)
    last_ref[...] = v_ref[ROWS - FAR :, :]
    first_ref[...] = v_ref[:FAR, :]


def project_values(x, w):
    width = w.shape[1] // 2
    far = jax.ShapeDtypeStruct((FAR, width), jnp.bfloat16)
    return pl.pallas_call(
        values_kernel,
        out_shape=(
            jax.ShapeDtypeStruct((ROWS, width), jnp.float32),
            jax.ShapeDtypeStruct((Q_BLOCKS, BLOCK), jnp.float32),
            jax.ShapeDtypeStruct((ROWS, width), jnp.bfloat16),
            far,
            far,
        ),
        in_specs=[VMEM, HBM],
        out_specs=(VMEM,) * 5,
        scratch_shapes=[
            pltpu.VMEM((2, D, width), jnp.bfloat16),
            pltpu.SemaphoreType.DMA((2,)),
        ],
        compiler_params=pltpu.CompilerParams(vmem_limit_bytes=14 << 20),
        name="values",
    )(x, w)


def head_factors(squares_ref):
    total = squares_ref[0]
    for device in range(1, N_HEAD):
        total = total + squares_ref[device]
    return lax.rsqrt(total / (HEADS * HEAD_DIM) + EPS)


def unit(source, target, gain_ref, factors):
    for block in range(Q_BLOCKS):
        factor = jnp.transpose(jnp.broadcast_to(factors[block : block + 1], (128, BLOCK)))
        rows = slice(block * BLOCK, block * BLOCK + BLOCK)
        for start in range(0, source.shape[1], HEAD_DIM):
            cols = slice(start, start + HEAD_DIM)
            target[rows, cols] = (source[rows, cols] * factor * gain_ref[:, cols]).astype(
                jnp.bfloat16
            )


def unit_keys_kernel(k_ref, squares_ref, gain_ref, marks_ref, out_ref, last_ref, first_ref):
    unit(k_ref, out_ref, gain_ref, head_factors(squares_ref))
    out_ref[ROWS:, :] = marks_ref[...]
    last_ref[:FAR, :] = out_ref[ROWS - FAR : ROWS, :]
    first_ref[:FAR, :] = out_ref[:FAR, :]
    spare = jnp.zeros((MARK_ROWS - 1, out_ref.shape[1]), jnp.float32)
    marks = marks_ref[...].astype(jnp.float32)
    last_ref[FAR:, :] = jnp.concatenate([marks[Q_BLOCKS - 1 : Q_BLOCKS], spare]).astype(jnp.bfloat16)
    first_ref[FAR:, :] = jnp.concatenate([marks[:1], spare]).astype(jnp.bfloat16)


def unit_keys(k, squares, gain, marks):
    width = k.shape[1]
    far = jax.ShapeDtypeStruct((FAR + MARK_ROWS, width), jnp.bfloat16)
    return pl.pallas_call(
        unit_keys_kernel,
        out_shape=(jax.ShapeDtypeStruct((ROWS + MARK_ROWS, width), jnp.bfloat16), far, far),
        in_specs=[VMEM] * 4,
        out_specs=(VMEM,) * 3,
        compiler_params=pltpu.CompilerParams(vmem_limit_bytes=8 << 20),
        name="unit_keys",
    )(k, squares, gain, marks)


def attend_kernel(
    q_ref, squares_ref, q_gain_ref, own_ref, ka, kb, kc, kd, ke, va, vb, vc, vd, ve,
    out_ref, q_hat, k_win, v_win, near_ref, s_ref,
):
    start = 0
    for k_part, v_part in ((ka, va), (kb, vb), (kc, vc), (kd, vd), (ke, ve)):
        rows = v_part.shape[0]
        k_win[start : start + rows, :] = k_part[:rows, :]
        v_win[start : start + rows, :] = v_part[...]
        marks = k_part[rows:, :].astype(jnp.float32)
        if start > OWN:
            marks = jnp.where(marks == 0, BEYOND, marks)
        for n in range(rows // CHUNK):
            near_ref[start // CHUNK + n] = marks[n : n + 1]
        start += rows
    unit(q_ref, q_hat, q_gain_ref, head_factors(squares_ref))

    scale = 1.0 / math.sqrt(HEAD_DIM)
    heads = range(q_ref.shape[1] // HEAD_DIM)
    cols = [slice(head * HEAD_DIM, head * HEAD_DIM + HEAD_DIM) for head in heads]
    for block in range(Q_BLOCKS):
        rows = slice(block * BLOCK, block * BLOCK + BLOCK)
        own = own_ref[rows, :]
        low, high = jnp.min(own), jnp.max(own)
        near = near_ref[...]
        below = jnp.sum((near < low).astype(jnp.float32)).astype(jnp.int32)
        within = jnp.sum((near <= high).astype(jnp.float32)).astype(jnp.int32)
        first, last = below // CHUNK, (within + CHUNK - 1) // CHUNK

        def scores(c, tops):
            allowed = own == near_ref[c]
            new = []
            for head in heads:
                s = lax.dot_general(
                    q_hat[rows, cols[head]],
                    k_win[pl.ds(c * CHUNK, CHUNK), cols[head]],
                    (((1,), (1,)), ((), ())),
                    preferred_element_type=jnp.float32,
                )
                s = jnp.where(allowed, s * scale, NEG)
                s_ref[head, c] = s
                top = tops[head]
                for part in range(CHUNK // 128):
                    top = jnp.maximum(top, s[:, part * 128 : part * 128 + 128])
                new.append(top)
            return tuple(new)

        lowest = jnp.full((BLOCK, 128), NEG, jnp.float32)
        tops = lax.fori_loop(first, last, scores, (lowest,) * len(heads))
        highest = [jnp.max(top, axis=1, keepdims=True) for top in tops]

        def expos(c, totals):
            new = []
            for head in heads:
                e = jnp.exp(s_ref[head, c] - highest[head])
                s_ref[head, c] = e
                total = totals[head]
                for part in range(CHUNK // 128):
                    total = total + e[:, part * 128 : part * 128 + 128]
                new.append(total)
            return tuple(new)

        zeros = jnp.zeros((BLOCK, 128), jnp.float32)
        totals = lax.fori_loop(first, last, expos, (zeros,) * len(heads))
        inverse = [1.0 / jnp.sum(total, axis=1, keepdims=True) for total in totals]

        def mix(c, accs):
            new = []
            for head in heads:
                w = (s_ref[head, c] * inverse[head]).astype(jnp.bfloat16)
                v = v_win[pl.ds(c * CHUNK, CHUNK), cols[head]]
                new.append(accs[head] + jnp.dot(w, v, preferred_element_type=jnp.float32))
            return tuple(new)

        accs = lax.fori_loop(first, last, mix, (zeros,) * len(heads))
        for head in heads:
            out_ref[rows, cols[head]] = accs[head].astype(jnp.bfloat16)


def attend(q, squares, gain, own, k_parts, v_parts):
    width = q.shape[1]
    return pl.pallas_call(
        attend_kernel,
        out_shape=jax.ShapeDtypeStruct((ROWS, width), jnp.bfloat16),
        in_specs=[VMEM] * 14,
        out_specs=VMEM,
        scratch_shapes=[
            pltpu.VMEM((ROWS, width), jnp.bfloat16),
            pltpu.VMEM((WINDOW, width), jnp.bfloat16),
            pltpu.VMEM((WINDOW, width), jnp.bfloat16),
            pltpu.VMEM((WINDOW // CHUNK, 1, CHUNK), jnp.float32),
            pltpu.VMEM((width // HEAD_DIM, WINDOW // CHUNK, BLOCK, CHUNK), jnp.float32),
        ],
        compiler_params=pltpu.CompilerParams(vmem_limit_bytes=24 << 20),
        name="attend",
    )(q, squares, gain, own, *k_parts, *v_parts)


def on_device(tokens, ln_gain, w_query, w_key, w_value, q_gain, k_gain, seg_ids):
    width = w_query.shape[1]
    vq = jnp.concatenate([w_value, w_query], axis=1)
    vq = copies_to_all(vq, "seq", NY, OVER_Y).reshape(NY * SHARD_ROWS, 2 * width)
    vq, w_key = lax.optimization_barrier((vq, w_key))
    vq = lax.all_gather(vq, "seq", axis=0, axis_index_groups=OVER_Z, tiled=True)
    k_z = lax.all_gather(w_key, "seq", axis=0, axis_index_groups=OVER_Z)
    k_z, tokens, seg_ids = lax.optimization_barrier((k_z, tokens, seg_ids))
    k_all = copies_to_all(k_z.reshape(NZ * SHARD_ROWS, width), "seq", NY, OVER_Y)
    normed, moved = norm(tokens, ln_gain[None, :])
    marks = (seg_ids + 1).astype(jnp.float32)
    mark_rows = jnp.pad(marks.reshape(-1, width), ((0, MARK_ROWS - ROWS // width), (0, 0)))

    keys, squares = project_keys(normed, k_all.reshape(D, width))
    squares = copies_to_all(squares, "head", N_HEAD)
    k_own, k_last, k_first = unit_keys(
        keys, squares, k_gain[None, :], mark_rows.astype(jnp.bfloat16)
    )
    k_parts = (shifted(k_last, 2), shifted(k_own, 1), k_own, shifted(k_own, -1), shifted(k_first, -2))

    vq = pltpu.with_memory_space_constraint(vq, pltpu.HBM)
    queries, squares, v_own, v_last, v_first = project_values(moved, vq)
    squares = copies_to_all(squares, "head", N_HEAD)
    v_parts = (shifted(v_last, 2), shifted(v_own, 1), v_own, shifted(v_own, -1), shifted(v_first, -2))
    return attend(queries, squares, q_gain[None, :], marks[:, None], k_parts, v_parts)


def solution(mesh):
    return jax.shard_map(
        on_device,
        mesh=mesh,
        in_specs=(
            P("seq", None),
            P(),
            P("seq", "head"),
            P("seq", "head"),
            P("seq", "head"),
            P("head"),
            P("head"),
            P("seq"),
        ),
        out_specs=P("seq", "head"),
        check_vma=False,
    )
```

time: 218 us -> 179 us (0.82)
  the two profiles are of different devices: /device:TPU:42 before, /device:TPU:24 now
where the time goes in v4:
time: 179 us; the launch traced here: 176 us
  blocking collectives  48.3 us (27%)
  starting transfers between devices  44.5 us (25%)
  Pallas kernels  29.7 us (17%)
  waiting for transfers between devices  19.3 us (11%)
  local copies, waits for them, and re-layouts  19.1 us (11%)
  between operations  13.6 us (8%)
    all_gather x1, blocking collectives, on_device(): k_z = lax.all_gather(w_key, 'seq', axis=0, axis_index_groups=OVER_Z)  35.9 us
    ppermute x8, starting transfers between devices, shifted(): return lax.ppermute(value, 'seq', pairs)  29.8 us
    unnamed x26, local copies, waits for them, and re-layouts  14.8 us
    all_to_all x3, starting transfers between devices, copies_to_all(): return lax.all_to_all(stacked, axis, 0, 0, axis_index_groups=groups)  14.7 us
    pallas_call x1, Pallas kernels, attend(): pl.pallas_call(attend_kernel, out_shape=jax.ShapeDtypeStruct((ROWS, width...  12.8 us
    all_to_all x1, blocking collectives, copies_to_all(): return lax.all_to_all(stacked, axis, 0, 0, axis_index_groups=groups)  12.4 us
    ppermute x8, waiting for transfers between devices, shifted(): return lax.ppermute(value, 'seq', pairs)  9.88 us
    all_to_all x3, waiting for transfers between devices, copies_to_all(): return lax.all_to_all(stacked, axis, 0, 0, axis_index_groups=groups)  9.41 us
  transfers between devices with their start and end apart: 12, of which 3 were waited for; matrix products, arithmetic and copies ran while one was open for 2% of the time, Pallas kernels for 10%

profile of v4, /device:TPU:24, one launch (start us, length us, event | category | flops | bytes accessed | tf_op | source)
XLA Modules:
  0.0 175.9 jit_solution(11460123033471124591)
XLA Ops:
  6.5 0.0 copy-start.11
  6.5 0.0 all-gather.4.cloned.1.call-start
  6.5 0.8 pad_maximum_fusion
  7.3 12.4 %all_to_all.20 = bf16[4,50,512]{2,1,0:T(8,128)(2,1)S(1)} all-to-all(bf16[4,50,512]{2,1,0:T(8,128)(2,1)S(1)} %broadcast_in_dim.18), channel_id=1, replica_groups={{0,16,32,48},{1,17,33,49},{2,18,34,50},{3,19,35,51},{4,20,36,52},{5,21,..., dimensions={0} | all-to-all | bytes 409600 | tf_op jit(solution)/shard_map/all_to_all | solution.py:41
  19.7 0.7 reshape.14
  20.5 0.0 all-gather.4.cloned.1.call-update
  20.5 35.9 %all-gather.1 = bf16[16,50,256]{2,1,0:T(8,128)(2,1)S(1)} all-gather(bf16[1,50,256]{2,1,0:T(8,128)(2,1)} %bitcast.7), channel_id=2, replica_groups={{0,1,2,3,4,5,6,7,8,9,10,11,12,13,14,15},{16,17,18,19,20,21,22,23,24,25,..., dimensions={0}, use_global_device_ids=true | all-gather | bytes 435200 | tf_op jit(solution)/shard_map/all_gather | solution.py:296
  56.4 0.1 broadcast_in_dim.42
  56.6 1.3 broadcast_in_dim.43
  57.8 6.5 %all-to-all-start.2 = ((bf16[4,800,256]{2,1,0:T(8,128)(2,1)}), bf16[4,800,256]{2,1,0:T(8,128)(2,1)S(1)}, u32[]{:S(2)}, u32[]{:S(2)}) async-start(bf16[4,800,256]{2,1,0:T(8,128)(2,1)} %broadcast_in_dim.43), calls=%async_computation.2 | async-start | bytes 3276800 | tf_op jit(solution)/shard_map/all_to_all | solution.py:41
  64.4 0.0 copy-done.11
  64.4 0.0 copy-start.2
  64.4 2.4 %copy-done.2 = bf16[768,3200]{1,0:T(8,128)(2,1)S(1)} copy-done((bf16[768,3200]{1,0:T(8,128)(2,1)S(1)}, bf16[768,3200]{1,0:T(8,128)(2,1)}, u32[]{:S(2)}) %copy-start.2) | copy-done | bytes 4915224
  66.8 0.0 copy-start.12
  66.8 0.0 copy-start.9
  66.8 8.2 %norm.1 = (bf16[768,3200]{1,0:T(8,128)(2,1)S(1)}, bf16[768,3200]{1,0:T(8,128)(2,1)S(1)}) custom-call(bf16[768,3200]{1,0:T(8,128)(2,1)S(1)} %copy-done.2, f32[1,3200]{1,0:T(1,128)S(1)} %broadcast_in_dim.38.gain_ref), custom_call_target="tpu_custom_call" | custom-call | tf_op jit(solution)/shard_map/norm/pallas_call | solution.py:64
  75.0 0.0 copy-start
  75.0 2.2 %copy-done = bf16[768,3200]{1,0:T(8,128)(2,1)} copy-done((bf16[768,3200]{1,0:T(8,128)(2,1)}, bf16[768,3200]{1,0:T(8,128)(2,1)S(1)}, u32[]{:S(2)}) %copy-start) | copy-done | bytes 4915224
  77.2 0.0 copy-start.3
  77.2 2.2 %copy-done.3 = bf16[768,3200]{1,0:T(8,128)(2,1)} copy-done((bf16[768,3200]{1,0:T(8,128)(2,1)}, bf16[768,3200]{1,0:T(8,128)(2,1)S(1)}, u32[]{:S(2)}) %copy-start.3) | copy-done | bytes 4915224
  79.4 0.0 all-to-all-done.2
  79.4 0.0 copy-start.1
  79.4 2.4 %copy-done.1 = bf16[768,3200]{1,0:T(8,128)(2,1)S(1)} copy-done((bf16[768,3200]{1,0:T(8,128)(2,1)S(1)}, bf16[768,3200]{1,0:T(8,128)(2,1)}, u32[]{:S(2)}) %copy-start.1) | copy-done | bytes 4915224
  81.9 1.6 keys.1
  83.5 0.0 copy-start.10
  83.5 0.6 broadcast_in_dim.44
  84.2 4.2 %all-to-all-start.3 = ((f32[8,3,256]{2,1,0:T(4,128)}), f32[8,3,256]{2,1,0:T(4,128)S(1)}, u32[]{:S(2)}, u32[]{:S(2)}) async-start(f32[8,3,256]{2,1,0:T(4,128)} %broadcast_in_dim.44), calls=%async_computation.3 | async-start | bytes 65536 | tf_op jit(solution)/shard_map/all_to_all | solution.py:41
  88.4 0.0 copy-done.12
  88.4 0.6 fusion
  89.0 4.8 %all-to-all-done.3.squares_ref = f32[8,3,256]{2,1,0:T(4,128)S(1)} async-done(((f32[8,3,256]{2,1,0:T(4,128)}), f32[8,3,256]{2,1,0:T(4,128)S(1)}, u32[]{:S(2)}, u32[]{:S(2)}) %all-to-all-start.3) | async-done | bytes 24608 | tf_op jit(solution)/shard_map/all_to_all | solution.py:41
  93.8 0.0 copy-done.9
  93.8 0.9 unit_keys.1
  94.7 1.9 %collective-permute-start.1 = (bf16[776,256]{1,0:T(8,128)(2,1)S(1)}, bf16[776,256]{1,0:T(8,128)(2,1)S(1)}, u32[]{:S(2)}, u32[]{:S(2)}) collective-permute-start(bf16[776,256]{1,0:T(8,128)(2,1)S(1)} %get-tuple-element.34.kc), channel_id=1, source_target_pairs={{0,1},{1,2},{2,3},{3,4},{4,5},{5,6},{6,7},{7,8},{8,9},{9,10},{10,1... | collective-permute-start | bytes 1191944 | tf_op jit(solution)/shard_map/ppermute | solution.py:46
  96.7 1.9 %collective-permute-start = (bf16[264,256]{1,0:T(8,128)(2,1)}, bf16[264,256]{1,0:T(8,128)(2,1)S(1)}, u32[]{:S(2)}, u32[]{:S(2)}) collective-permute-start(bf16[264,256]{1,0:T(8,128)(2,1)} %get-tuple-element.33), channel_id=1, source_target_pairs={{0,2},{1,3},{2,4},{3,5},{4,6},{5,7},{6,8},{7,9},{8,10},{9,11},{10,... | collective-permute-start | bytes 405512 | tf_op jit(solution)/shard_map/ppermute | solution.py:46
  98.6 6.0 %collective-permute-start.2 = (bf16[776,256]{1,0:T(8,128)(2,1)S(1)}, bf16[776,256]{1,0:T(8,128)(2,1)S(1)}, u32[]{:S(2)}, u32[]{:S(2)}) collective-permute-start(bf16[776,256]{1,0:T(8,128)(2,1)S(1)} %get-tuple-element.34.kc), channel_id=1, source_target_pairs={{1,0},{2,1},{3,2},{4,3},{5,4},{6,5},{7,6},{8,7},{9,8},{10,9},{11,1... | collective-permute-start | bytes 1191944 | tf_op jit(solution)/shard_map/ppermute | solution.py:46
  104.6 0.0 all-gather.4.cloned.1.call-done.w_ref
  104.7 0.0 copy-start.4
  104.7 2.4 %copy-done.4 = bf16[768,3200]{1,0:T(8,128)(2,1)S(1)} copy-done((bf16[768,3200]{1,0:T(8,128)(2,1)S(1)}, bf16[768,3200]{1,0:T(8,128)(2,1)}, u32[]{:S(2)}) %copy-start.4) | copy-done | bytes 4915224
  107.0 6.1 %values.1 = (f32[768,256]{1,0:T(8,128)S(1)}, f32[3,256]{1,0:T(4,128)S(1)}, bf16[768,256]{1,0:T(8,128)(2,1)S(1)}, bf16[256,256]{1,0:T(8,128)(2,1)}, bf16[256,256]{1,0:T(8,128)(2,1)}) custom-call(bf16[768,3200]{1,0:T(8,128)(2,1)S(1)} %copy-done.4, bf16[3200,512]{1,0:T(8,128)(2,1)} %all-gather.4.cloned.1.call-done.w_ref), custom_call_target="tpu_custom_call" | custom-call | tf_op jit(solution)/shard_map/values/pallas_call | solution.py:130
  113.2 1.9 %collective-permute-start.5 = (bf16[768,256]{1,0:T(8,128)(2,1)S(1)}, bf16[768,256]{1,0:T(8,128)(2,1)S(1)}, u32[]{:S(2)}, u32[]{:S(2)}) collective-permute-start(bf16[768,256]{1,0:T(8,128)(2,1)S(1)} %get-tuple-element.37.vc), channel_id=1, source_target_pairs={{0,1},{1,2},{2,3},{3,4},{4,5},{5,6},{6,7},{7,8},{8,9},{9,10},{10,1... | collective-permute-start | bytes 1179656 | tf_op jit(solution)/shard_map/ppermute | solution.py:46
  115.1 6.0 %collective-permute-start.6 = (bf16[768,256]{1,0:T(8,128)(2,1)S(1)}, bf16[768,256]{1,0:T(8,128)(2,1)S(1)}, u32[]{:S(2)}, u32[]{:S(2)}) collective-permute-start(bf16[768,256]{1,0:T(8,128)(2,1)S(1)} %get-tuple-element.37.vc), channel_id=1, source_target_pairs={{1,0},{2,1},{3,2},{4,3},{5,4},{6,5},{7,6},{8,7},{9,8},{10,9},{11,1... | collective-permute-start | bytes 1179656 | tf_op jit(solution)/shard_map/ppermute | solution.py:46
  121.1 0.0 collective-permute-done.ka
  121.1 0.0 copy-start.5
  121.2 0.6 copy-done.5
  121.8 2.7 %collective-permute-start.3 = (bf16[264,256]{1,0:T(8,128)(2,1)S(1)}, bf16[264,256]{1,0:T(8,128)(2,1)S(1)}, u32[]{:S(2)}, u32[]{:S(2)}) collective-permute-start(bf16[264,256]{1,0:T(8,128)(2,1)S(1)} %get-tuple-element.35), channel_id=1, source_target_pairs={{2,0},{3,1},{4,2},{5,3},{6,4},{7,5},{8,6},{9,7},{10,8},{11,9},{12,... | collective-permute-start | bytes 405512 | tf_op jit(solution)/shard_map/ppermute | solution.py:46
  124.5 9.9 %collective-permute-done.3.ke = bf16[264,256]{1,0:T(8,128)(2,1)S(1)} collective-permute-done((bf16[264,256]{1,0:T(8,128)(2,1)S(1)}, bf16[264,256]{1,0:T(8,128)(2,1)S(1)}, u32[]{:S(2)}, u32[]{:S(2)}) %collective-permute-start.3) | collective-permute-done | bytes 135200 | tf_op jit(solution)/shard_map/ppermute | solution.py:46
  134.4 0.6 copy-done.7
  135.0 2.4 %collective-permute-start.4 = (bf16[256,256]{1,0:T(8,128)(2,1)}, bf16[256,256]{1,0:T(8,128)(2,1)}, u32[]{:S(2)}, u32[]{:S(2)}) collective-permute-start(bf16[256,256]{1,0:T(8,128)(2,1)} %get-tuple-element.36), channel_id=1, source_target_pairs={{0,2},{1,3},{2,4},{3,5},{4,6},{5,7},{6,8},{7,9},{8,10},{9,11},{10,... | collective-permute-start | bytes 393224 | tf_op jit(solution)/shard_map/ppermute | solution.py:46
  137.4 0.0 collective-permute-done.1.kb
  137.4 6.9 %collective-permute-start.7 = (bf16[256,256]{1,0:T(8,128)(2,1)}, bf16[256,256]{1,0:T(8,128)(2,1)}, u32[]{:S(2)}, u32[]{:S(2)}) collective-permute-start(bf16[256,256]{1,0:T(8,128)(2,1)} %get-tuple-element.38), channel_id=1, source_target_pairs={{2,0},{3,1},{4,2},{5,3},{6,4},{7,5},{8,6},{9,7},{10,8},{11,9},{12,... | collective-permute-start | bytes 393224 | tf_op jit(solution)/shard_map/ppermute | solution.py:46
  144.4 0.6 broadcast_in_dim.39
  145.0 3.9 %all-to-all-start.1 = ((f32[8,3,256]{2,1,0:T(4,128)}), f32[8,3,256]{2,1,0:T(4,128)}, u32[]{:S(2)}, u32[]{:S(2)}) async-start(f32[8,3,256]{2,1,0:T(4,128)} %broadcast_in_dim.39), calls=%async_computation.1 | async-start | bytes 65536 | tf_op jit(solution)/shard_map/all_to_all | solution.py:41
  148.9 0.8 broadcast_in_dim.46.own_ref
  149.8 0.0 collective-permute-done.2.kd
  149.8 4.6 %all-to-all-done.1.squares_ref = f32[8,3,256]{2,1,0:T(4,128)} async-done(((f32[8,3,256]{2,1,0:T(4,128)}), f32[8,3,256]{2,1,0:T(4,128)}, u32[]{:S(2)}, u32[]{:S(2)}) %all-to-all-start.1) | async-done | bytes 24608 | tf_op jit(solution)/shard_map/all_to_all | solution.py:41
  154.4 0.0 collective-permute-done.4.va
  154.4 0.0 collective-permute-done.7.ve
  154.4 0.0 collective-permute-done.5.vb
  154.4 0.0 collective-permute-done.6.vd
  154.4 0.0 copy-done.10
  154.4 0.0 copy-start.6
  154.4 0.9 copy-done.6
  155.3 0.9 copy-done.8
  156.2 12.8 %attend.1 = bf16[768,256]{1,0:T(8,128)(2,1)} custom-call(f32[768,256]{1,0:T(8,128)S(1)} %get-tuple-element.26.q_ref, f32[8,3,256]{2,1,0:T(4,128)} %all-to-all-done.1.squares_ref, f32[1,256]{1,0:T(1,128)S(1)} %bitcast.6, f32[768,1]{1,0:T(8,128)S(1)} %broadcast_in_dim.46.own_ref, bf16[264,256]{1,0:T(8,128)(2,1)S(1)} %copy-done.6, ...), custom_call_target="tpu_custom_call" | custom-call | tf_op jit(solution)/shard_map/attend/pallas_call | solution.py:273
  (6 shorter events, 0.1 us)
Async XLA Ops:
  6.5 57.8 %copy-start.11 = (f32[3200]{0:T(1024)S(1)}, f32[3200]{0:T(1024)}, u32[]{:S(2)}) copy-start(f32[3200]{0:T(1024)} %param.9) | copy-start | bytes 38404
  6.5 98.1 %all-gather.4.cloned.1.call-start = ((), (), s32[]{:S(2)}) async-start(), calls=%async_computation.4 | async-start | bytes 3481600 | tf_op jit(solution)/shard_map/all_gather | solution.py:295
  57.8 21.6 %all-to-all-start.2 = ((bf16[4,800,256]{2,1,0:T(8,128)(2,1)}), bf16[4,800,256]{2,1,0:T(8,128)(2,1)S(1)}, u32[]{:S(2)}, u32[]{:S(2)}) async-start(bf16[4,800,256]{2,1,0:T(8,128)(2,1)} %broadcast_in_dim.43), calls=%async_computation.2 | async-start | bytes 3276800 | tf_op jit(solution)/shard_map/all_to_all | solution.py:41
  64.4 2.4 %copy-start.2 = (bf16[768,3200]{1,0:T(8,128)(2,1)S(1)}, bf16[768,3200]{1,0:T(8,128)(2,1)}, u32[]{:S(2)}) copy-start(bf16[768,3200]{1,0:T(8,128)(2,1)} %x_ref) | copy-start | bytes 14745604
  66.8 21.6 %copy-start.12 = (s32[768]{0:T(1024)S(1)}, s32[768]{0:T(1024)}, u32[]{:S(2)}) copy-start(s32[768]{0:T(1024)} %param.15) | copy-start | bytes 9220
  66.8 27.0 %copy-start.9 = (f32[256]{0:T(256)S(1)}, f32[256]{0:T(256)}, u32[]{:S(2)}) copy-start(f32[256]{0:T(256)} %param.14) | copy-start | bytes 3076
  75.0 2.2 %copy-start = (bf16[768,3200]{1,0:T(8,128)(2,1)}, bf16[768,3200]{1,0:T(8,128)(2,1)S(1)}, u32[]{:S(2)}) copy-start(bf16[768,3200]{1,0:T(8,128)(2,1)S(1)} %get-tuple-element.29.x_ref) | copy-start | bytes 14745604
  77.2 2.2 %copy-start.3 = (bf16[768,3200]{1,0:T(8,128)(2,1)}, bf16[768,3200]{1,0:T(8,128)(2,1)S(1)}, u32[]{:S(2)}) copy-start(bf16[768,3200]{1,0:T(8,128)(2,1)S(1)} %get-tuple-element.24.x_ref) | copy-start | bytes 14745604
  79.4 2.4 %copy-start.1 = (bf16[768,3200]{1,0:T(8,128)(2,1)S(1)}, bf16[768,3200]{1,0:T(8,128)(2,1)}, u32[]{:S(2)}) copy-start(bf16[768,3200]{1,0:T(8,128)(2,1)} %copy-done) | copy-start | bytes 14745604
  83.5 70.9 %copy-start.10 = (f32[256]{0:T(256)S(1)}, f32[256]{0:T(256)}, u32[]{:S(2)}) copy-start(f32[256]{0:T(256)} %param.13) | copy-start | bytes 3076
  84.2 9.7 %all-to-all-start.3 = ((f32[8,3,256]{2,1,0:T(4,128)}), f32[8,3,256]{2,1,0:T(4,128)S(1)}, u32[]{:S(2)}, u32[]{:S(2)}) async-start(f32[8,3,256]{2,1,0:T(4,128)} %broadcast_in_dim.44), calls=%async_computation.3 | async-start | bytes 65536 | tf_op jit(solution)/shard_map/all_to_all | solution.py:41
  94.7 42.7 %collective-permute-start.1 = (bf16[776,256]{1,0:T(8,128)(2,1)S(1)}, bf16[776,256]{1,0:T(8,128)(2,1)S(1)}, u32[]{:S(2)}, u32[]{:S(2)}) collective-permute-start(bf16[776,256]{1,0:T(8,128)(2,1)S(1)} %get-tuple-element.34.kc), channel_id=1, source_target_pairs={{0,1},{1,2},{2,3},{3,4},{4,5},{5,6},{6,7},{7,8},{8,9},{9,10},{10,1... | collective-permute-start | bytes 1191944 | tf_op jit(solution)/shard_map/ppermute | solution.py:46
  96.7 24.5 %collective-permute-start = (bf16[264,256]{1,0:T(8,128)(2,1)}, bf16[264,256]{1,0:T(8,128)(2,1)S(1)}, u32[]{:S(2)}, u32[]{:S(2)}) collective-permute-start(bf16[264,256]{1,0:T(8,128)(2,1)} %get-tuple-element.33), channel_id=1, source_target_pairs={{0,2},{1,3},{2,4},{3,5},{4,6},{5,7},{6,8},{7,9},{8,10},{9,11},{10,... | collective-permute-start | bytes 405512 | tf_op jit(solution)/shard_map/ppermute | solution.py:46
  98.6 51.2 %collective-permute-start.2 = (bf16[776,256]{1,0:T(8,128)(2,1)S(1)}, bf16[776,256]{1,0:T(8,128)(2,1)S(1)}, u32[]{:S(2)}, u32[]{:S(2)}) collective-permute-start(bf16[776,256]{1,0:T(8,128)(2,1)S(1)} %get-tuple-element.34.kc), channel_id=1, source_target_pairs={{1,0},{2,1},{3,2},{4,3},{5,4},{6,5},{7,6},{8,7},{9,8},{10,9},{11,1... | collective-permute-start | bytes 1191944 | tf_op jit(solution)/shard_map/ppermute | solution.py:46
  104.7 2.4 %copy-start.4 = (bf16[768,3200]{1,0:T(8,128)(2,1)S(1)}, bf16[768,3200]{1,0:T(8,128)(2,1)}, u32[]{:S(2)}) copy-start(bf16[768,3200]{1,0:T(8,128)(2,1)} %copy-done.3) | copy-start | bytes 14745604
  113.2 41.2 %collective-permute-start.5 = (bf16[768,256]{1,0:T(8,128)(2,1)S(1)}, bf16[768,256]{1,0:T(8,128)(2,1)S(1)}, u32[]{:S(2)}, u32[]{:S(2)}) collective-permute-start(bf16[768,256]{1,0:T(8,128)(2,1)S(1)} %get-tuple-element.37.vc), channel_id=1, source_target_pairs={{0,1},{1,2},{2,3},{3,4},{4,5},{5,6},{6,7},{7,8},{8,9},{9,10},{10,1... | collective-permute-start | bytes 1179656 | tf_op jit(solution)/shard_map/ppermute | solution.py:46
  115.1 39.3 %collective-permute-start.6 = (bf16[768,256]{1,0:T(8,128)(2,1)S(1)}, bf16[768,256]{1,0:T(8,128)(2,1)S(1)}, u32[]{:S(2)}, u32[]{:S(2)}) collective-permute-start(bf16[768,256]{1,0:T(8,128)(2,1)S(1)} %get-tuple-element.37.vc), channel_id=1, source_target_pairs={{1,0},{2,1},{3,2},{4,3},{5,4},{6,5},{7,6},{8,7},{9,8},{10,9},{11,1... | collective-permute-start | bytes 1179656 | tf_op jit(solution)/shard_map/ppermute | solution.py:46
  121.1 0.7 copy-start.5
  121.8 12.6 %collective-permute-start.3 = (bf16[264,256]{1,0:T(8,128)(2,1)S(1)}, bf16[264,256]{1,0:T(8,128)(2,1)S(1)}, u32[]{:S(2)}, u32[]{:S(2)}) collective-permute-start(bf16[264,256]{1,0:T(8,128)(2,1)S(1)} %get-tuple-element.35), channel_id=1, source_target_pairs={{2,0},{3,1},{4,2},{5,3},{6,4},{7,5},{8,6},{9,7},{10,8},{11,9},{12,... | collective-permute-start | bytes 405512 | tf_op jit(solution)/shard_map/ppermute | solution.py:46
  134.4 0.7 copy-start.7
  135.0 19.4 %collective-permute-start.4 = (bf16[256,256]{1,0:T(8,128)(2,1)}, bf16[256,256]{1,0:T(8,128)(2,1)}, u32[]{:S(2)}, u32[]{:S(2)}) collective-permute-start(bf16[256,256]{1,0:T(8,128)(2,1)} %get-tuple-element.36), channel_id=1, source_target_pairs={{0,2},{1,3},{2,4},{3,5},{4,6},{5,7},{6,8},{7,9},{8,10},{9,11},{10,... | collective-permute-start | bytes 393224 | tf_op jit(solution)/shard_map/ppermute | solution.py:46
  137.4 16.9 %collective-permute-start.7 = (bf16[256,256]{1,0:T(8,128)(2,1)}, bf16[256,256]{1,0:T(8,128)(2,1)}, u32[]{:S(2)}, u32[]{:S(2)}) collective-permute-start(bf16[256,256]{1,0:T(8,128)(2,1)} %get-tuple-element.38), channel_id=1, source_target_pairs={{2,0},{3,1},{4,2},{5,3},{6,4},{7,5},{8,6},{9,7},{10,8},{11,9},{12,... | collective-permute-start | bytes 393224 | tf_op jit(solution)/shard_map/ppermute | solution.py:46
  145.0 9.4 %all-to-all-start.1 = ((f32[8,3,256]{2,1,0:T(4,128)}), f32[8,3,256]{2,1,0:T(4,128)}, u32[]{:S(2)}, u32[]{:S(2)}) async-start(f32[8,3,256]{2,1,0:T(4,128)} %broadcast_in_dim.39), calls=%async_computation.1 | async-start | bytes 65536 | tf_op jit(solution)/shard_map/all_to_all | solution.py:41
  154.4 0.9 copy-start.6
  155.3 0.9 copy-start.8
Sparse Core Ops, SparseCore 0:
  20.6 77.5 all-gather.3

commit v5 on v4

--- a/solution.py
+++ b/solution.py
@@ -46,27 +46,31 @@
     return lax.ppermute(value, "seq", pairs)
 
 
-def norm_kernel(x_ref, gain_ref, out_ref, moved_ref):
+def normalised(x_ref, gain_ref):
     x = x_ref[...].astype(jnp.float32)
     mean = jnp.sum(x * x, axis=1, keepdims=True) * (1.0 / D)
-    out_ref[...] = (x * lax.rsqrt(mean + EPS) * gain_ref[...]).astype(jnp.bfloat16)
+    return (x * lax.rsqrt(mean + EPS) * gain_ref[...]).astype(jnp.bfloat16)
+
+
+def norm_kernel(x_ref, gain_ref, out_ref, plain):
+    plain[...] = normalised(x_ref, gain_ref)
     for z in range(NZ):
         for y in range(NY):
             source = (y * NZ + z) * SHARD_ROWS
             target = (z * NY + y) * SHARD_ROWS
-            moved_ref[:, target : target + SHARD_ROWS] = out_ref[:, source : source + SHARD_ROWS]
+            out_ref[:, target : target + SHARD_ROWS] = plain[:, source : source + SHARD_ROWS]
 
 
 def norm(tokens, gain):
     rows = 128
     block = pl.BlockSpec((rows, D), lambda i: (i, 0))
-    shape = jax.ShapeDtypeStruct((ROWS, D), jnp.bfloat16)
     return pl.pallas_call(
         norm_kernel,
-        out_shape=(shape, shape),
+        out_shape=jax.ShapeDtypeStruct((ROWS, D), jnp.bfloat16),
         grid=(ROWS // rows,),
         in_specs=[block, pl.BlockSpec((1, D), lambda i: (0, 0))],
-        out_specs=(block, block),
+        out_specs=block,
+        scratch_shapes=[pltpu.VMEM((rows, D), jnp.bfloat16)],
         compiler_params=pltpu.CompilerParams(vmem_limit_bytes=10 << 20),
         name="norm",
     )(tokens, gain)
@@ -77,15 +81,82 @@
     return jnp.transpose(jnp.broadcast_to(sums, (BLOCK, 128)))[:1]
 
 
-def keys_kernel(x_ref, w_ref, k_ref, squares_ref):
-    for block in range(Q_BLOCKS):
-        rows = slice(block * BLOCK, block * BLOCK + BLOCK)
-        k = jnp.dot(x_ref[rows, :], w_ref[...], preferred_element_type=jnp.float32)
+def loads_of(x_ref, x, sem):
+    loads = []
+    for block in range(Q_BLOCKS):
+        rows = pl.ds(block * BLOCK, BLOCK)
+        loads.append(pltpu.make_async_copy(x_ref.at[rows], x.at[rows], sem.at[block]))
+    return loads
+
+
+def values_kernel(
+    x_ref, w_ref, v_ref, last_ref, first_ref, q_ref, squares_ref, x, wv, wq, sem
+):
+    width = wv.shape[1]
+    load_v = pltpu.make_async_copy(w_ref.at[:, pl.ds(0, width)], wv, sem.at[Q_BLOCKS])
+    load_q = pltpu.make_async_copy(w_ref.at[:, pl.ds(width, width)], wq, sem.at[Q_BLOCKS + 1])
+    loads = loads_of(x_ref, x, sem)
+    for load in (load_v, *loads, load_q):
+        load.start()
+    load_v.wait()
+    for block in range(Q_BLOCKS):
+        loads[block].wait()
+        rows = slice(block * BLOCK, block * BLOCK + BLOCK)
+        v = jnp.dot(x[rows, :], wv[...], preferred_element_type=jnp.float32).astype(jnp.bfloat16)
+        v_ref[rows, :] = v
+        if block == 0:
+            first_ref[...] = v
+        if block == Q_BLOCKS - 1:
+            last_ref[...] = v
+    load_q.wait()
+    for block in range(Q_BLOCKS):
+        rows = slice(block * BLOCK, block * BLOCK + BLOCK)
+        q = jnp.dot(x[rows, :], wq[...], preferred_element_type=jnp.float32)
+        q_ref[rows, :] = q
+        squares_ref[block : block + 1, :] = row_squares(q)
+
+
+def project_values(x, w, width):
+    far = jax.ShapeDtypeStruct((FAR, width), jnp.bfloat16)
+    return pl.pallas_call(
+        values_kernel,
+        out_shape=(
+            jax.ShapeDtypeStruct((ROWS, width), jnp.bfloat16),
+            far,
+            far,
+            jax.ShapeDtypeStruct((ROWS, width), jnp.float32),
+            jax.ShapeDtypeStruct((Q_BLOCKS, BLOCK), jnp.float32),
+        ),
+        in_specs=[HBM, HBM],
+        out_specs=(VMEM,) * 5,
+        scratch_shapes=[
+            pltpu.VMEM((ROWS, D), jnp.bfloat16),
+            pltpu.VMEM((D, width), jnp.bfloat16),
+            pltpu.VMEM((D, width), jnp.bfloat16),
+            pltpu.SemaphoreType.DMA((Q_BLOCKS + 2,)),
+        ],
+        compiler_params=pltpu.CompilerParams(vmem_limit_bytes=16 << 20),
+        name="values",
+    )(x, w)
+
+
+def keys_kernel(x_ref, gain_ref, w_ref, k_ref, squares_ref, x, w, sem):
+    load_w = pltpu.make_async_copy(w_ref, w, sem.at[Q_BLOCKS])
+    loads = loads_of(x_ref, x, sem)
+    for load in (loads[0], load_w, *loads[1:]):
+        load.start()
+    for block in range(Q_BLOCKS):
+        rows = slice(block * BLOCK, block * BLOCK + BLOCK)
+        loads[block].wait()
+        normed = normalised(x.at[rows, :], gain_ref)
+        if block == 0:
+            load_w.wait()
+        k = jnp.dot(normed, w[...], preferred_element_type=jnp.float32)
         k_ref[rows, :] = k
         squares_ref[block : block + 1, :] = row_squares(k)
 
 
-def project_keys(x, w):
+def project_keys(tokens, gain, w):
     width = w.shape[1]
     return pl.pallas_call(
         keys_kernel,
@@ -93,58 +164,20 @@
             jax.ShapeDtypeStruct((ROWS, width), jnp.float32),
             jax.ShapeDtypeStruct((Q_BLOCKS, BLOCK), jnp.float32),
         ),
-        in_specs=[VMEM, VMEM],
-        out_specs=(VMEM, VMEM),
-        compiler_params=pltpu.CompilerParams(vmem_limit_bytes=12 << 20),
+        in_specs=[HBM, VMEM, HBM],
+        out_specs=(VMEM,) * 2,
+        scratch_shapes=[
+            pltpu.VMEM((ROWS, D), jnp.bfloat16),
+            pltpu.VMEM((D, width), jnp.bfloat16),
+            pltpu.SemaphoreType.DMA((Q_BLOCKS + 1,)),
+        ],
+        compiler_params=pltpu.CompilerParams(vmem_limit_bytes=20 << 20),
         name="keys",
-    )(x, w)
-
-
-def values_kernel(x_ref, w_ref, q_ref, squares_ref, v_ref, last_ref, first_ref, w, sem):
-    width = v_ref.shape[1]
-    loads = [
-        pltpu.make_async_copy(w_ref.at[:, pl.ds(n * width, width)], w.at[n], sem.at[n])
-        for n in range(2)
-    ]
-    loads[1].start()
-    loads[0].start()
-    loads[1].wait()
-    for block in range(Q_BLOCKS):
-        rows = slice(block * BLOCK, block * BLOCK + BLOCK)
-        q = jnp.dot(x_ref[rows, :], w[1], preferred_element_type=jnp.float32)
-        q_ref[rows, :] = q
-        squares_ref[block : block + 1, :] = row_squares(q)
-    loads[0].wait()
-    for block in range(Q_BLOCKS):
-        rows = slice(block * BLOCK, block * BLOCK + BLOCK)
-        v_ref[rows, :] = jnp.dot(
-            x_ref[rows, :], w[0], preferred_element_type=jnp.float32
-        ).astype(jnp.bfloat16)
-    last_ref[...] = v_ref[ROWS - FAR :, :]
-    first_ref[...] = v_ref[:FAR, :]
-
-
-def project_values(x, w):
-    width = w.shape[1] // 2
-    far = jax.ShapeDtypeStruct((FAR, width), jnp.bfloat16)
-    return pl.pallas_call(
-        values_kernel,
-        out_shape=(
-            jax.ShapeDtypeStruct((ROWS, width), jnp.float32),
-            jax.ShapeDtypeStruct((Q_BLOCKS, BLOCK), jnp.float32),
-            jax.ShapeDtypeStruct((ROWS, width), jnp.bfloat16),
-            far,
-            far,
-        ),
-        in_specs=[VMEM, HBM],
-        out_specs=(VMEM,) * 5,
-        scratch_shapes=[
-            pltpu.VMEM((2, D, width), jnp.bfloat16),
-            pltpu.SemaphoreType.DMA((2,)),
-        ],
-        compiler_params=pltpu.CompilerParams(vmem_limit_bytes=14 << 20),
-        name="values",
-    )(x, w)
+    )(tokens, gain, w)
+
+
+def in_hbm(value):
+    return pltpu.with_memory_space_constraint(value, pltpu.HBM)
 
 
 def head_factors(squares_ref):
@@ -190,15 +223,18 @@
 
 
 def attend_kernel(
-    q_ref, squares_ref, q_gain_ref, own_ref, ka, kb, kc, kd, ke, va, vb, vc, vd, ve,
+    q_ref, squares_ref, q_gain_ref, own_ref, kb, kc, kd, far_a, far_e, vb, vc, vd,
     out_ref, q_hat, k_win, v_win, near_ref, s_ref,
 ):
     start = 0
-    for k_part, v_part in ((ka, va), (kb, vb), (kc, vc), (kd, vd), (ke, ve)):
-        rows = v_part.shape[0]
+    for k_part, v_part in ((far_a, None), (kb, vb), (kc, vc), (kd, vd), (far_e, None)):
+        rows = FAR if v_part is None else ROWS
         k_win[start : start + rows, :] = k_part[:rows, :]
-        v_win[start : start + rows, :] = v_part[...]
-        marks = k_part[rows:, :].astype(jnp.float32)
+        if v_part is None:
+            v_win[start : start + rows, :] = k_part[rows + MARK_ROWS :, :]
+        else:
+            v_win[start : start + rows, :] = v_part[...]
+        marks = k_part[rows : rows + MARK_ROWS, :].astype(jnp.float32)
         if start > OWN:
             marks = jnp.where(marks == 0, BEYOND, marks)
         for n in range(rows // CHUNK):
@@ -268,12 +304,12 @@
             out_ref[rows, cols[head]] = accs[head].astype(jnp.bfloat16)
 
 
-def attend(q, squares, gain, own, k_parts, v_parts):
+def attend(q, squares, gain, own, k_parts, far_parts, v_parts):
     width = q.shape[1]
     return pl.pallas_call(
         attend_kernel,
         out_shape=jax.ShapeDtypeStruct((ROWS, width), jnp.bfloat16),
-        in_specs=[VMEM] * 14,
+        in_specs=[VMEM] * 12,
         out_specs=VMEM,
         scratch_shapes=[
             pltpu.VMEM((ROWS, width), jnp.bfloat16),
@@ -284,7 +320,7 @@
         ],
         compiler_params=pltpu.CompilerParams(vmem_limit_bytes=24 << 20),
         name="attend",
-    )(q, squares, gain, own, *k_parts, *v_parts)
+    )(q, squares, gain, own, *k_parts, *far_parts, *v_parts)
 
 
 def on_device(tokens, ln_gain, w_query, w_key, w_value, q_gain, k_gain, seg_ids):
@@ -294,24 +330,32 @@
     vq, w_key = lax.optimization_barrier((vq, w_key))
     vq = lax.all_gather(vq, "seq", axis=0, axis_index_groups=OVER_Z, tiled=True)
     k_z = lax.all_gather(w_key, "seq", axis=0, axis_index_groups=OVER_Z)
-    k_z, tokens, seg_ids = lax.optimization_barrier((k_z, tokens, seg_ids))
+    gain = ln_gain[None, :]
+    k_z, late_tokens, seg_ids = lax.optimization_barrier((k_z, tokens, seg_ids))
     k_all = copies_to_all(k_z.reshape(NZ * SHARD_ROWS, width), "seq", NY, OVER_Y)
-    normed, moved = norm(tokens, ln_gain[None, :])
+    k_all, moved = lax.optimization_barrier((k_all, norm(late_tokens, gain)))
+    moved = in_hbm(moved)
     marks = (seg_ids + 1).astype(jnp.float32)
     mark_rows = jnp.pad(marks.reshape(-1, width), ((0, MARK_ROWS - ROWS // width), (0, 0)))
 
-    keys, squares = project_keys(normed, k_all.reshape(D, width))
+    keys, squares = project_keys(in_hbm(tokens), gain, in_hbm(k_all.reshape(D, width)))
     squares = copies_to_all(squares, "head", N_HEAD)
     k_own, k_last, k_first = unit_keys(
         keys, squares, k_gain[None, :], mark_rows.astype(jnp.bfloat16)
     )
-    k_parts = (shifted(k_last, 2), shifted(k_own, 1), k_own, shifted(k_own, -1), shifted(k_first, -2))
-
-    vq = pltpu.with_memory_space_constraint(vq, pltpu.HBM)
-    queries, squares, v_own, v_last, v_first = project_values(moved, vq)
+    k_parts = (shifted(k_own, 1), k_own, shifted(k_own, -1))
+
+    vq = in_hbm(vq)
+    v_own, v_last, v_first, queries, squares = project_values(moved, vq, width)
     squares = copies_to_all(squares, "head", N_HEAD)
-    v_parts = (shifted(v_last, 2), shifted(v_own, 1), v_own, shifted(v_own, -1), shifted(v_first, -2))
-    return attend(queries, squares, q_gain[None, :], marks[:, None], k_parts, v_parts)
+    far_parts = (
+        shifted(jnp.concatenate([k_last, v_last], axis=0), 2),
+        shifted(jnp.concatenate([k_first, v_first], axis=0), -2),
+    )
+    v_parts = (shifted(v_own, 1), v_own, shifted(v_own, -1))
+    return attend(
+        queries, squares, q_gain[None, :], marks[:, None], k_parts, far_parts, v_parts
+    )
 
 
 def solution(mesh):

time: 179 us -> 162 us (0.905)
  waiting for transfers between devices: 19.3 us -> 11.3 us
  local copies, waits for them, and re-layouts: 19.1 us -> 11.5 us
  starting transfers between devices: 44.5 us -> 37.1 us
  Pallas kernels: 29.7 us -> 35.5 us
    ppermute x8 -> x6, waiting for transfers between devices: 9.88 us -> 1.88 us  [shifted(): return lax.ppermute(value, 'seq', pairs)]
    unnamed x26 -> x22, local copies, waits for them, and re-layouts: 14.8 us -> 7.17 us
    ppermute x8 -> x6, starting transfers between devices: 29.8 us -> 22.7 us  [shifted(): return lax.ppermute(value, 'seq', pairs)]
    pallas_call x1, Pallas kernels: 1.64 us -> 5.94 us  [project_keys(): pl.pallas_call(keys_kernel, out_shape=(jax.ShapeDtypeStruct((ROWS, width)...]
  transfers between devices with their start and end apart: 12 -> 10, of which waited for: 3 -> 4; matrix products, arithmetic and copies ran while one was open for 2% -> 3% of each run, Pallas kernels for 10% -> 13%
where the time goes in v5:
time: 162 us; the launch traced here: 160 us
  blocking collectives  48.3 us (30%)
  starting transfers between devices  37.1 us (23%)
  Pallas kernels  35.5 us (22%)
  between operations  13.6 us (8%)
  local copies, waits for them, and re-layouts  11.5 us (7%)
  waiting for transfers between devices  11.3 us (7%)
  other arithmetic  2.81 us (2%)
    all_gather x1, blocking collectives, on_device(): k_z = lax.all_gather(w_key, 'seq', axis=0, axis_index_groups=OVER_Z)  35.9 us
    ppermute x6, starting transfers between devices, shifted(): return lax.ppermute(value, 'seq', pairs)  22.7 us
    all_to_all x3, starting transfers between devices, copies_to_all(): return lax.all_to_all(stacked, axis, 0, 0, axis_index_groups=groups)  14.4 us
    pallas_call x1, Pallas kernels, attend(): pl.pallas_call(attend_kernel, out_shape=jax.ShapeDtypeStruct((ROWS, width...  14.1 us
    all_to_all x1, blocking collectives, copies_to_all(): return lax.all_to_all(stacked, axis, 0, 0, axis_index_groups=groups)  12.4 us
    all_to_all x3, waiting for transfers between devices, copies_to_all(): return lax.all_to_all(stacked, axis, 0, 0, axis_index_groups=groups)  9.41 us
    pallas_call x1, Pallas kernels, norm(): pl.pallas_call(norm_kernel, out_shape=jax.ShapeDtypeStruct((ROWS, D), jnp...  8.15 us
    unnamed x22, local copies, waits for them, and re-layouts  7.17 us
  transfers between devices with their start and end apart: 10, of which 4 were waited for; matrix products, arithmetic and copies ran while one was open for 3% of the time, Pallas kernels for 13%

profile of v5, /device:TPU:24, one launch (start us, length us, event | category | flops | bytes accessed | tf_op | source)
XLA Modules:
  0.0 160.2 jit_solution(509135904387773694)
XLA Ops:
  6.5 0.0 all-gather.4.cloned.1.call-start
  6.5 0.8 pad_maximum_fusion.2
  7.3 12.4 %all_to_all.20 = bf16[4,50,512]{2,1,0:T(8,128)(2,1)S(1)} all-to-all(bf16[4,50,512]{2,1,0:T(8,128)(2,1)S(1)} %broadcast_in_dim.18), channel_id=1, replica_groups={{0,16,32,48},{1,17,33,49},{2,18,34,50},{3,19,35,51},{4,20,36,52},{5,21,..., dimensions={0} | all-to-all | bytes 409600 | tf_op jit(solution)/shard_map/all_to_all | solution.py:41
  19.7 0.7 reshape.14
  20.5 0.0 all-gather.4.cloned.1.call-update
  20.5 0.0 copy-start.9
  20.5 35.9 %all-gather.1 = bf16[16,50,256]{2,1,0:T(8,128)(2,1)S(1)} all-gather(bf16[1,50,256]{2,1,0:T(8,128)(2,1)} %bitcast.7), channel_id=2, replica_groups={{0,1,2,3,4,5,6,7,8,9,10,11,12,13,14,15},{16,17,18,19,20,21,22,23,24,25,..., dimensions={0}, use_global_device_ids=true | all-gather | bytes 435200 | tf_op jit(solution)/shard_map/all_gather | solution.py:332
  56.4 0.1 broadcast_in_dim.38
  56.6 1.3 broadcast_in_dim.39
  57.9 6.8 %all-to-all-start.1 = ((bf16[4,800,256]{2,1,0:T(8,128)(2,1)}), bf16[4,800,256]{2,1,0:T(8,128)(2,1)S(1)}, u32[]{:S(2)}, u32[]{:S(2)}) async-start(bf16[4,800,256]{2,1,0:T(8,128)(2,1)} %broadcast_in_dim.39), calls=%async_computation.1 | async-start | bytes 3276800 | tf_op jit(solution)/shard_map/all_to_all | solution.py:41
  64.7 0.0 copy-done.9
  64.7 0.0 copy-start
  64.7 2.4 %copy-done = bf16[768,3200]{1,0:T(8,128)(2,1)S(1)} copy-done((bf16[768,3200]{1,0:T(8,128)(2,1)S(1)}, bf16[768,3200]{1,0:T(8,128)(2,1)}, u32[]{:S(2)}) %copy-start) | copy-done | bytes 4915224
  67.1 8.1 %norm.1.x_ref = bf16[768,3200]{1,0:T(8,128)(2,1)S(1)} custom-call(bf16[768,3200]{1,0:T(8,128)(2,1)S(1)} %copy-done, f32[1,3200]{1,0:T(1,128)S(1)} %broadcast_in_dim.40.gain_ref), custom_call_target="tpu_custom_call" | custom-call | tf_op jit(solution)/shard_map/norm/pallas_call | solution.py:67
  75.3 0.0 copy-start.1
  75.3 2.2 %copy-done.1 = bf16[768,3200]{1,0:T(8,128)(2,1)} copy-done((bf16[768,3200]{1,0:T(8,128)(2,1)}, bf16[768,3200]{1,0:T(8,128)(2,1)S(1)}, u32[]{:S(2)}) %copy-start.1) | copy-done | bytes 4915224
  77.5 0.0 all-to-all-done.1
  77.5 0.0 copy-start.8
  77.5 1.2 copy-done.8
  78.7 0.0 copy-start.10
  78.7 0.0 copy-start.6
  78.7 5.9 %keys.1 = (f32[768,256]{1,0:T(8,128)S(1)}, f32[3,256]{1,0:T(4,128)S(1)}) custom-call(bf16[768,3200]{1,0:T(8,128)(2,1)} %x_ref.2, f32[1,3200]{1,0:T(1,128)S(1)} %broadcast_in_dim.40.gain_ref, bf16[3200,256]{1,0:T(8,128)(2,1)} %bitcast.6), custom_call_target="tpu_custom_call" | custom-call | tf_op jit(solution)/shard_map/keys/pallas_call | solution.py:161
  84.7 0.6 broadcast_in_dim.44
  85.3 3.6 %all-to-all-start.3 = ((f32[8,3,256]{2,1,0:T(4,128)}), f32[8,3,256]{2,1,0:T(4,128)S(1)}, u32[]{:S(2)}, u32[]{:S(2)}) async-start(f32[8,3,256]{2,1,0:T(4,128)} %broadcast_in_dim.44), calls=%async_computation.3 | async-start | bytes 65536 | tf_op jit(solution)/shard_map/all_to_all | solution.py:41
  88.9 0.0 copy-done.10
  88.9 0.6 fusion
  89.5 4.8 %all-to-all-done.3.squares_ref = f32[8,3,256]{2,1,0:T(4,128)S(1)} async-done(((f32[8,3,256]{2,1,0:T(4,128)}), f32[8,3,256]{2,1,0:T(4,128)S(1)}, u32[]{:S(2)}, u32[]{:S(2)}) %all-to-all-start.3) | async-done | bytes 24608 | tf_op jit(solution)/shard_map/all_to_all | solution.py:41
  94.3 0.0 copy-done.6
  94.3 0.2 unit_keys.1
  94.6 0.0 copy-start.2
  94.6 0.6 copy-done.2
  95.2 0.0 copy-start.4
  95.2 0.7 copy-done.4
  95.9 0.0 copy-start.5
  95.9 0.0 copy-start.3
  95.9 0.0 copy-start.7
  95.9 2.0 %collective-permute-start = (bf16[776,256]{1,0:T(8,128)(2,1)S(1)}, bf16[776,256]{1,0:T(8,128)(2,1)S(1)}, u32[]{:S(2)}, u32[]{:S(2)}) collective-permute-start(bf16[776,256]{1,0:T(8,128)(2,1)S(1)} %get-tuple-element.33.kc), channel_id=1, source_target_pairs={{0,1},{1,2},{2,3},{3,4},{4,5},{5,6},{6,7},{7,8},{8,9},{9,10},{10,1... | collective-permute-start | bytes 1191944 | tf_op jit(solution)/shard_map/ppermute | solution.py:46
  97.9 6.0 %collective-permute-start.1 = (bf16[776,256]{1,0:T(8,128)(2,1)S(1)}, bf16[776,256]{1,0:T(8,128)(2,1)S(1)}, u32[]{:S(2)}, u32[]{:S(2)}) collective-permute-start(bf16[776,256]{1,0:T(8,128)(2,1)S(1)} %get-tuple-element.33.kc), channel_id=1, source_target_pairs={{1,0},{2,1},{3,2},{4,3},{5,4},{6,5},{7,6},{8,7},{9,8},{10,9},{11,1... | collective-permute-start | bytes 1191944 | tf_op jit(solution)/shard_map/ppermute | solution.py:46
  104.0 0.0 all-gather.4.cloned.1.call-done.w_ref
  104.0 7.1 %values.1 = (bf16[768,256]{1,0:T(8,128)(2,1)S(1)}, bf16[256,256]{1,0:T(8,128)(2,1)S(1)}, bf16[256,256]{1,0:T(8,128)(2,1)S(1)}, f32[768,256]{1,0:T(8,128)S(1)}, f32[3,256]{1,0:T(4,128)S(1)}) custom-call(bf16[768,3200]{1,0:T(8,128)(2,1)} %copy-done.1, bf16[3200,512]{1,0:T(8,128)(2,1)} %all-gather.4.cloned.1.call-done.w_ref), custom_call_target="tpu_custom_call" | custom-call | tf_op jit(solution)/shard_map/values/pallas_call | solution.py:121
  111.1 1.9 %collective-permute-start.4 = (bf16[768,256]{1,0:T(8,128)(2,1)S(1)}, bf16[768,256]{1,0:T(8,128)(2,1)S(1)}, u32[]{:S(2)}, u32[]{:S(2)}) collective-permute-start(bf16[768,256]{1,0:T(8,128)(2,1)S(1)} %get-tuple-element.38.vc), channel_id=1, source_target_pairs={{0,1},{1,2},{2,3},{3,4},{4,5},{5,6},{6,7},{7,8},{8,9},{9,10},{10,1... | collective-permute-start | bytes 1179656 | tf_op jit(solution)/shard_map/ppermute | solution.py:46
  113.0 6.0 %collective-permute-start.5 = (bf16[768,256]{1,0:T(8,128)(2,1)S(1)}, bf16[768,256]{1,0:T(8,128)(2,1)S(1)}, u32[]{:S(2)}, u32[]{:S(2)}) collective-permute-start(bf16[768,256]{1,0:T(8,128)(2,1)S(1)} %get-tuple-element.38.vc), channel_id=1, source_target_pairs={{1,0},{2,1},{3,2},{4,3},{5,4},{6,5},{7,6},{8,7},{9,8},{10,9},{11,1... | collective-permute-start | bytes 1179656 | tf_op jit(solution)/shard_map/ppermute | solution.py:46
  119.1 0.0 copy-done.5
  119.1 0.7 pad_maximum_fusion.1
  119.8 1.9 %collective-permute-start.3 = (bf16[520,256]{1,0:T(8,128)(2,1)}, bf16[520,256]{1,0:T(8,128)(2,1)}, u32[]{:S(2)}, u32[]{:S(2)}) collective-permute-start(bf16[520,256]{1,0:T(8,128)(2,1)} %pad_maximum_fusion.1), channel_id=1, source_target_pairs={{2,0},{3,1},{4,2},{5,3},{6,4},{7,5},{8,6},{9,7},{10,8},{11,9},{12,... | collective-permute-start | bytes 798728 | tf_op jit(solution)/shard_map/ppermute | solution.py:46
  121.7 0.0 copy-done.3
  121.7 0.7 pad_maximum_fusion
  122.5 0.0 collective-permute-done.kb
  122.5 4.8 %collective-permute-start.2 = (bf16[520,256]{1,0:T(8,128)(2,1)}, bf16[520,256]{1,0:T(8,128)(2,1)}, u32[]{:S(2)}, u32[]{:S(2)}) collective-permute-start(bf16[520,256]{1,0:T(8,128)(2,1)} %pad_maximum_fusion), channel_id=1, source_target_pairs={{0,2},{1,3},{2,4},{3,5},{4,6},{5,7},{6,8},{7,9},{8,10},{9,11},{10,... | collective-permute-start | bytes 798728 | tf_op jit(solution)/shard_map/ppermute | solution.py:46
  127.3 0.6 broadcast_in_dim.41
  127.9 4.0 %all-to-all-start.2 = ((f32[8,3,256]{2,1,0:T(4,128)}), f32[8,3,256]{2,1,0:T(4,128)}, u32[]{:S(2)}, u32[]{:S(2)}) async-start(f32[8,3,256]{2,1,0:T(4,128)} %broadcast_in_dim.41), calls=%async_computation.2 | async-start | bytes 65536 | tf_op jit(solution)/shard_map/all_to_all | solution.py:41
  131.9 0.8 broadcast_in_dim.46.own_ref
  132.7 0.0 collective-permute-done.1.kd
  132.7 4.6 %all-to-all-done.2.squares_ref = f32[8,3,256]{2,1,0:T(4,128)} async-done(((f32[8,3,256]{2,1,0:T(4,128)}), f32[8,3,256]{2,1,0:T(4,128)}, u32[]{:S(2)}, u32[]{:S(2)}) %all-to-all-start.2) | async-done | bytes 24608 | tf_op jit(solution)/shard_map/all_to_all | solution.py:41
  137.3 0.8 collective-permute-done.3.far_e
  138.1 1.1 collective-permute-done.2.far_a
  139.2 0.0 collective-permute-done.4.vb
  139.2 0.0 collective-permute-done.5.vd
  139.2 0.0 copy-done.7
  139.2 14.1 %attend.1 = bf16[768,256]{1,0:T(8,128)(2,1)} custom-call(f32[768,256]{1,0:T(8,128)S(1)} %get-tuple-element.27.q_ref, f32[8,3,256]{2,1,0:T(4,128)} %all-to-all-done.2.squares_ref, f32[1,256]{1,0:T(1,128)S(1)} %bitcast.5, f32[768,1]{1,0:T(8,128)S(1)} %broadcast_in_dim.46.own_ref, bf16[776,256]{1,0:T(8,128)(2,1)S(1)} %collective-permute-done.kb, ...), custom_call_target="tpu_custom_call" | custom-call | tf_op jit(solution)/shard_map/attend/pallas_call | solution.py:309
  (4 shorter events, 0.1 us)
Async XLA Ops:
  6.5 97.5 %all-gather.4.cloned.1.call-start = ((), (), s32[]{:S(2)}) async-start(), calls=%async_computation.4 | async-start | bytes 3481600 | tf_op jit(solution)/shard_map/all_gather | solution.py:331
  20.5 44.2 %copy-start.9 = (f32[3200]{0:T(1024)S(1)}, f32[3200]{0:T(1024)}, u32[]{:S(2)}) copy-start(f32[3200]{0:T(1024)} %param.9) | copy-start | bytes 38404
  57.9 19.6 %all-to-all-start.1 = ((bf16[4,800,256]{2,1,0:T(8,128)(2,1)}), bf16[4,800,256]{2,1,0:T(8,128)(2,1)S(1)}, u32[]{:S(2)}, u32[]{:S(2)}) async-start(bf16[4,800,256]{2,1,0:T(8,128)(2,1)} %broadcast_in_dim.39), calls=%async_computation.1 | async-start | bytes 3276800 | tf_op jit(solution)/shard_map/all_to_all | solution.py:41
  64.7 2.4 %copy-start = (bf16[768,3200]{1,0:T(8,128)(2,1)S(1)}, bf16[768,3200]{1,0:T(8,128)(2,1)}, u32[]{:S(2)}) copy-start(bf16[768,3200]{1,0:T(8,128)(2,1)} %x_ref.2) | copy-start | bytes 14745604
  75.3 2.2 %copy-start.1 = (bf16[768,3200]{1,0:T(8,128)(2,1)}, bf16[768,3200]{1,0:T(8,128)(2,1)S(1)}, u32[]{:S(2)}) copy-start(bf16[768,3200]{1,0:T(8,128)(2,1)S(1)} %norm.1.x_ref) | copy-start | bytes 14745604
  77.5 1.2 copy-start.8
  78.7 10.2 %copy-start.10 = (s32[768]{0:T(1024)S(1)}, s32[768]{0:T(1024)}, u32[]{:S(2)}) copy-start(s32[768]{0:T(1024)} %param.15) | copy-start | bytes 9220
  78.7 15.6 %copy-start.6 = (f32[256]{0:T(256)S(1)}, f32[256]{0:T(256)}, u32[]{:S(2)}) copy-start(f32[256]{0:T(256)} %param.14) | copy-start | bytes 3076
  85.3 9.1 %all-to-all-start.3 = ((f32[8,3,256]{2,1,0:T(4,128)}), f32[8,3,256]{2,1,0:T(4,128)S(1)}, u32[]{:S(2)}, u32[]{:S(2)}) async-start(f32[8,3,256]{2,1,0:T(4,128)} %broadcast_in_dim.44), calls=%async_computation.3 | async-start | bytes 65536 | tf_op jit(solution)/shard_map/all_to_all | solution.py:41
  94.6 0.7 copy-start.2
  95.2 0.7 copy-start.4
  95.9 23.2 %copy-start.5 = (bf16[264,256]{1,0:T(8,128)(2,1)S(1)}, bf16[264,256]{1,0:T(8,128)(2,1)}, u32[]{:S(2)}) copy-start(bf16[264,256]{1,0:T(8,128)(2,1)} %copy-done.4) | copy-start | bytes 405508
  95.9 25.8 %copy-start.3 = (bf16[264,256]{1,0:T(8,128)(2,1)S(1)}, bf16[264,256]{1,0:T(8,128)(2,1)}, u32[]{:S(2)}) copy-start(bf16[264,256]{1,0:T(8,128)(2,1)} %copy-done.2) | copy-start | bytes 405508
  95.9 43.3 %copy-start.7 = (f32[256]{0:T(256)S(1)}, f32[256]{0:T(256)}, u32[]{:S(2)}) copy-start(f32[256]{0:T(256)} %param.13) | copy-start | bytes 3076
  95.9 26.6 %collective-permute-start = (bf16[776,256]{1,0:T(8,128)(2,1)S(1)}, bf16[776,256]{1,0:T(8,128)(2,1)S(1)}, u32[]{:S(2)}, u32[]{:S(2)}) collective-permute-start(bf16[776,256]{1,0:T(8,128)(2,1)S(1)} %get-tuple-element.33.kc), channel_id=1, source_target_pairs={{0,1},{1,2},{2,3},{3,4},{4,5},{5,6},{6,7},{7,8},{8,9},{9,10},{10,1... | collective-permute-start | bytes 1191944 | tf_op jit(solution)/shard_map/ppermute | solution.py:46
  97.9 34.8 %collective-permute-start.1 = (bf16[776,256]{1,0:T(8,128)(2,1)S(1)}, bf16[776,256]{1,0:T(8,128)(2,1)S(1)}, u32[]{:S(2)}, u32[]{:S(2)}) collective-permute-start(bf16[776,256]{1,0:T(8,128)(2,1)S(1)} %get-tuple-element.33.kc), channel_id=1, source_target_pairs={{1,0},{2,1},{3,2},{4,3},{5,4},{6,5},{7,6},{8,7},{9,8},{10,9},{11,1... | collective-permute-start | bytes 1191944 | tf_op jit(solution)/shard_map/ppermute | solution.py:46
  111.1 28.1 %collective-permute-start.4 = (bf16[768,256]{1,0:T(8,128)(2,1)S(1)}, bf16[768,256]{1,0:T(8,128)(2,1)S(1)}, u32[]{:S(2)}, u32[]{:S(2)}) collective-permute-start(bf16[768,256]{1,0:T(8,128)(2,1)S(1)} %get-tuple-element.38.vc), channel_id=1, source_target_pairs={{0,1},{1,2},{2,3},{3,4},{4,5},{5,6},{6,7},{7,8},{8,9},{9,10},{10,1... | collective-permute-start | bytes 1179656 | tf_op jit(solution)/shard_map/ppermute | solution.py:46
  113.0 26.1 %collective-permute-start.5 = (bf16[768,256]{1,0:T(8,128)(2,1)S(1)}, bf16[768,256]{1,0:T(8,128)(2,1)S(1)}, u32[]{:S(2)}, u32[]{:S(2)}) collective-permute-start(bf16[768,256]{1,0:T(8,128)(2,1)S(1)} %get-tuple-element.38.vc), channel_id=1, source_target_pairs={{1,0},{2,1},{3,2},{4,3},{5,4},{6,5},{7,6},{8,7},{9,8},{10,9},{11,1... | collective-permute-start | bytes 1179656 | tf_op jit(solution)/shard_map/ppermute | solution.py:46
  119.8 18.3 %collective-permute-start.3 = (bf16[520,256]{1,0:T(8,128)(2,1)}, bf16[520,256]{1,0:T(8,128)(2,1)}, u32[]{:S(2)}, u32[]{:S(2)}) collective-permute-start(bf16[520,256]{1,0:T(8,128)(2,1)} %pad_maximum_fusion.1), channel_id=1, source_target_pairs={{2,0},{3,1},{4,2},{5,3},{6,4},{7,5},{8,6},{9,7},{10,8},{11,9},{12,... | collective-permute-start | bytes 798728 | tf_op jit(solution)/shard_map/ppermute | solution.py:46
  122.5 16.7 %collective-permute-start.2 = (bf16[520,256]{1,0:T(8,128)(2,1)}, bf16[520,256]{1,0:T(8,128)(2,1)}, u32[]{:S(2)}, u32[]{:S(2)}) collective-permute-start(bf16[520,256]{1,0:T(8,128)(2,1)} %pad_maximum_fusion), channel_id=1, source_target_pairs={{0,2},{1,3},{2,4},{3,5},{4,6},{5,7},{6,8},{7,9},{8,10},{9,11},{10,... | collective-permute-start | bytes 798728 | tf_op jit(solution)/shard_map/ppermute | solution.py:46
  127.9 9.4 %all-to-all-start.2 = ((f32[8,3,256]{2,1,0:T(4,128)}), f32[8,3,256]{2,1,0:T(4,128)}, u32[]{:S(2)}, u32[]{:S(2)}) async-start(f32[8,3,256]{2,1,0:T(4,128)} %broadcast_in_dim.41), calls=%async_computation.2 | async-start | bytes 65536 | tf_op jit(solution)/shard_map/all_to_all | solution.py:41
Sparse Core Ops, SparseCore 0:
  20.6 77.7 all-gather.3

commit v6 on v5

--- a/solution.py
+++ b/solution.py
@@ -24,6 +24,8 @@
 N_BLOCKS = WINDOW // BLOCK
 Q_BLOCKS = ROWS // BLOCK
 CHUNK = 256
+TOGETHER = 2
+PADDED = WINDOW + (TOGETHER - 1) * CHUNK
 NEG = -1e30
 BEYOND = 1e6
 SHARD_ROWS = D // N_SEQ
@@ -89,55 +91,52 @@
     return loads
 
 
-def values_kernel(
-    x_ref, w_ref, v_ref, last_ref, first_ref, q_ref, squares_ref, x, wv, wq, sem
-):
-    width = wv.shape[1]
-    load_v = pltpu.make_async_copy(w_ref.at[:, pl.ds(0, width)], wv, sem.at[Q_BLOCKS])
-    load_q = pltpu.make_async_copy(w_ref.at[:, pl.ds(width, width)], wq, sem.at[Q_BLOCKS + 1])
+def loaded_blocks(x_ref, w_ref, at, x, w, sem):
+    load_w = pltpu.make_async_copy(w_ref.at[:, pl.ds(at, w.shape[1])], w, sem.at[Q_BLOCKS])
     loads = loads_of(x_ref, x, sem)
-    for load in (load_v, *loads, load_q):
+    for load in (load_w, *loads):
         load.start()
-    load_v.wait()
+    load_w.wait()
     for block in range(Q_BLOCKS):
         loads[block].wait()
         rows = slice(block * BLOCK, block * BLOCK + BLOCK)
-        v = jnp.dot(x[rows, :], wv[...], preferred_element_type=jnp.float32).astype(jnp.bfloat16)
+        yield block, rows, jnp.dot(x[rows, :], w[...], preferred_element_type=jnp.float32)
+
+
+def values_kernel(
+    x_ref, w_ref, k_last, k_first, v_ref, last_ref, first_ref, x, w, sem
+):
+    last_ref[: FAR + MARK_ROWS, :] = k_last[...]
+    first_ref[: FAR + MARK_ROWS, :] = k_first[...]
+    for block, rows, y in loaded_blocks(x_ref, w_ref, 0, x, w, sem):
+        v = y.astype(jnp.bfloat16)
         v_ref[rows, :] = v
         if block == 0:
-            first_ref[...] = v
+            first_ref[FAR + MARK_ROWS :, :] = v
         if block == Q_BLOCKS - 1:
-            last_ref[...] = v
-    load_q.wait()
-    for block in range(Q_BLOCKS):
-        rows = slice(block * BLOCK, block * BLOCK + BLOCK)
-        q = jnp.dot(x[rows, :], wq[...], preferred_element_type=jnp.float32)
+            last_ref[FAR + MARK_ROWS :, :] = v
+
+
+def queries_kernel(x_ref, w_ref, q_ref, squares_ref, x, w, sem):
+    for block, rows, q in loaded_blocks(x_ref, w_ref, w.shape[1], x, w, sem):
         q_ref[rows, :] = q
         squares_ref[block : block + 1, :] = row_squares(q)
 
 
-def project_values(x, w, width):
-    far = jax.ShapeDtypeStruct((FAR, width), jnp.bfloat16)
-    return pl.pallas_call(
-        values_kernel,
-        out_shape=(
-            jax.ShapeDtypeStruct((ROWS, width), jnp.bfloat16),
-            far,
-            far,
-            jax.ShapeDtypeStruct((ROWS, width), jnp.float32),
-            jax.ShapeDtypeStruct((Q_BLOCKS, BLOCK), jnp.float32),
-        ),
-        in_specs=[HBM, HBM],
-        out_specs=(VMEM,) * 5,
+def project(kernel, name, outs, width, x, w, *more):
+    return pl.pallas_call(
+        kernel,
+        out_shape=outs,
+        in_specs=[HBM, HBM] + [VMEM] * len(more),
+        out_specs=(VMEM,) * len(outs),
         scratch_shapes=[
             pltpu.VMEM((ROWS, D), jnp.bfloat16),
             pltpu.VMEM((D, width), jnp.bfloat16),
-            pltpu.VMEM((D, width), jnp.bfloat16),
-            pltpu.SemaphoreType.DMA((Q_BLOCKS + 2,)),
+            pltpu.SemaphoreType.DMA((Q_BLOCKS + 1,)),
         ],
         compiler_params=pltpu.CompilerParams(vmem_limit_bytes=16 << 20),
-        name="values",
-    )(x, w)
+        name=name,
+    )(x, w, *more)
 
 
 def keys_kernel(x_ref, gain_ref, w_ref, k_ref, squares_ref, x, w, sem):
@@ -223,7 +222,7 @@
 
 
 def attend_kernel(
-    q_ref, squares_ref, q_gain_ref, own_ref, kb, kc, kd, far_a, far_e, vb, vc, vd,
+    marks_ref, q_ref, squares_ref, q_gain_ref, own_ref, kb, kc, kd, far_a, far_e, vb, vc, vd,
     out_ref, q_hat, k_win, v_win, near_ref, s_ref,
 ):
     start = 0
@@ -240,6 +239,20 @@
         for n in range(rows // CHUNK):
             near_ref[start // CHUNK + n] = marks[n : n + 1]
         start += rows
+    k_win[WINDOW:, :] = jnp.zeros((PADDED - WINDOW, k_win.shape[1]), jnp.bfloat16)
+    v_win[WINDOW:, :] = jnp.zeros((PADDED - WINDOW, v_win.shape[1]), jnp.bfloat16)
+    for c in range(WINDOW // CHUNK, PADDED // CHUNK):
+        near_ref[c] = jnp.full((1, CHUNK), BEYOND, jnp.float32)
+    near = [near_ref[c] for c in range(WINDOW // CHUNK)]
+    bounds = []
+    for block in range(Q_BLOCKS):
+        low, high = marks_ref[block * BLOCK], marks_ref[block * BLOCK + BLOCK - 1]
+        below = sum((marks < low).astype(jnp.float32) for marks in near)
+        within = sum((marks <= high).astype(jnp.float32) for marks in near)
+        below = jnp.sum(below).astype(jnp.int32)
+        within = jnp.sum(within).astype(jnp.int32)
+        first = below // CHUNK
+        bounds.append((first, ((within + CHUNK - 1) // CHUNK - first + TOGETHER - 1) // TOGETHER))
     unit(q_ref, q_hat, q_gain_ref, head_factors(squares_ref))
 
     scale = 1.0 / math.sqrt(HEAD_DIM)
@@ -248,79 +261,70 @@
     for block in range(Q_BLOCKS):
         rows = slice(block * BLOCK, block * BLOCK + BLOCK)
         own = own_ref[rows, :]
-        low, high = jnp.min(own), jnp.max(own)
-        near = near_ref[...]
-        below = jnp.sum((near < low).astype(jnp.float32)).astype(jnp.int32)
-        within = jnp.sum((near <= high).astype(jnp.float32)).astype(jnp.int32)
-        first, last = below // CHUNK, (within + CHUNK - 1) // CHUNK
-
-        def scores(c, tops):
-            allowed = own == near_ref[c]
-            new = []
-            for head in heads:
-                s = lax.dot_general(
-                    q_hat[rows, cols[head]],
-                    k_win[pl.ds(c * CHUNK, CHUNK), cols[head]],
-                    (((1,), (1,)), ((), ())),
-                    preferred_element_type=jnp.float32,
-                )
-                s = jnp.where(allowed, s * scale, NEG)
-                s_ref[head, c] = s
-                top = tops[head]
-                for part in range(CHUNK // 128):
-                    top = jnp.maximum(top, s[:, part * 128 : part * 128 + 128])
-                new.append(top)
-            return tuple(new)
+        first, steps = bounds[block]
+
+        def scores(step, tops):
+            tops = list(tops)
+            for c in [first + step * TOGETHER + n for n in range(TOGETHER)]:
+                allowed = own == near_ref[c]
+                for head in heads:
+                    s = lax.dot_general(
+                        q_hat[rows, cols[head]],
+                        k_win[pl.ds(pl.multiple_of(c * CHUNK, CHUNK), CHUNK), cols[head]],
+                        (((1,), (1,)), ((), ())),
+                        preferred_element_type=jnp.float32,
+                    )
+                    s = jnp.where(allowed, s * scale, NEG)
+                    s_ref[head, c] = s
+                    for part in range(CHUNK // 128):
+                        tops[head] = jnp.maximum(tops[head], s[:, part * 128 : part * 128 + 128])
+            return tuple(tops)
 
         lowest = jnp.full((BLOCK, 128), NEG, jnp.float32)
-        tops = lax.fori_loop(first, last, scores, (lowest,) * len(heads))
+        tops = lax.fori_loop(0, steps, scores, (lowest,) * len(heads))
         highest = [jnp.max(top, axis=1, keepdims=True) for top in tops]
 
-        def expos(c, totals):
-            new = []
-            for head in heads:
-                e = jnp.exp(s_ref[head, c] - highest[head])
-                s_ref[head, c] = e
-                total = totals[head]
-                for part in range(CHUNK // 128):
-                    total = total + e[:, part * 128 : part * 128 + 128]
-                new.append(total)
-            return tuple(new)
+        def mix(step, sums):
+            sums = list(sums)
+            for c in [first + step * TOGETHER + n for n in range(TOGETHER)]:
+                for head in heads:
+                    total, acc = sums[head]
+                    e = jnp.exp(s_ref[head, c] - highest[head])
+                    for part in range(CHUNK // 128):
+                        total = total + e[:, part * 128 : part * 128 + 128]
+                    v = v_win[pl.ds(pl.multiple_of(c * CHUNK, CHUNK), CHUNK), cols[head]]
+                    acc = acc + jnp.dot(
+                        e.astype(jnp.bfloat16), v, preferred_element_type=jnp.float32
+                    )
+                    sums[head] = (total, acc)
+            return tuple(sums)
 
         zeros = jnp.zeros((BLOCK, 128), jnp.float32)
-        totals = lax.fori_loop(first, last, expos, (zeros,) * len(heads))
-        inverse = [1.0 / jnp.sum(total, axis=1, keepdims=True) for total in totals]
-
-        def mix(c, accs):
-            new = []
-            for head in heads:
-                w = (s_ref[head, c] * inverse[head]).astype(jnp.bfloat16)
-                v = v_win[pl.ds(c * CHUNK, CHUNK), cols[head]]
-                new.append(accs[head] + jnp.dot(w, v, preferred_element_type=jnp.float32))
-            return tuple(new)
-
-        accs = lax.fori_loop(first, last, mix, (zeros,) * len(heads))
+        sums = lax.fori_loop(0, steps, mix, ((zeros, zeros),) * len(heads))
         for head in heads:
-            out_ref[rows, cols[head]] = accs[head].astype(jnp.bfloat16)
-
-
-def attend(q, squares, gain, own, k_parts, far_parts, v_parts):
+            total, acc = sums[head]
+            out_ref[rows, cols[head]] = (acc / jnp.sum(total, axis=1, keepdims=True)).astype(
+                jnp.bfloat16
+            )
+
+
+def attend(marks, q, squares, gain, own, k_parts, far_parts, v_parts):
     width = q.shape[1]
     return pl.pallas_call(
         attend_kernel,
         out_shape=jax.ShapeDtypeStruct((ROWS, width), jnp.bfloat16),
-        in_specs=[VMEM] * 12,
+        in_specs=[SMEM] + [VMEM] * 12,
         out_specs=VMEM,
         scratch_shapes=[
             pltpu.VMEM((ROWS, width), jnp.bfloat16),
-            pltpu.VMEM((WINDOW, width), jnp.bfloat16),
-            pltpu.VMEM((WINDOW, width), jnp.bfloat16),
-            pltpu.VMEM((WINDOW // CHUNK, 1, CHUNK), jnp.float32),
-            pltpu.VMEM((width // HEAD_DIM, WINDOW // CHUNK, BLOCK, CHUNK), jnp.float32),
+            pltpu.VMEM((PADDED, width), jnp.bfloat16),
+            pltpu.VMEM((PADDED, width), jnp.bfloat16),
+            pltpu.VMEM((PADDED // CHUNK, 1, CHUNK), jnp.float32),
+            pltpu.VMEM((width // HEAD_DIM, PADDED // CHUNK, BLOCK, CHUNK), jnp.float32),
         ],
         compiler_params=pltpu.CompilerParams(vmem_limit_bytes=24 << 20),
         name="attend",
-    )(q, squares, gain, own, *k_parts, *far_parts, *v_parts)
+    )(marks, q, squares, gain, own, *k_parts, *far_parts, *v_parts)
 
 
 def on_device(tokens, ln_gain, w_query, w_key, w_value, q_gain, k_gain, seg_ids):
@@ -346,15 +350,22 @@
     k_parts = (shifted(k_own, 1), k_own, shifted(k_own, -1))
 
     vq = in_hbm(vq)
-    v_own, v_last, v_first, queries, squares = project_values(moved, vq, width)
+    far = jax.ShapeDtypeStruct((2 * FAR + MARK_ROWS, width), jnp.bfloat16)
+    outs = (jax.ShapeDtypeStruct((ROWS, width), jnp.bfloat16), far, far)
+    v_own, far_last, far_first = project(
+        values_kernel, "values", outs, width, moved, vq, k_last, k_first
+    )
+    far_parts = (shifted(far_last, 2), shifted(far_first, -2))
+    moved, v_own = lax.optimization_barrier((moved, v_own))
+    outs = (
+        jax.ShapeDtypeStruct((ROWS, width), jnp.float32),
+        jax.ShapeDtypeStruct((Q_BLOCKS, BLOCK), jnp.float32),
+    )
+    queries, squares = project(queries_kernel, "queries", outs, width, in_hbm(moved), vq)
     squares = copies_to_all(squares, "head", N_HEAD)
-    far_parts = (
-        shifted(jnp.concatenate([k_last, v_last], axis=0), 2),
-        shifted(jnp.concatenate([k_first, v_first], axis=0), -2),
-    )
     v_parts = (shifted(v_own, 1), v_own, shifted(v_own, -1))
     return attend(
-        queries, squares, q_gain[None, :], marks[:, None], k_parts, far_parts, v_parts
+        marks, queries, squares, q_gain[None, :], marks[:, None], k_parts, far_parts, v_parts
     )
 
 

time: 162 us -> 158 us (0.975)
  Pallas kernels: 35.5 us -> 32.9 us
  other arithmetic: 2.81 us -> 0.78 us
  starting transfers between devices: 37.1 us -> 39.1 us
    pallas_call x1, Pallas kernels: 14.1 us -> 8.32 us  [attend(): pl.pallas_call(attend_kernel, out_shape=jax.ShapeDtypeStruct((ROWS, width...]
    pallas_call x1 -> x2, Pallas kernels: 7.09 us -> 10.3 us  [project(): pl.pallas_call(kernel, out_shape=outs, in_specs=[HBM, HBM] + [VMEM] * len...]
    ppermute x6, starting transfers between devices: 22.7 us -> 24.8 us  [shifted(): return lax.ppermute(value, 'seq', pairs)]
    ppermute x6, waiting for transfers between devices: 1.88 us -> 0.02 us  [shifted(): return lax.ppermute(value, 'seq', pairs)]
    unnamed x22 -> x14, local copies, waits for them, and re-layouts: 7.17 us -> 6.54 us
  transfers between devices with their start and end apart: 10 -> 10, of which waited for: 4 -> 2; matrix products, arithmetic and copies ran while one was open for 3% -> 2% of each run, Pallas kernels for 13% -> 16%
where the time goes in v6:
time: 158 us; the launch traced here: 156 us
  blocking collectives  48.3 us (31%)
  starting transfers between devices  39.1 us (25%)
  Pallas kernels  32.9 us (21%)
  between operations  13.6 us (9%)
  waiting for transfers between devices  10.7 us (7%)
  local copies, waits for them, and re-layouts  10.2 us (6%)
    all_gather x1, blocking collectives, on_device(): k_z = lax.all_gather(w_key, 'seq', axis=0, axis_index_groups=OVER_Z)  35.9 us
    ppermute x6, starting transfers between devices, shifted(): return lax.ppermute(value, 'seq', pairs)  24.8 us
    all_to_all x3, starting transfers between devices, copies_to_all(): return lax.all_to_all(stacked, axis, 0, 0, axis_index_groups=groups)  14.3 us
    all_to_all x1, blocking collectives, copies_to_all(): return lax.all_to_all(stacked, axis, 0, 0, axis_index_groups=groups)  12.4 us
    all_to_all x3, waiting for transfers between devices, copies_to_all(): return lax.all_to_all(stacked, axis, 0, 0, axis_index_groups=groups)  10.7 us
    pallas_call x2, Pallas kernels, project(): pl.pallas_call(kernel, out_shape=outs, in_specs=[HBM, HBM] + [VMEM] * len...  10.3 us
    pallas_call x1, Pallas kernels, attend(): pl.pallas_call(attend_kernel, out_shape=jax.ShapeDtypeStruct((ROWS, width...  8.32 us
    pallas_call x1, Pallas kernels, norm(): pl.pallas_call(norm_kernel, out_shape=jax.ShapeDtypeStruct((ROWS, D), jnp...  8.15 us
  transfers between devices with their start and end apart: 10, of which 2 were waited for; matrix products, arithmetic and copies ran while one was open for 2% of the time, Pallas kernels for 16%

profile of v6, /device:TPU:24, one launch (start us, length us, event | category | flops | bytes accessed | tf_op | source)
XLA Modules:
  0.0 155.7 jit_solution(908590818866437079)
XLA Ops:
  6.5 0.0 all-gather.4.cloned.1.call-start
  6.5 0.8 pad_maximum_fusion
  7.3 12.4 %all_to_all.20 = bf16[4,50,512]{2,1,0:T(8,128)(2,1)S(1)} all-to-all(bf16[4,50,512]{2,1,0:T(8,128)(2,1)S(1)} %broadcast_in_dim.18), channel_id=1, replica_groups={{0,16,32,48},{1,17,33,49},{2,18,34,50},{3,19,35,51},{4,20,36,52},{5,21,..., dimensions={0} | all-to-all | bytes 409600 | tf_op jit(solution)/shard_map/all_to_all | solution.py:43
  19.7 0.7 reshape.14
  20.5 0.0 all-gather.4.cloned.1.call-update
  20.5 0.0 copy-start.5
  20.5 35.9 %all-gather.1 = bf16[16,50,256]{2,1,0:T(8,128)(2,1)S(1)} all-gather(bf16[1,50,256]{2,1,0:T(8,128)(2,1)} %bitcast.7), channel_id=2, replica_groups={{0,1,2,3,4,5,6,7,8,9,10,11,12,13,14,15},{16,17,18,19,20,21,22,23,24,25,..., dimensions={0}, use_global_device_ids=true | all-gather | bytes 435200 | tf_op jit(solution)/shard_map/all_gather | solution.py:336
  56.4 0.1 broadcast_in_dim.38
  56.6 1.3 broadcast_in_dim.39
  57.9 6.8 %all-to-all-start.1 = ((bf16[4,800,256]{2,1,0:T(8,128)(2,1)}), bf16[4,800,256]{2,1,0:T(8,128)(2,1)S(1)}, u32[]{:S(2)}, u32[]{:S(2)}) async-start(bf16[4,800,256]{2,1,0:T(8,128)(2,1)} %broadcast_in_dim.39), calls=%async_computation.1 | async-start | bytes 3276800 | tf_op jit(solution)/shard_map/all_to_all | solution.py:43
  64.7 0.0 copy-done.5
  64.7 0.0 copy-start.1
  64.7 2.4 %copy-done.1 = bf16[768,3200]{1,0:T(8,128)(2,1)S(1)} copy-done((bf16[768,3200]{1,0:T(8,128)(2,1)S(1)}, bf16[768,3200]{1,0:T(8,128)(2,1)}, u32[]{:S(2)}) %copy-start.1) | copy-done | bytes 4915224
  67.1 8.1 %norm.1.x_ref = bf16[768,3200]{1,0:T(8,128)(2,1)S(1)} custom-call(bf16[768,3200]{1,0:T(8,128)(2,1)S(1)} %copy-done.1, f32[1,3200]{1,0:T(1,128)S(1)} %broadcast_in_dim.40.gain_ref), custom_call_target="tpu_custom_call" | custom-call | tf_op jit(solution)/shard_map/norm/pallas_call | solution.py:69
  75.3 0.0 copy-start
  75.3 2.2 %copy-done = bf16[768,3200]{1,0:T(8,128)(2,1)} copy-done((bf16[768,3200]{1,0:T(8,128)(2,1)}, bf16[768,3200]{1,0:T(8,128)(2,1)S(1)}, u32[]{:S(2)}) %copy-start) | copy-done | bytes 4915224
  77.5 0.0 all-to-all-done.1
  77.5 0.0 copy-start.4
  77.5 1.2 copy-done.4
  78.7 0.0 copy-start.6
  78.7 0.0 copy-start.2
  78.7 5.9 %keys.1 = (f32[768,256]{1,0:T(8,128)S(1)}, f32[3,256]{1,0:T(4,128)S(1)}) custom-call(bf16[768,3200]{1,0:T(8,128)(2,1)} %x_ref.2, f32[1,3200]{1,0:T(1,128)S(1)} %broadcast_in_dim.40.gain_ref, bf16[3200,256]{1,0:T(8,128)(2,1)} %bitcast.6), custom_call_target="tpu_custom_call" | custom-call | tf_op jit(solution)/shard_map/keys/pallas_call | solution.py:160
  84.7 0.6 broadcast_in_dim.41
  85.3 3.6 %all-to-all-start.2 = ((f32[8,3,256]{2,1,0:T(4,128)}), f32[8,3,256]{2,1,0:T(4,128)S(1)}, u32[]{:S(2)}, u32[]{:S(2)}) async-start(f32[8,3,256]{2,1,0:T(4,128)} %broadcast_in_dim.41), calls=%async_computation.2 | async-start | bytes 65536 | tf_op jit(solution)/shard_map/all_to_all | solution.py:43
  88.9 0.0 copy-done.6
  89.0 5.4 %all-to-all-done.2.squares_ref = f32[8,3,256]{2,1,0:T(4,128)S(1)} async-done(((f32[8,3,256]{2,1,0:T(4,128)}), f32[8,3,256]{2,1,0:T(4,128)S(1)}, u32[]{:S(2)}, u32[]{:S(2)}) %all-to-all-start.2) | async-done | bytes 24608 | tf_op jit(solution)/shard_map/all_to_all | solution.py:43
  94.4 0.0 copy-done.2
  94.4 0.2 unit_keys.1
  94.6 1.9 %collective-permute-start = (bf16[776,256]{1,0:T(8,128)(2,1)S(1)}, bf16[776,256]{1,0:T(8,128)(2,1)S(1)}, u32[]{:S(2)}, u32[]{:S(2)}) collective-permute-start(bf16[776,256]{1,0:T(8,128)(2,1)S(1)} %get-tuple-element.39.kc), channel_id=1, source_target_pairs={{0,1},{1,2},{2,3},{3,4},{4,5},{5,6},{6,7},{7,8},{8,9},{9,10},{10,1... | collective-permute-start | bytes 1191944 | tf_op jit(solution)/shard_map/ppermute | solution.py:48
  96.5 6.0 %collective-permute-start.1 = (bf16[776,256]{1,0:T(8,128)(2,1)S(1)}, bf16[776,256]{1,0:T(8,128)(2,1)S(1)}, u32[]{:S(2)}, u32[]{:S(2)}) collective-permute-start(bf16[776,256]{1,0:T(8,128)(2,1)S(1)} %get-tuple-element.39.kc), channel_id=1, source_target_pairs={{1,0},{2,1},{3,2},{4,3},{5,4},{6,5},{7,6},{8,7},{9,8},{10,9},{11,1... | collective-permute-start | bytes 1191944 | tf_op jit(solution)/shard_map/ppermute | solution.py:48
  102.6 0.0 all-gather.4.cloned.1.call-done.w_ref
  102.6 5.3 %values.1 = (bf16[768,256]{1,0:T(8,128)(2,1)S(1)}, bf16[520,256]{1,0:T(8,128)(2,1)}, bf16[520,256]{1,0:T(8,128)(2,1)}) custom-call(bf16[768,3200]{1,0:T(8,128)(2,1)} %copy-done, bf16[3200,512]{1,0:T(8,128)(2,1)} %all-gather.4.cloned.1.call-done.w_ref, bf16[264,256]{1,0:T(8,128)(2,1)S(1)} %get-tuple-element.33.k_last, ...), custom_call_target="tpu_custom_call" | custom-call | tf_op jit(solution)/shard_map/values/pallas_call | solution.py:127
  107.9 1.9 %collective-permute-start.4 = (bf16[768,256]{1,0:T(8,128)(2,1)S(1)}, bf16[768,256]{1,0:T(8,128)(2,1)S(1)}, u32[]{:S(2)}, u32[]{:S(2)}) collective-permute-start(bf16[768,256]{1,0:T(8,128)(2,1)S(1)} %get-tuple-element.42.vc), channel_id=1, source_target_pairs={{0,1},{1,2},{2,3},{3,4},{4,5},{5,6},{6,7},{7,8},{8,9},{9,10},{10,1... | collective-permute-start | bytes 1179656 | tf_op jit(solution)/shard_map/ppermute | solution.py:48
  109.9 6.0 %collective-permute-start.5 = (bf16[768,256]{1,0:T(8,128)(2,1)S(1)}, bf16[768,256]{1,0:T(8,128)(2,1)S(1)}, u32[]{:S(2)}, u32[]{:S(2)}) collective-permute-start(bf16[768,256]{1,0:T(8,128)(2,1)S(1)} %get-tuple-element.42.vc), channel_id=1, source_target_pairs={{1,0},{2,1},{3,2},{4,3},{5,4},{6,5},{7,6},{8,7},{9,8},{10,9},{11,1... | collective-permute-start | bytes 1179656 | tf_op jit(solution)/shard_map/ppermute | solution.py:48
  115.9 1.9 %collective-permute-start.2 = (bf16[520,256]{1,0:T(8,128)(2,1)}, bf16[520,256]{1,0:T(8,128)(2,1)}, u32[]{:S(2)}, u32[]{:S(2)}) collective-permute-start(bf16[520,256]{1,0:T(8,128)(2,1)} %get-tuple-element.40), channel_id=1, source_target_pairs={{0,2},{1,3},{2,4},{3,5},{4,6},{5,7},{6,8},{7,9},{8,10},{9,11},{10,... | collective-permute-start | bytes 798728 | tf_op jit(solution)/shard_map/ppermute | solution.py:48
  117.8 0.0 collective-permute-done.kb
  117.8 6.9 %collective-permute-start.3 = (bf16[520,256]{1,0:T(8,128)(2,1)}, bf16[520,256]{1,0:T(8,128)(2,1)}, u32[]{:S(2)}, u32[]{:S(2)}) collective-permute-start(bf16[520,256]{1,0:T(8,128)(2,1)} %get-tuple-element.41), channel_id=1, source_target_pairs={{2,0},{3,1},{4,2},{5,3},{6,4},{7,5},{8,6},{9,7},{10,8},{11,9},{12,... | collective-permute-start | bytes 798728 | tf_op jit(solution)/shard_map/ppermute | solution.py:48
  124.8 5.0 %queries.1 = (f32[768,256]{1,0:T(8,128)S(1)}, f32[3,256]{1,0:T(4,128)S(1)}) custom-call(bf16[768,3200]{1,0:T(8,128)(2,1)} %copy-done, bf16[3200,512]{1,0:T(8,128)(2,1)} %all-gather.4.cloned.1.call-done.w_ref), custom_call_target="tpu_custom_call" | custom-call | tf_op jit(solution)/shard_map/queries/pallas_call | solution.py:127
  129.8 0.6 broadcast_in_dim.43
  130.4 4.0 %all-to-all-start.3 = ((f32[8,3,256]{2,1,0:T(4,128)}), f32[8,3,256]{2,1,0:T(4,128)}, u32[]{:S(2)}, u32[]{:S(2)}) async-start(f32[8,3,256]{2,1,0:T(4,128)} %broadcast_in_dim.43), calls=%async_computation.3 | async-start | bytes 65536 | tf_op jit(solution)/shard_map/all_to_all | solution.py:43
  134.3 0.2 broadcast_in_dim.46.own_ref
  134.5 0.0 collective-permute-done.1.kd
  134.5 5.3 %all-to-all-done.3.squares_ref = f32[8,3,256]{2,1,0:T(4,128)} async-done(((f32[8,3,256]{2,1,0:T(4,128)}), f32[8,3,256]{2,1,0:T(4,128)}, u32[]{:S(2)}, u32[]{:S(2)}) %all-to-all-start.3) | async-done | bytes 24608 | tf_op jit(solution)/shard_map/all_to_all | solution.py:43
  139.8 0.0 collective-permute-done.2.far_a
  139.8 0.0 collective-permute-done.3.far_e
  139.8 0.0 collective-permute-done.4.vb
  139.8 0.0 collective-permute-done.5.vd
  139.8 0.0 copy-start.3
  139.8 0.7 copy-done.3
  140.5 8.3 %attend.1 = bf16[768,256]{1,0:T(8,128)(2,1)} custom-call(f32[768]{0:T(1024)S(1)} %get-tuple-element.44.marks_ref, f32[768,256]{1,0:T(8,128)S(1)} %get-tuple-element.37.q_ref, f32[8,3,256]{2,1,0:T(4,128)} %all-to-all-done.3.squares_ref, f32[1,256]{1,0:T(1,128)S(1)} %bitcast.5, f32[768,1]{1,0:T(8,128)S(1)} %broadcast_in_dim.46.own_ref, ...), custom_call_target="tpu_custom_call" | custom-call | tf_op jit(solution)/shard_map/attend/pallas_call | solution.py:313
  (5 shorter events, 0.1 us)
Async XLA Ops:
  6.5 96.0 %all-gather.4.cloned.1.call-start = ((), (), s32[]{:S(2)}) async-start(), calls=%async_computation.4 | async-start | bytes 3481600 | tf_op jit(solution)/shard_map/all_gather | solution.py:335
  20.5 44.2 %copy-start.5 = (f32[3200]{0:T(1024)S(1)}, f32[3200]{0:T(1024)}, u32[]{:S(2)}) copy-start(f32[3200]{0:T(1024)} %param.9) | copy-start | bytes 38404
  57.9 19.6 %all-to-all-start.1 = ((bf16[4,800,256]{2,1,0:T(8,128)(2,1)}), bf16[4,800,256]{2,1,0:T(8,128)(2,1)S(1)}, u32[]{:S(2)}, u32[]{:S(2)}) async-start(bf16[4,800,256]{2,1,0:T(8,128)(2,1)} %broadcast_in_dim.39), calls=%async_computation.1 | async-start | bytes 3276800 | tf_op jit(solution)/shard_map/all_to_all | solution.py:43
  64.7 2.4 %copy-start.1 = (bf16[768,3200]{1,0:T(8,128)(2,1)S(1)}, bf16[768,3200]{1,0:T(8,128)(2,1)}, u32[]{:S(2)}) copy-start(bf16[768,3200]{1,0:T(8,128)(2,1)} %x_ref.2) | copy-start | bytes 14745604
  75.3 2.2 %copy-start = (bf16[768,3200]{1,0:T(8,128)(2,1)}, bf16[768,3200]{1,0:T(8,128)(2,1)S(1)}, u32[]{:S(2)}) copy-start(bf16[768,3200]{1,0:T(8,128)(2,1)S(1)} %norm.1.x_ref) | copy-start | bytes 14745604
  77.5 1.2 copy-start.4
  78.7 10.2 %copy-start.6 = (s32[768]{0:T(1024)S(1)}, s32[768]{0:T(1024)}, u32[]{:S(2)}) copy-start(s32[768]{0:T(1024)} %param.15) | copy-start | bytes 9220
  78.7 15.6 %copy-start.2 = (f32[256]{0:T(256)S(1)}, f32[256]{0:T(256)}, u32[]{:S(2)}) copy-start(f32[256]{0:T(256)} %param.14) | copy-start | bytes 3076
  85.3 9.0 %all-to-all-start.2 = ((f32[8,3,256]{2,1,0:T(4,128)}), f32[8,3,256]{2,1,0:T(4,128)S(1)}, u32[]{:S(2)}, u32[]{:S(2)}) async-start(f32[8,3,256]{2,1,0:T(4,128)} %broadcast_in_dim.41), calls=%async_computation.2 | async-start | bytes 65536 | tf_op jit(solution)/shard_map/all_to_all | solution.py:43
  94.6 23.2 %collective-permute-start = (bf16[776,256]{1,0:T(8,128)(2,1)S(1)}, bf16[776,256]{1,0:T(8,128)(2,1)S(1)}, u32[]{:S(2)}, u32[]{:S(2)}) collective-permute-start(bf16[776,256]{1,0:T(8,128)(2,1)S(1)} %get-tuple-element.39.kc), channel_id=1, source_target_pairs={{0,1},{1,2},{2,3},{3,4},{4,5},{5,6},{6,7},{7,8},{8,9},{9,10},{10,1... | collective-permute-start | bytes 1191944 | tf_op jit(solution)/shard_map/ppermute | solution.py:48
  96.5 38.0 %collective-permute-start.1 = (bf16[776,256]{1,0:T(8,128)(2,1)S(1)}, bf16[776,256]{1,0:T(8,128)(2,1)S(1)}, u32[]{:S(2)}, u32[]{:S(2)}) collective-permute-start(bf16[776,256]{1,0:T(8,128)(2,1)S(1)} %get-tuple-element.39.kc), channel_id=1, source_target_pairs={{1,0},{2,1},{3,2},{4,3},{5,4},{6,5},{7,6},{8,7},{9,8},{10,9},{11,1... | collective-permute-start | bytes 1191944 | tf_op jit(solution)/shard_map/ppermute | solution.py:48
  107.9 31.9 %collective-permute-start.4 = (bf16[768,256]{1,0:T(8,128)(2,1)S(1)}, bf16[768,256]{1,0:T(8,128)(2,1)S(1)}, u32[]{:S(2)}, u32[]{:S(2)}) collective-permute-start(bf16[768,256]{1,0:T(8,128)(2,1)S(1)} %get-tuple-element.42.vc), channel_id=1, source_target_pairs={{0,1},{1,2},{2,3},{3,4},{4,5},{5,6},{6,7},{7,8},{8,9},{9,10},{10,1... | collective-permute-start | bytes 1179656 | tf_op jit(solution)/shard_map/ppermute | solution.py:48
  109.9 29.9 %collective-permute-start.5 = (bf16[768,256]{1,0:T(8,128)(2,1)S(1)}, bf16[768,256]{1,0:T(8,128)(2,1)S(1)}, u32[]{:S(2)}, u32[]{:S(2)}) collective-permute-start(bf16[768,256]{1,0:T(8,128)(2,1)S(1)} %get-tuple-element.42.vc), channel_id=1, source_target_pairs={{1,0},{2,1},{3,2},{4,3},{5,4},{6,5},{7,6},{8,7},{9,8},{10,9},{11,1... | collective-permute-start | bytes 1179656 | tf_op jit(solution)/shard_map/ppermute | solution.py:48
  115.9 23.9 %collective-permute-start.2 = (bf16[520,256]{1,0:T(8,128)(2,1)}, bf16[520,256]{1,0:T(8,128)(2,1)}, u32[]{:S(2)}, u32[]{:S(2)}) collective-permute-start(bf16[520,256]{1,0:T(8,128)(2,1)} %get-tuple-element.40), channel_id=1, source_target_pairs={{0,2},{1,3},{2,4},{3,5},{4,6},{5,7},{6,8},{7,9},{8,10},{9,11},{10,... | collective-permute-start | bytes 798728 | tf_op jit(solution)/shard_map/ppermute | solution.py:48
  117.8 21.9 %collective-permute-start.3 = (bf16[520,256]{1,0:T(8,128)(2,1)}, bf16[520,256]{1,0:T(8,128)(2,1)}, u32[]{:S(2)}, u32[]{:S(2)}) collective-permute-start(bf16[520,256]{1,0:T(8,128)(2,1)} %get-tuple-element.41), channel_id=1, source_target_pairs={{2,0},{3,1},{4,2},{5,3},{6,4},{7,5},{8,6},{9,7},{10,8},{11,9},{12,... | collective-permute-start | bytes 798728 | tf_op jit(solution)/shard_map/ppermute | solution.py:48
  130.4 9.4 %all-to-all-start.3 = ((f32[8,3,256]{2,1,0:T(4,128)}), f32[8,3,256]{2,1,0:T(4,128)}, u32[]{:S(2)}, u32[]{:S(2)}) async-start(f32[8,3,256]{2,1,0:T(4,128)} %broadcast_in_dim.43), calls=%async_computation.3 | async-start | bytes 65536 | tf_op jit(solution)/shard_map/all_to_all | solution.py:43
  139.8 0.7 copy-start.3
Sparse Core Ops, SparseCore 0:
  20.6 77.7 all-gather.3

commit v7 on v6

--- a/solution.py
+++ b/solution.py
@@ -284,28 +284,32 @@
         tops = lax.fori_loop(0, steps, scores, (lowest,) * len(heads))
         highest = [jnp.max(top, axis=1, keepdims=True) for top in tops]
 
-        def mix(step, sums):
-            sums = list(sums)
+        def expos(step, totals):
+            totals = list(totals)
             for c in [first + step * TOGETHER + n for n in range(TOGETHER)]:
                 for head in heads:
-                    total, acc = sums[head]
                     e = jnp.exp(s_ref[head, c] - highest[head])
+                    s_ref[head, c] = e
                     for part in range(CHUNK // 128):
-                        total = total + e[:, part * 128 : part * 128 + 128]
+                        totals[head] = totals[head] + e[:, part * 128 : part * 128 + 128]
+            return tuple(totals)
+
+        zeros = jnp.zeros((BLOCK, 128), jnp.float32)
+        totals = lax.fori_loop(0, steps, expos, (zeros,) * len(heads))
+        inverse = [1.0 / jnp.sum(total, axis=1, keepdims=True) for total in totals]
+
+        def mix(step, accs):
+            accs = list(accs)
+            for c in [first + step * TOGETHER + n for n in range(TOGETHER)]:
+                for head in heads:
+                    w = (s_ref[head, c] * inverse[head]).astype(jnp.bfloat16)
                     v = v_win[pl.ds(pl.multiple_of(c * CHUNK, CHUNK), CHUNK), cols[head]]
-                    acc = acc + jnp.dot(
-                        e.astype(jnp.bfloat16), v, preferred_element_type=jnp.float32
-                    )
-                    sums[head] = (total, acc)
-            return tuple(sums)
-
-        zeros = jnp.zeros((BLOCK, 128), jnp.float32)
-        sums = lax.fori_loop(0, steps, mix, ((zeros, zeros),) * len(heads))
+                    accs[head] = accs[head] + jnp.dot(w, v, preferred_element_type=jnp.float32)
+            return tuple(accs)
+
+        accs = lax.fori_loop(0, steps, mix, (zeros,) * len(heads))
         for head in heads:
-            total, acc = sums[head]
-            out_ref[rows, cols[head]] = (acc / jnp.sum(total, axis=1, keepdims=True)).astype(
-                jnp.bfloat16
-            )
+            out_ref[rows, cols[head]] = accs[head].astype(jnp.bfloat16)
 
 
 def attend(marks, q, squares, gain, own, k_parts, far_parts, v_parts):

time: 158 us -> 160 us (1.013)
  no operation moved by 1% of the time
where the time goes in v7:
time: 160 us; the launch traced here: 157 us
  blocking collectives  48.3 us (30%)
  starting transfers between devices  39.1 us (24%)
  Pallas kernels  33.9 us (21%)
  between operations  13.6 us (8%)
  waiting for transfers between devices  10.7 us (7%)
  local copies, waits for them, and re-layouts  10.2 us (6%)
    all_gather x1, blocking collectives, on_device(): k_z = lax.all_gather(w_key, 'seq', axis=0, axis_index_groups=OVER_Z)  35.9 us
    ppermute x6, starting transfers between devices, shifted(): return lax.ppermute(value, 'seq', pairs)  24.8 us
    all_to_all x3, starting transfers between devices, copies_to_all(): return lax.all_to_all(stacked, axis, 0, 0, axis_index_groups=groups)  14.3 us
    all_to_all x1, blocking collectives, copies_to_all(): return lax.all_to_all(stacked, axis, 0, 0, axis_index_groups=groups)  12.4 us
    all_to_all x3, waiting for transfers between devices, copies_to_all(): return lax.all_to_all(stacked, axis, 0, 0, axis_index_groups=groups)  10.7 us
    pallas_call x2, Pallas kernels, project(): pl.pallas_call(kernel, out_shape=outs, in_specs=[HBM, HBM] + [VMEM] * len...  10.3 us
    pallas_call x1, Pallas kernels, attend(): pl.pallas_call(attend_kernel, out_shape=jax.ShapeDtypeStruct((ROWS, width...  9.24 us
    pallas_call x1, Pallas kernels, norm(): pl.pallas_call(norm_kernel, out_shape=jax.ShapeDtypeStruct((ROWS, D), jnp...  8.15 us
  transfers between devices with their start and end apart: 10, of which 2 were waited for; matrix products, arithmetic and copies ran while one was open for 2% of the time, Pallas kernels for 16%

profile of v7, /device:TPU:24, one launch (start us, length us, event | category | flops | bytes accessed | tf_op | source)
XLA Modules:
  0.0 156.6 jit_solution(9210625109530450469)
XLA Ops:
  6.5 0.0 all-gather.4.cloned.1.call-start
  6.5 0.8 pad_maximum_fusion
  7.3 12.4 %all_to_all.20 = bf16[4,50,512]{2,1,0:T(8,128)(2,1)S(1)} all-to-all(bf16[4,50,512]{2,1,0:T(8,128)(2,1)S(1)} %broadcast_in_dim.18), channel_id=1, replica_groups={{0,16,32,48},{1,17,33,49},{2,18,34,50},{3,19,35,51},{4,20,36,52},{5,21,..., dimensions={0} | all-to-all | bytes 409600 | tf_op jit(solution)/shard_map/all_to_all | solution.py:43
  19.7 0.7 reshape.14
  20.5 0.0 all-gather.4.cloned.1.call-update
  20.5 0.0 copy-start.5
  20.5 35.9 %all-gather.1 = bf16[16,50,256]{2,1,0:T(8,128)(2,1)S(1)} all-gather(bf16[1,50,256]{2,1,0:T(8,128)(2,1)} %bitcast.7), channel_id=2, replica_groups={{0,1,2,3,4,5,6,7,8,9,10,11,12,13,14,15},{16,17,18,19,20,21,22,23,24,25,..., dimensions={0}, use_global_device_ids=true | all-gather | bytes 435200 | tf_op jit(solution)/shard_map/all_gather | solution.py:340
  56.4 0.1 broadcast_in_dim.38
  56.6 1.3 broadcast_in_dim.39
  57.9 6.8 %all-to-all-start.1 = ((bf16[4,800,256]{2,1,0:T(8,128)(2,1)}), bf16[4,800,256]{2,1,0:T(8,128)(2,1)S(1)}, u32[]{:S(2)}, u32[]{:S(2)}) async-start(bf16[4,800,256]{2,1,0:T(8,128)(2,1)} %broadcast_in_dim.39), calls=%async_computation.1 | async-start | bytes 3276800 | tf_op jit(solution)/shard_map/all_to_all | solution.py:43
  64.7 0.0 copy-done.5
  64.7 0.0 copy-start.1
  64.7 2.4 %copy-done.1 = bf16[768,3200]{1,0:T(8,128)(2,1)S(1)} copy-done((bf16[768,3200]{1,0:T(8,128)(2,1)S(1)}, bf16[768,3200]{1,0:T(8,128)(2,1)}, u32[]{:S(2)}) %copy-start.1) | copy-done | bytes 4915224
  67.1 8.1 %norm.1.x_ref = bf16[768,3200]{1,0:T(8,128)(2,1)S(1)} custom-call(bf16[768,3200]{1,0:T(8,128)(2,1)S(1)} %copy-done.1, f32[1,3200]{1,0:T(1,128)S(1)} %broadcast_in_dim.40.gain_ref), custom_call_target="tpu_custom_call" | custom-call | tf_op jit(solution)/shard_map/norm/pallas_call | solution.py:69
  75.3 0.0 copy-start
  75.3 2.2 %copy-done = bf16[768,3200]{1,0:T(8,128)(2,1)} copy-done((bf16[768,3200]{1,0:T(8,128)(2,1)}, bf16[768,3200]{1,0:T(8,128)(2,1)S(1)}, u32[]{:S(2)}) %copy-start) | copy-done | bytes 4915224
  77.5 0.0 all-to-all-done.1
  77.5 0.0 copy-start.4
  77.5 1.2 copy-done.4
  78.7 0.0 copy-start.6
  78.7 0.0 copy-start.2
  78.7 5.9 %keys.1 = (f32[768,256]{1,0:T(8,128)S(1)}, f32[3,256]{1,0:T(4,128)S(1)}) custom-call(bf16[768,3200]{1,0:T(8,128)(2,1)} %x_ref.2, f32[1,3200]{1,0:T(1,128)S(1)} %broadcast_in_dim.40.gain_ref, bf16[3200,256]{1,0:T(8,128)(2,1)} %bitcast.6), custom_call_target="tpu_custom_call" | custom-call | tf_op jit(solution)/shard_map/keys/pallas_call | solution.py:160
  84.7 0.6 broadcast_in_dim.41
  85.3 3.6 %all-to-all-start.2 = ((f32[8,3,256]{2,1,0:T(4,128)}), f32[8,3,256]{2,1,0:T(4,128)S(1)}, u32[]{:S(2)}, u32[]{:S(2)}) async-start(f32[8,3,256]{2,1,0:T(4,128)} %broadcast_in_dim.41), calls=%async_computation.2 | async-start | bytes 65536 | tf_op jit(solution)/shard_map/all_to_all | solution.py:43
  88.9 0.0 copy-done.6
  89.0 5.4 %all-to-all-done.2.squares_ref = f32[8,3,256]{2,1,0:T(4,128)S(1)} async-done(((f32[8,3,256]{2,1,0:T(4,128)}), f32[8,3,256]{2,1,0:T(4,128)S(1)}, u32[]{:S(2)}, u32[]{:S(2)}) %all-to-all-start.2) | async-done | bytes 24608 | tf_op jit(solution)/shard_map/all_to_all | solution.py:43
  94.4 0.0 copy-done.2
  94.4 0.2 unit_keys.1
  94.6 1.9 %collective-permute-start = (bf16[776,256]{1,0:T(8,128)(2,1)S(1)}, bf16[776,256]{1,0:T(8,128)(2,1)S(1)}, u32[]{:S(2)}, u32[]{:S(2)}) collective-permute-start(bf16[776,256]{1,0:T(8,128)(2,1)S(1)} %get-tuple-element.39.kc), channel_id=1, source_target_pairs={{0,1},{1,2},{2,3},{3,4},{4,5},{5,6},{6,7},{7,8},{8,9},{9,10},{10,1... | collective-permute-start | bytes 1191944 | tf_op jit(solution)/shard_map/ppermute | solution.py:48
  96.5 6.0 %collective-permute-start.1 = (bf16[776,256]{1,0:T(8,128)(2,1)S(1)}, bf16[776,256]{1,0:T(8,128)(2,1)S(1)}, u32[]{:S(2)}, u32[]{:S(2)}) collective-permute-start(bf16[776,256]{1,0:T(8,128)(2,1)S(1)} %get-tuple-element.39.kc), channel_id=1, source_target_pairs={{1,0},{2,1},{3,2},{4,3},{5,4},{6,5},{7,6},{8,7},{9,8},{10,9},{11,1... | collective-permute-start | bytes 1191944 | tf_op jit(solution)/shard_map/ppermute | solution.py:48
  102.6 0.0 all-gather.4.cloned.1.call-done.w_ref
  102.6 5.3 %values.1 = (bf16[768,256]{1,0:T(8,128)(2,1)S(1)}, bf16[520,256]{1,0:T(8,128)(2,1)}, bf16[520,256]{1,0:T(8,128)(2,1)}) custom-call(bf16[768,3200]{1,0:T(8,128)(2,1)} %copy-done, bf16[3200,512]{1,0:T(8,128)(2,1)} %all-gather.4.cloned.1.call-done.w_ref, bf16[264,256]{1,0:T(8,128)(2,1)S(1)} %get-tuple-element.33.k_last, ...), custom_call_target="tpu_custom_call" | custom-call | tf_op jit(solution)/shard_map/values/pallas_call | solution.py:127
  107.9 1.9 %collective-permute-start.4 = (bf16[768,256]{1,0:T(8,128)(2,1)S(1)}, bf16[768,256]{1,0:T(8,128)(2,1)S(1)}, u32[]{:S(2)}, u32[]{:S(2)}) collective-permute-start(bf16[768,256]{1,0:T(8,128)(2,1)S(1)} %get-tuple-element.42.vc), channel_id=1, source_target_pairs={{0,1},{1,2},{2,3},{3,4},{4,5},{5,6},{6,7},{7,8},{8,9},{9,10},{10,1... | collective-permute-start | bytes 1179656 | tf_op jit(solution)/shard_map/ppermute | solution.py:48
  109.9 6.0 %collective-permute-start.5 = (bf16[768,256]{1,0:T(8,128)(2,1)S(1)}, bf16[768,256]{1,0:T(8,128)(2,1)S(1)}, u32[]{:S(2)}, u32[]{:S(2)}) collective-permute-start(bf16[768,256]{1,0:T(8,128)(2,1)S(1)} %get-tuple-element.42.vc), channel_id=1, source_target_pairs={{1,0},{2,1},{3,2},{4,3},{5,4},{6,5},{7,6},{8,7},{9,8},{10,9},{11,1... | collective-permute-start | bytes 1179656 | tf_op jit(solution)/shard_map/ppermute | solution.py:48
  115.9 1.9 %collective-permute-start.2 = (bf16[520,256]{1,0:T(8,128)(2,1)}, bf16[520,256]{1,0:T(8,128)(2,1)}, u32[]{:S(2)}, u32[]{:S(2)}) collective-permute-start(bf16[520,256]{1,0:T(8,128)(2,1)} %get-tuple-element.40), channel_id=1, source_target_pairs={{0,2},{1,3},{2,4},{3,5},{4,6},{5,7},{6,8},{7,9},{8,10},{9,11},{10,... | collective-permute-start | bytes 798728 | tf_op jit(solution)/shard_map/ppermute | solution.py:48
  117.8 0.0 collective-permute-done.kb
  117.8 6.9 %collective-permute-start.3 = (bf16[520,256]{1,0:T(8,128)(2,1)}, bf16[520,256]{1,0:T(8,128)(2,1)}, u32[]{:S(2)}, u32[]{:S(2)}) collective-permute-start(bf16[520,256]{1,0:T(8,128)(2,1)} %get-tuple-element.41), channel_id=1, source_target_pairs={{2,0},{3,1},{4,2},{5,3},{6,4},{7,5},{8,6},{9,7},{10,8},{11,9},{12,... | collective-permute-start | bytes 798728 | tf_op jit(solution)/shard_map/ppermute | solution.py:48
  124.8 5.0 %queries.1 = (f32[768,256]{1,0:T(8,128)S(1)}, f32[3,256]{1,0:T(4,128)S(1)}) custom-call(bf16[768,3200]{1,0:T(8,128)(2,1)} %copy-done, bf16[3200,512]{1,0:T(8,128)(2,1)} %all-gather.4.cloned.1.call-done.w_ref), custom_call_target="tpu_custom_call" | custom-call | tf_op jit(solution)/shard_map/queries/pallas_call | solution.py:127
  129.8 0.6 broadcast_in_dim.43
  130.4 4.0 %all-to-all-start.3 = ((f32[8,3,256]{2,1,0:T(4,128)}), f32[8,3,256]{2,1,0:T(4,128)}, u32[]{:S(2)}, u32[]{:S(2)}) async-start(f32[8,3,256]{2,1,0:T(4,128)} %broadcast_in_dim.43), calls=%async_computation.3 | async-start | bytes 65536 | tf_op jit(solution)/shard_map/all_to_all | solution.py:43
  134.3 0.2 broadcast_in_dim.46.own_ref
  134.5 0.0 collective-permute-done.1.kd
  134.5 5.3 %all-to-all-done.3.squares_ref = f32[8,3,256]{2,1,0:T(4,128)} async-done(((f32[8,3,256]{2,1,0:T(4,128)}), f32[8,3,256]{2,1,0:T(4,128)}, u32[]{:S(2)}, u32[]{:S(2)}) %all-to-all-start.3) | async-done | bytes 24608 | tf_op jit(solution)/shard_map/all_to_all | solution.py:43
  139.8 0.0 collective-permute-done.2.far_a
  139.8 0.0 collective-permute-done.3.far_e
  139.8 0.0 collective-permute-done.4.vb
  139.8 0.0 collective-permute-done.5.vd
  139.8 0.0 copy-start.3
  139.8 0.7 copy-done.3
  140.5 9.2 %attend.1 = bf16[768,256]{1,0:T(8,128)(2,1)} custom-call(f32[768]{0:T(1024)S(1)} %get-tuple-element.44.marks_ref, f32[768,256]{1,0:T(8,128)S(1)} %get-tuple-element.37.q_ref, f32[8,3,256]{2,1,0:T(4,128)} %all-to-all-done.3.squares_ref, f32[1,256]{1,0:T(1,128)S(1)} %bitcast.5, f32[768,1]{1,0:T(8,128)S(1)} %broadcast_in_dim.46.own_ref, ...), custom_call_target="tpu_custom_call" | custom-call | tf_op jit(solution)/shard_map/attend/pallas_call | solution.py:317
  (5 shorter events, 0.1 us)
Async XLA Ops:
  6.5 96.0 %all-gather.4.cloned.1.call-start = ((), (), s32[]{:S(2)}) async-start(), calls=%async_computation.4 | async-start | bytes 3481600 | tf_op jit(solution)/shard_map/all_gather | solution.py:339
  20.5 44.2 %copy-start.5 = (f32[3200]{0:T(1024)S(1)}, f32[3200]{0:T(1024)}, u32[]{:S(2)}) copy-start(f32[3200]{0:T(1024)} %param.9) | copy-start | bytes 38404
  57.9 19.6 %all-to-all-start.1 = ((bf16[4,800,256]{2,1,0:T(8,128)(2,1)}), bf16[4,800,256]{2,1,0:T(8,128)(2,1)S(1)}, u32[]{:S(2)}, u32[]{:S(2)}) async-start(bf16[4,800,256]{2,1,0:T(8,128)(2,1)} %broadcast_in_dim.39), calls=%async_computation.1 | async-start | bytes 3276800 | tf_op jit(solution)/shard_map/all_to_all | solution.py:43
  64.7 2.4 %copy-start.1 = (bf16[768,3200]{1,0:T(8,128)(2,1)S(1)}, bf16[768,3200]{1,0:T(8,128)(2,1)}, u32[]{:S(2)}) copy-start(bf16[768,3200]{1,0:T(8,128)(2,1)} %x_ref.2) | copy-start | bytes 14745604
  75.3 2.2 %copy-start = (bf16[768,3200]{1,0:T(8,128)(2,1)}, bf16[768,3200]{1,0:T(8,128)(2,1)S(1)}, u32[]{:S(2)}) copy-start(bf16[768,3200]{1,0:T(8,128)(2,1)S(1)} %norm.1.x_ref) | copy-start | bytes 14745604
  77.5 1.2 copy-start.4
  78.7 10.2 %copy-start.6 = (s32[768]{0:T(1024)S(1)}, s32[768]{0:T(1024)}, u32[]{:S(2)}) copy-start(s32[768]{0:T(1024)} %param.15) | copy-start | bytes 9220
  78.7 15.6 %copy-start.2 = (f32[256]{0:T(256)S(1)}, f32[256]{0:T(256)}, u32[]{:S(2)}) copy-start(f32[256]{0:T(256)} %param.14) | copy-start | bytes 3076
  85.3 9.0 %all-to-all-start.2 = ((f32[8,3,256]{2,1,0:T(4,128)}), f32[8,3,256]{2,1,0:T(4,128)S(1)}, u32[]{:S(2)}, u32[]{:S(2)}) async-start(f32[8,3,256]{2,1,0:T(4,128)} %broadcast_in_dim.41), calls=%async_computation.2 | async-start | bytes 65536 | tf_op jit(solution)/shard_map/all_to_all | solution.py:43
  94.6 23.2 %collective-permute-start = (bf16[776,256]{1,0:T(8,128)(2,1)S(1)}, bf16[776,256]{1,0:T(8,128)(2,1)S(1)}, u32[]{:S(2)}, u32[]{:S(2)}) collective-permute-start(bf16[776,256]{1,0:T(8,128)(2,1)S(1)} %get-tuple-element.39.kc), channel_id=1, source_target_pairs={{0,1},{1,2},{2,3},{3,4},{4,5},{5,6},{6,7},{7,8},{8,9},{9,10},{10,1... | collective-permute-start | bytes 1191944 | tf_op jit(solution)/shard_map/ppermute | solution.py:48
  96.5 38.0 %collective-permute-start.1 = (bf16[776,256]{1,0:T(8,128)(2,1)S(1)}, bf16[776,256]{1,0:T(8,128)(2,1)S(1)}, u32[]{:S(2)}, u32[]{:S(2)}) collective-permute-start(bf16[776,256]{1,0:T(8,128)(2,1)S(1)} %get-tuple-element.39.kc), channel_id=1, source_target_pairs={{1,0},{2,1},{3,2},{4,3},{5,4},{6,5},{7,6},{8,7},{9,8},{10,9},{11,1... | collective-permute-start | bytes 1191944 | tf_op jit(solution)/shard_map/ppermute | solution.py:48
  107.9 31.9 %collective-permute-start.4 = (bf16[768,256]{1,0:T(8,128)(2,1)S(1)}, bf16[768,256]{1,0:T(8,128)(2,1)S(1)}, u32[]{:S(2)}, u32[]{:S(2)}) collective-permute-start(bf16[768,256]{1,0:T(8,128)(2,1)S(1)} %get-tuple-element.42.vc), channel_id=1, source_target_pairs={{0,1},{1,2},{2,3},{3,4},{4,5},{5,6},{6,7},{7,8},{8,9},{9,10},{10,1... | collective-permute-start | bytes 1179656 | tf_op jit(solution)/shard_map/ppermute | solution.py:48
  109.9 29.9 %collective-permute-start.5 = (bf16[768,256]{1,0:T(8,128)(2,1)S(1)}, bf16[768,256]{1,0:T(8,128)(2,1)S(1)}, u32[]{:S(2)}, u32[]{:S(2)}) collective-permute-start(bf16[768,256]{1,0:T(8,128)(2,1)S(1)} %get-tuple-element.42.vc), channel_id=1, source_target_pairs={{1,0},{2,1},{3,2},{4,3},{5,4},{6,5},{7,6},{8,7},{9,8},{10,9},{11,1... | collective-permute-start | bytes 1179656 | tf_op jit(solution)/shard_map/ppermute | solution.py:48
  115.9 23.9 %collective-permute-start.2 = (bf16[520,256]{1,0:T(8,128)(2,1)}, bf16[520,256]{1,0:T(8,128)(2,1)}, u32[]{:S(2)}, u32[]{:S(2)}) collective-permute-start(bf16[520,256]{1,0:T(8,128)(2,1)} %get-tuple-element.40), channel_id=1, source_target_pairs={{0,2},{1,3},{2,4},{3,5},{4,6},{5,7},{6,8},{7,9},{8,10},{9,11},{10,... | collective-permute-start | bytes 798728 | tf_op jit(solution)/shard_map/ppermute | solution.py:48
  117.8 21.9 %collective-permute-start.3 = (bf16[520,256]{1,0:T(8,128)(2,1)}, bf16[520,256]{1,0:T(8,128)(2,1)}, u32[]{:S(2)}, u32[]{:S(2)}) collective-permute-start(bf16[520,256]{1,0:T(8,128)(2,1)} %get-tuple-element.41), channel_id=1, source_target_pairs={{2,0},{3,1},{4,2},{5,3},{6,4},{7,5},{8,6},{9,7},{10,8},{11,9},{12,... | collective-permute-start | bytes 798728 | tf_op jit(solution)/shard_map/ppermute | solution.py:48
  130.4 9.4 %all-to-all-start.3 = ((f32[8,3,256]{2,1,0:T(4,128)}), f32[8,3,256]{2,1,0:T(4,128)}, u32[]{:S(2)}, u32[]{:S(2)}) async-start(f32[8,3,256]{2,1,0:T(4,128)} %broadcast_in_dim.43), calls=%async_computation.3 | async-start | bytes 65536 | tf_op jit(solution)/shard_map/all_to_all | solution.py:43
  139.8 0.7 copy-start.3
Sparse Core Ops, SparseCore 0:
  20.6 77.7 all-gather.3

commit v8 on v7

--- a/solution.py
+++ b/solution.py
@@ -24,7 +24,7 @@
 N_BLOCKS = WINDOW // BLOCK
 Q_BLOCKS = ROWS // BLOCK
 CHUNK = 256
-TOGETHER = 2
+TOGETHER = 3
 PADDED = WINDOW + (TOGETHER - 1) * CHUNK
 NEG = -1e30
 BEYOND = 1e6

time: 160 us -> 159 us (level)
  the two profiles are of different devices: /device:TPU:24 before, /device:TPU:8 now
where the time goes in v8:
time: 159 us; the launch traced here: 158 us
  blocking collectives  48.1 us (30%)
  starting transfers between devices  40.1 us (25%)
  Pallas kernels  34.4 us (22%)
  between operations  13.6 us (9%)
  waiting for transfers between devices  10.7 us (7%)
  local copies, waits for them, and re-layouts  10.2 us (6%)
    all_gather x1, blocking collectives, on_device(): k_z = lax.all_gather(w_key, 'seq', axis=0, axis_index_groups=OVER_Z)  34.9 us
    ppermute x6, starting transfers between devices, shifted(): return lax.ppermute(value, 'seq', pairs)  24.8 us
    all_to_all x3, starting transfers between devices, copies_to_all(): return lax.all_to_all(stacked, axis, 0, 0, axis_index_groups=groups)  15.4 us
    all_to_all x1, blocking collectives, copies_to_all(): return lax.all_to_all(stacked, axis, 0, 0, axis_index_groups=groups)  13.2 us
    all_to_all x3, waiting for transfers between devices, copies_to_all(): return lax.all_to_all(stacked, axis, 0, 0, axis_index_groups=groups)  10.7 us
    pallas_call x2, Pallas kernels, project(): pl.pallas_call(kernel, out_shape=outs, in_specs=[HBM, HBM] + [VMEM] * len...  10.3 us
    pallas_call x1, Pallas kernels, attend(): pl.pallas_call(attend_kernel, out_shape=jax.ShapeDtypeStruct((ROWS, width...  9.75 us
    pallas_call x1, Pallas kernels, norm(): pl.pallas_call(norm_kernel, out_shape=jax.ShapeDtypeStruct((ROWS, D), jnp...  8.15 us
  transfers between devices with their start and end apart: 10, of which 2 were waited for; matrix products, arithmetic and copies ran while one was open for 2% of the time, Pallas kernels for 16%

profile of v8, /device:TPU:8, one launch (start us, length us, event | category | flops | bytes accessed | tf_op | source)
XLA Modules:
  0.0 157.9 jit_solution(9492079869144952015)
XLA Ops:
  6.5 0.0 all-gather.4.cloned.1.call-start
  6.5 0.8 pad_maximum_fusion
  7.3 13.2 %all_to_all.20 = bf16[4,50,512]{2,1,0:T(8,128)(2,1)S(1)} all-to-all(bf16[4,50,512]{2,1,0:T(8,128)(2,1)S(1)} %broadcast_in_dim.18), channel_id=1, replica_groups={{0,16,32,48},{1,17,33,49},{2,18,34,50},{3,19,35,51},{4,20,36,52},{5,21,..., dimensions={0} | all-to-all | bytes 409600 | tf_op jit(solution)/shard_map/all_to_all | solution.py:43
  20.6 0.7 reshape.14
  21.3 0.0 all-gather.4.cloned.1.call-update
  21.3 0.0 copy-start.5
  21.4 34.9 %all-gather.1 = bf16[16,50,256]{2,1,0:T(8,128)(2,1)S(1)} all-gather(bf16[1,50,256]{2,1,0:T(8,128)(2,1)} %bitcast.7), channel_id=2, replica_groups={{0,1,2,3,4,5,6,7,8,9,10,11,12,13,14,15},{16,17,18,19,20,21,22,23,24,25,..., dimensions={0}, use_global_device_ids=true | all-gather | bytes 435200 | tf_op jit(solution)/shard_map/all_gather | solution.py:340
  56.2 0.1 broadcast_in_dim.38
  56.4 1.3 broadcast_in_dim.39
  57.7 7.2 %all-to-all-start.1 = ((bf16[4,800,256]{2,1,0:T(8,128)(2,1)}), bf16[4,800,256]{2,1,0:T(8,128)(2,1)S(1)}, u32[]{:S(2)}, u32[]{:S(2)}) async-start(bf16[4,800,256]{2,1,0:T(8,128)(2,1)} %broadcast_in_dim.39), calls=%async_computation.1 | async-start | bytes 3276800 | tf_op jit(solution)/shard_map/all_to_all | solution.py:43
  64.9 0.0 copy-done.5
  64.9 0.0 copy-start.1
  64.9 2.4 %copy-done.1 = bf16[768,3200]{1,0:T(8,128)(2,1)S(1)} copy-done((bf16[768,3200]{1,0:T(8,128)(2,1)S(1)}, bf16[768,3200]{1,0:T(8,128)(2,1)}, u32[]{:S(2)}) %copy-start.1) | copy-done | bytes 4915224
  67.4 8.1 %norm.1.x_ref = bf16[768,3200]{1,0:T(8,128)(2,1)S(1)} custom-call(bf16[768,3200]{1,0:T(8,128)(2,1)S(1)} %copy-done.1, f32[1,3200]{1,0:T(1,128)S(1)} %broadcast_in_dim.40.gain_ref), custom_call_target="tpu_custom_call" | custom-call | tf_op jit(solution)/shard_map/norm/pallas_call | solution.py:69
  75.5 0.0 copy-start
  75.5 2.2 %copy-done = bf16[768,3200]{1,0:T(8,128)(2,1)} copy-done((bf16[768,3200]{1,0:T(8,128)(2,1)}, bf16[768,3200]{1,0:T(8,128)(2,1)S(1)}, u32[]{:S(2)}) %copy-start) | copy-done | bytes 4915224
  77.7 0.0 all-to-all-done.1
  77.7 0.0 copy-start.4
  77.7 1.2 copy-done.4
  79.0 0.0 copy-start.6
  79.0 0.0 copy-start.2
  79.0 5.9 %keys.1 = (f32[768,256]{1,0:T(8,128)S(1)}, f32[3,256]{1,0:T(4,128)S(1)}) custom-call(bf16[768,3200]{1,0:T(8,128)(2,1)} %x_ref.2, f32[1,3200]{1,0:T(1,128)S(1)} %broadcast_in_dim.40.gain_ref, bf16[3200,256]{1,0:T(8,128)(2,1)} %bitcast.6), custom_call_target="tpu_custom_call" | custom-call | tf_op jit(solution)/shard_map/keys/pallas_call | solution.py:160
  84.9 0.6 broadcast_in_dim.41
  85.5 4.2 %all-to-all-start.2 = ((f32[8,3,256]{2,1,0:T(4,128)}), f32[8,3,256]{2,1,0:T(4,128)S(1)}, u32[]{:S(2)}, u32[]{:S(2)}) async-start(f32[8,3,256]{2,1,0:T(4,128)} %broadcast_in_dim.41), calls=%async_computation.2 | async-start | bytes 65536 | tf_op jit(solution)/shard_map/all_to_all | solution.py:43
  89.8 0.0 copy-done.6
  89.8 5.4 %all-to-all-done.2.squares_ref = f32[8,3,256]{2,1,0:T(4,128)S(1)} async-done(((f32[8,3,256]{2,1,0:T(4,128)}), f32[8,3,256]{2,1,0:T(4,128)S(1)}, u32[]{:S(2)}, u32[]{:S(2)}) %all-to-all-start.2) | async-done | bytes 24608 | tf_op jit(solution)/shard_map/all_to_all | solution.py:43
  95.2 0.0 copy-done.2
  95.2 0.2 unit_keys.1
  95.4 1.9 %collective-permute-start = (bf16[776,256]{1,0:T(8,128)(2,1)S(1)}, bf16[776,256]{1,0:T(8,128)(2,1)S(1)}, u32[]{:S(2)}, u32[]{:S(2)}) collective-permute-start(bf16[776,256]{1,0:T(8,128)(2,1)S(1)} %get-tuple-element.39.kc), channel_id=1, source_target_pairs={{0,1},{1,2},{2,3},{3,4},{4,5},{5,6},{6,7},{7,8},{8,9},{9,10},{10,1... | collective-permute-start | bytes 1191944 | tf_op jit(solution)/shard_map/ppermute | solution.py:48
  97.4 6.0 %collective-permute-start.1 = (bf16[776,256]{1,0:T(8,128)(2,1)S(1)}, bf16[776,256]{1,0:T(8,128)(2,1)S(1)}, u32[]{:S(2)}, u32[]{:S(2)}) collective-permute-start(bf16[776,256]{1,0:T(8,128)(2,1)S(1)} %get-tuple-element.39.kc), channel_id=1, source_target_pairs={{1,0},{2,1},{3,2},{4,3},{5,4},{6,5},{7,6},{8,7},{9,8},{10,9},{11,1... | collective-permute-start | bytes 1191944 | tf_op jit(solution)/shard_map/ppermute | solution.py:48
  103.4 0.0 all-gather.4.cloned.1.call-done.w_ref
  103.4 5.3 %values.1 = (bf16[768,256]{1,0:T(8,128)(2,1)S(1)}, bf16[520,256]{1,0:T(8,128)(2,1)}, bf16[520,256]{1,0:T(8,128)(2,1)}) custom-call(bf16[768,3200]{1,0:T(8,128)(2,1)} %copy-done, bf16[3200,512]{1,0:T(8,128)(2,1)} %all-gather.4.cloned.1.call-done.w_ref, bf16[264,256]{1,0:T(8,128)(2,1)S(1)} %get-tuple-element.33.k_last, ...), custom_call_target="tpu_custom_call" | custom-call | tf_op jit(solution)/shard_map/values/pallas_call | solution.py:127
  108.8 1.9 %collective-permute-start.4 = (bf16[768,256]{1,0:T(8,128)(2,1)S(1)}, bf16[768,256]{1,0:T(8,128)(2,1)S(1)}, u32[]{:S(2)}, u32[]{:S(2)}) collective-permute-start(bf16[768,256]{1,0:T(8,128)(2,1)S(1)} %get-tuple-element.42.vc), channel_id=1, source_target_pairs={{0,1},{1,2},{2,3},{3,4},{4,5},{5,6},{6,7},{7,8},{8,9},{9,10},{10,1... | collective-permute-start | bytes 1179656 | tf_op jit(solution)/shard_map/ppermute | solution.py:48
  110.7 6.0 %collective-permute-start.5 = (bf16[768,256]{1,0:T(8,128)(2,1)S(1)}, bf16[768,256]{1,0:T(8,128)(2,1)S(1)}, u32[]{:S(2)}, u32[]{:S(2)}) collective-permute-start(bf16[768,256]{1,0:T(8,128)(2,1)S(1)} %get-tuple-element.42.vc), channel_id=1, source_target_pairs={{1,0},{2,1},{3,2},{4,3},{5,4},{6,5},{7,6},{8,7},{9,8},{10,9},{11,1... | collective-permute-start | bytes 1179656 | tf_op jit(solution)/shard_map/ppermute | solution.py:48
  116.7 1.9 %collective-permute-start.2 = (bf16[520,256]{1,0:T(8,128)(2,1)}, bf16[520,256]{1,0:T(8,128)(2,1)}, u32[]{:S(2)}, u32[]{:S(2)}) collective-permute-start(bf16[520,256]{1,0:T(8,128)(2,1)} %get-tuple-element.40), channel_id=1, source_target_pairs={{0,2},{1,3},{2,4},{3,5},{4,6},{5,7},{6,8},{7,9},{8,10},{9,11},{10,... | collective-permute-start | bytes 798728 | tf_op jit(solution)/shard_map/ppermute | solution.py:48
  118.7 0.0 collective-permute-done.kb
  118.7 6.9 %collective-permute-start.3 = (bf16[520,256]{1,0:T(8,128)(2,1)}, bf16[520,256]{1,0:T(8,128)(2,1)}, u32[]{:S(2)}, u32[]{:S(2)}) collective-permute-start(bf16[520,256]{1,0:T(8,128)(2,1)} %get-tuple-element.41), channel_id=1, source_target_pairs={{2,0},{3,1},{4,2},{5,3},{6,4},{7,5},{8,6},{9,7},{10,8},{11,9},{12,... | collective-permute-start | bytes 798728 | tf_op jit(solution)/shard_map/ppermute | solution.py:48
  125.6 5.0 %queries.1 = (f32[768,256]{1,0:T(8,128)S(1)}, f32[3,256]{1,0:T(4,128)S(1)}) custom-call(bf16[768,3200]{1,0:T(8,128)(2,1)} %copy-done, bf16[3200,512]{1,0:T(8,128)(2,1)} %all-gather.4.cloned.1.call-done.w_ref), custom_call_target="tpu_custom_call" | custom-call | tf_op jit(solution)/shard_map/queries/pallas_call | solution.py:127
  130.6 0.6 broadcast_in_dim.43
  131.2 4.0 %all-to-all-start.3 = ((f32[8,3,256]{2,1,0:T(4,128)}), f32[8,3,256]{2,1,0:T(4,128)}, u32[]{:S(2)}, u32[]{:S(2)}) async-start(f32[8,3,256]{2,1,0:T(4,128)} %broadcast_in_dim.43), calls=%async_computation.3 | async-start | bytes 65536 | tf_op jit(solution)/shard_map/all_to_all | solution.py:43
  135.2 0.2 broadcast_in_dim.46.own_ref
  135.3 0.0 collective-permute-done.1.kd
  135.3 5.3 %all-to-all-done.3.squares_ref = f32[8,3,256]{2,1,0:T(4,128)} async-done(((f32[8,3,256]{2,1,0:T(4,128)}), f32[8,3,256]{2,1,0:T(4,128)}, u32[]{:S(2)}, u32[]{:S(2)}) %all-to-all-start.3) | async-done | bytes 24608 | tf_op jit(solution)/shard_map/all_to_all | solution.py:43
  140.6 0.0 collective-permute-done.2.far_a
  140.6 0.0 collective-permute-done.3.far_e
  140.6 0.0 collective-permute-done.4.vb
  140.6 0.0 collective-permute-done.5.vd
  140.6 0.0 copy-start.3
  140.6 0.7 copy-done.3
  141.3 9.8 %attend.1 = bf16[768,256]{1,0:T(8,128)(2,1)} custom-call(f32[768]{0:T(1024)S(1)} %get-tuple-element.44.marks_ref, f32[768,256]{1,0:T(8,128)S(1)} %get-tuple-element.37.q_ref, f32[8,3,256]{2,1,0:T(4,128)} %all-to-all-done.3.squares_ref, f32[1,256]{1,0:T(1,128)S(1)} %bitcast.5, f32[768,1]{1,0:T(8,128)S(1)} %broadcast_in_dim.46.own_ref, ...), custom_call_target="tpu_custom_call" | custom-call | tf_op jit(solution)/shard_map/attend/pallas_call | solution.py:317
  (5 shorter events, 0.1 us)
Async XLA Ops:
  6.5 96.9 %all-gather.4.cloned.1.call-start = ((), (), s32[]{:S(2)}) async-start(), calls=%async_computation.4 | async-start | bytes 3481600 | tf_op jit(solution)/shard_map/all_gather | solution.py:339
  21.3 43.6 %copy-start.5 = (f32[3200]{0:T(1024)S(1)}, f32[3200]{0:T(1024)}, u32[]{:S(2)}) copy-start(f32[3200]{0:T(1024)} %param.9) | copy-start | bytes 38404
  57.7 20.1 %all-to-all-start.1 = ((bf16[4,800,256]{2,1,0:T(8,128)(2,1)}), bf16[4,800,256]{2,1,0:T(8,128)(2,1)S(1)}, u32[]{:S(2)}, u32[]{:S(2)}) async-start(bf16[4,800,256]{2,1,0:T(8,128)(2,1)} %broadcast_in_dim.39), calls=%async_computation.1 | async-start | bytes 3276800 | tf_op jit(solution)/shard_map/all_to_all | solution.py:43
  64.9 2.4 %copy-start.1 = (bf16[768,3200]{1,0:T(8,128)(2,1)S(1)}, bf16[768,3200]{1,0:T(8,128)(2,1)}, u32[]{:S(2)}) copy-start(bf16[768,3200]{1,0:T(8,128)(2,1)} %x_ref.2) | copy-start | bytes 14745604
  75.5 2.2 %copy-start = (bf16[768,3200]{1,0:T(8,128)(2,1)}, bf16[768,3200]{1,0:T(8,128)(2,1)S(1)}, u32[]{:S(2)}) copy-start(bf16[768,3200]{1,0:T(8,128)(2,1)S(1)} %norm.1.x_ref) | copy-start | bytes 14745604
  77.7 1.2 copy-start.4
  79.0 10.8 %copy-start.6 = (s32[768]{0:T(1024)S(1)}, s32[768]{0:T(1024)}, u32[]{:S(2)}) copy-start(s32[768]{0:T(1024)} %param.15) | copy-start | bytes 9220
  79.0 16.2 %copy-start.2 = (f32[256]{0:T(256)S(1)}, f32[256]{0:T(256)}, u32[]{:S(2)}) copy-start(f32[256]{0:T(256)} %param.14) | copy-start | bytes 3076
  85.5 9.7 %all-to-all-start.2 = ((f32[8,3,256]{2,1,0:T(4,128)}), f32[8,3,256]{2,1,0:T(4,128)S(1)}, u32[]{:S(2)}, u32[]{:S(2)}) async-start(f32[8,3,256]{2,1,0:T(4,128)} %broadcast_in_dim.41), calls=%async_computation.2 | async-start | bytes 65536 | tf_op jit(solution)/shard_map/all_to_all | solution.py:43
  95.4 23.2 %collective-permute-start = (bf16[776,256]{1,0:T(8,128)(2,1)S(1)}, bf16[776,256]{1,0:T(8,128)(2,1)S(1)}, u32[]{:S(2)}, u32[]{:S(2)}) collective-permute-start(bf16[776,256]{1,0:T(8,128)(2,1)S(1)} %get-tuple-element.39.kc), channel_id=1, source_target_pairs={{0,1},{1,2},{2,3},{3,4},{4,5},{5,6},{6,7},{7,8},{8,9},{9,10},{10,1... | collective-permute-start | bytes 1191944 | tf_op jit(solution)/shard_map/ppermute | solution.py:48
  97.4 38.0 %collective-permute-start.1 = (bf16[776,256]{1,0:T(8,128)(2,1)S(1)}, bf16[776,256]{1,0:T(8,128)(2,1)S(1)}, u32[]{:S(2)}, u32[]{:S(2)}) collective-permute-start(bf16[776,256]{1,0:T(8,128)(2,1)S(1)} %get-tuple-element.39.kc), channel_id=1, source_target_pairs={{1,0},{2,1},{3,2},{4,3},{5,4},{6,5},{7,6},{8,7},{9,8},{10,9},{11,1... | collective-permute-start | bytes 1191944 | tf_op jit(solution)/shard_map/ppermute | solution.py:48
  108.8 31.9 %collective-permute-start.4 = (bf16[768,256]{1,0:T(8,128)(2,1)S(1)}, bf16[768,256]{1,0:T(8,128)(2,1)S(1)}, u32[]{:S(2)}, u32[]{:S(2)}) collective-permute-start(bf16[768,256]{1,0:T(8,128)(2,1)S(1)} %get-tuple-element.42.vc), channel_id=1, source_target_pairs={{0,1},{1,2},{2,3},{3,4},{4,5},{5,6},{6,7},{7,8},{8,9},{9,10},{10,1... | collective-permute-start | bytes 1179656 | tf_op jit(solution)/shard_map/ppermute | solution.py:48
  110.7 29.9 %collective-permute-start.5 = (bf16[768,256]{1,0:T(8,128)(2,1)S(1)}, bf16[768,256]{1,0:T(8,128)(2,1)S(1)}, u32[]{:S(2)}, u32[]{:S(2)}) collective-permute-start(bf16[768,256]{1,0:T(8,128)(2,1)S(1)} %get-tuple-element.42.vc), channel_id=1, source_target_pairs={{1,0},{2,1},{3,2},{4,3},{5,4},{6,5},{7,6},{8,7},{9,8},{10,9},{11,1... | collective-permute-start | bytes 1179656 | tf_op jit(solution)/shard_map/ppermute | solution.py:48
  116.7 23.9 %collective-permute-start.2 = (bf16[520,256]{1,0:T(8,128)(2,1)}, bf16[520,256]{1,0:T(8,128)(2,1)}, u32[]{:S(2)}, u32[]{:S(2)}) collective-permute-start(bf16[520,256]{1,0:T(8,128)(2,1)} %get-tuple-element.40), channel_id=1, source_target_pairs={{0,2},{1,3},{2,4},{3,5},{4,6},{5,7},{6,8},{7,9},{8,10},{9,11},{10,... | collective-permute-start | bytes 798728 | tf_op jit(solution)/shard_map/ppermute | solution.py:48
  118.7 21.9 %collective-permute-start.3 = (bf16[520,256]{1,0:T(8,128)(2,1)}, bf16[520,256]{1,0:T(8,128)(2,1)}, u32[]{:S(2)}, u32[]{:S(2)}) collective-permute-start(bf16[520,256]{1,0:T(8,128)(2,1)} %get-tuple-element.41), channel_id=1, source_target_pairs={{2,0},{3,1},{4,2},{5,3},{6,4},{7,5},{8,6},{9,7},{10,8},{11,9},{12,... | collective-permute-start | bytes 798728 | tf_op jit(solution)/shard_map/ppermute | solution.py:48
  131.2 9.4 %all-to-all-start.3 = ((f32[8,3,256]{2,1,0:T(4,128)}), f32[8,3,256]{2,1,0:T(4,128)}, u32[]{:S(2)}, u32[]{:S(2)}) async-start(f32[8,3,256]{2,1,0:T(4,128)} %broadcast_in_dim.43), calls=%async_computation.3 | async-start | bytes 65536 | tf_op jit(solution)/shard_map/all_to_all | solution.py:43
  140.6 0.7 copy-start.3
Sparse Core Ops, SparseCore 0:
  21.5 77.0 all-gather.3
